TPU v7x, 512 devices: a whole 4x8x8 slice. The times are simulated.
512 devices in a mesh: ctx: 32 (over y_hi, z, core), tp: 16 (over x, y_lo).
Axes of the slice: x: 4, y: 8 (y_hi: 2, y_lo: 4; y = y_hi * 4 + y_lo), z: 8, core: 2. Of those that a mesh axis runs over, the one named last changes fastest.
Arguments:
- features: bfloat16 [4096, 3, 8192], P('ctx', None, 'tp'), may hold values from -6 to 6
- short_filter: float32 [3, 3, 8192], P(None, None, 'tp'), may hold values from -3 to 3
- decay_rate: float32 [16, 8192], P(None, 'tp'), may hold values from 2e-05 to 0.04
- residue: float32 [16, 8192], P(None, 'tp'), may hold values from -2 to 2
- skip: float32 [8192], P('tp'), may hold values from -2 to 2
- out_weight: bfloat16 [8192, 8192], P('tp', 'ctx'), may hold values from -0.125 to 0.125
Outputs:
- mixed: bfloat16 [4096, 8192], P('ctx', 'tp')
All inputs are finite; a program needn't handle non-finite values.
Results may differ from a plain program's by a relative error of at most 0.0049.
Values may be sent and summed in bfloat16 or wider, within the bound.
No kernel may reach another device: no remote copies, remote signals or barrier semaphores. Data moves between devices by JAX's collectives and lax.ppermute only.
A program may use at most 64 MiB of HBM per device.

v0:
```python
import jax
import jax.numpy as jnp
from jax import lax
from jax.sharding import PartitionSpec as P

BLOCK = 32


def from_behind(value, axis, by):
    size = lax.axis_size(axis)
    pairs = [(i, i + by) for i in range(size) if 0 <= i + by < size]
    return lax.ppermute(value, axis, pairs)


def carried_in(value, axis, combine, identity):
    size, index = (lax.axis_size(axis), lax.axis_index(axis))
    everything = jax.tree.map(lambda part: lax.all_gather(part, axis), value)
    start = jax.tree.map(
        lambda part, zero: jnp.broadcast_to(jnp.asarray(zero, part.dtype), part.shape),
        value,
        identity,
    )

    def step(k, before):
        reached = k < index
        new = combine(before, jax.tree.map(lambda part: part[k], everything))
        return jax.tree.map(lambda a, b: jnp.where(reached, a, b), new, before)

    return lax.fori_loop(0, size, step, start)


def shards(features, short_filter, decay_rate, residue, skip, out_weight):
    positions = features.shape[0]
    tap_count = short_filter.shape[0]
    channels = features.shape[2]
    halo_rows = from_behind(features[positions - (tap_count - 1) :], "ctx", 1)
    extended = jnp.concatenate([halo_rows, features], axis=0).astype(jnp.float32)
    filtered = jnp.zeros((positions, 3, channels), jnp.float32)
    for tap_index in range(tap_count):
        begin = tap_count - 1 - tap_index
        filtered = filtered + short_filter[tap_index][None] * extended[begin : begin + positions]
    query = filtered[:, 0]
    drive = filtered[:, 1] * filtered[:, 2]
    gain = residue * jnp.sqrt(-jnp.expm1(-2.0 * decay_rate))
    block_len = BLOCK
    block_count = positions // block_len
    offsets = jnp.arange(block_len, dtype=jnp.float32)
    powers = jnp.exp(-decay_rate[None] * offsets[:, None, None])
    kernel = jnp.sum(gain[None] * powers, axis=1)
    lag_table = jnp.arange(block_len)[:, None] - jnp.arange(block_len)[None, :]
    toeplitz = jnp.where(
        (lag_table >= 0)[:, :, None], kernel[jnp.clip(lag_table, 0, block_len - 1)], 0.0
    )
    blocks = drive.reshape(block_count, block_len, channels)
    inside = jnp.einsum("tsc,nsc->ntc", toeplitz, blocks, precision=lax.Precision.HIGHEST)
    block_ends = jnp.einsum("smc,nsc->nmc", powers[::-1], blocks, precision=lax.Precision.HIGHEST)
    block_decay = jnp.exp(-decay_rate * block_len)

    def advance(state, block_end):
        return (block_decay * state + block_end, state)

    zero_state = jnp.zeros_like(decay_rate)
    local_end, starts = lax.scan(advance, zero_state, block_ends)
    device_decay = jnp.exp(-decay_rate * positions)

    def combine(earlier, later):
        return (earlier[0] * later[0], later[0] * earlier[1] + later[1])

    carried_pair = carried_in(
        (device_decay, local_end), "ctx", combine, (jnp.ones_like(decay_rate), zero_state)
    )
    incoming = carried_pair[1]
    block_offsets = jnp.arange(block_count, dtype=jnp.float32) * block_len
    leading = jnp.exp(-decay_rate[None] * block_offsets[:, None, None])
    starts = starts + leading * incoming[None]
    after_start = gain[None] * jnp.exp(-decay_rate[None] * (offsets + 1.0)[:, None, None])
    carried = jnp.einsum("tmc,nmc->ntc", after_start, starts, precision=lax.Precision.HIGHEST)
    response = (inside + carried).reshape(positions, channels) + skip[None] * drive
    gated = (query * response).astype(jnp.bfloat16)
    partial_sums = jnp.dot(
        gated,
        lax.all_gather(out_weight, "ctx", axis=1, tiled=True),
        preferred_element_type=jnp.float32,
    )
    return lax.psum_scatter(partial_sums, "tp", scatter_dimension=1, tiled=True).astype(
        jnp.bfloat16
    )


def solution(mesh):
    in_specs = (
        P("ctx", None, "tp"),
        P(None, None, "tp"),
        P(None, "tp"),
        P(None, "tp"),
        P("tp"),
        P("tp", "ctx"),
    )
    out_specs = P("ctx", "tp")
    return jax.shard_map(shards, mesh=mesh, in_specs=in_specs, out_specs=out_specs, check_vma=False)
```

profile of v0, /device:TPU:56, one launch (start us, length us, event | category | flops | bytes accessed | tf_op | source)
XLA Modules:
  0.0 439.3 jit_solution(434469078434152546)
XLA Ops:
  7.3 1.9 collective-permute-start
  9.2 1.4 multiply_exponential_fusion.1
  11.0 6.9 %multiply_exponential_fusion = (f32[32,16,512]{0,1,2:T(8,128)}, f32[32,512]{0,1:T(8,128)S(1)}) fusion(f32[16,512]{0,1:T(8,128)S(1)} %copy.24, f32[16,512]{0,1:T(8,128)S(1)} %copy.23), kind=kLoop, calls=%fused_computation.14 | loop fusion | flops 770048 | bytes 1179648 | tf_op jit(solution)/shard_map/exp | solution.py:48
  18.0 7.3 %rev.3 = f32[32,16,512]{0,1,2:T(8,128)} reverse(f32[32,16,512]{0,1,2:T(8,128)} %get-tuple-element.201), dimensions={0} | reverse | bytes 2097152 | tf_op jit(solution)/shard_map/rev | solution.py:56
  25.7 0.8 copy-done
  26.9 8.4 %convolution_bitcast_fusion = f32[4,16,512]{1,0,2:T(4,128)S(1)} fusion(f32[4,32,512]{1,0,2:T(4,128)S(1)} %copy.27, f32[32,16,512]{0,1,2:T(8,128)} %rev.3), kind=kOutput, calls=%fused_computation.21 | convolution fusion | flops 12582912 | bytes 1441792 | tf_op jit(solution)/shard_map/smc,nsc->nmc/dot_general | solution.py:56
  35.6 2.6 while.27
  40.0 3.5 gather_fusion
  43.5 7.6 %copy.26 = f32[32,32,512]{1,0,2:T(8,128)} copy(f32[32,32,512]{2,1,0:T(8,128)S(1)} %bitcast.56) | data formatting | bytes 4194304 | tf_op jit(solution)/shard_map/gather | solution.py:52
  51.1 15.5 %fusion.1 = f32[512,4,32]{2,1,0:T(4,128)S(1)} fusion(f32[4,32,512]{1,0,2:T(4,128)S(1)} %copy.27, f32[32,32,512]{1,0,2:T(8,128)} %copy.26, pred[32,32]{1,0:T(8,128)(4,1)S(1)} %subtract_compare_fusion), kind=kOutput, calls=%fused_computation.6 | convolution fusion | flops 25690112 | bytes 2622464 | tf_op jit(solution)/shard_map/tsc,nsc->ntc/dot_general | solution.py:55
  66.6 32.9 %all-gather.8.cloned.1.call-done = f32[512,512]{1,0:T(8,128)} async-done(((f32[16,512]{1,0:T(8,128)}), f32[512,512]{1,0:T(8,128)}) %all-gather.8.cloned.1.call-update) | async-done | bytes 1048592 | tf_op jit(solution)/shard_map/all_gather | solution.py:17
  99.5 84.9 %all-gather.10.cloned.1.call-done = f32[512,512]{1,0:T(8,128)} async-done(((f32[16,512]{1,0:T(8,128)}), f32[512,512]{1,0:T(8,128)}) %all-gather.10.cloned.1.call-update) | async-done | bytes 1048592 | tf_op jit(solution)/shard_map/all_gather | solution.py:17
  184.4 26.0 %while.28 = (s32[]{:T(128)}, f32[16,512]{1,0:T(8,128)S(1)}, s32[]{:T(128)}, f32[32,16,512]{2,1,0:T(8,128)}, f32[32,16,512]{2,1,0:T(8,128)}, /*index=5*/s32[]{:T(128)}, s32[]{:T(128)}) while((s32[]{:T(128)}, f32[16,512]{1,0:T(8,128)S(1)}, s32[]{:T(128)}, f32[32,16,512]{2,1,0:T(8,128)}, f32[32,16,512]{2,1,0:T(8,128)}, ...), condition=%wide.region_4.5_spmd.clone, body=%wide.region_3.4_spmd.clone.sunk | while | flops 32772 | bytes 131173 | solution.py:29
  185.2 0.8 fusion.32
  186.0 0.8 fusion.32
  186.8 0.8 fusion.32
  187.6 0.8 fusion.32
  188.4 0.8 fusion.32
  189.3 0.8 fusion.32
  190.1 0.8 fusion.32
  190.9 0.8 fusion.32
  191.7 0.8 fusion.32
  192.5 0.8 fusion.32
  193.3 0.8 fusion.32
  194.1 0.8 fusion.32
  195.0 0.8 fusion.32
  195.8 0.8 fusion.32
  196.6 0.8 fusion.32
  197.4 0.8 fusion.32
  198.2 0.8 fusion.32
  199.0 0.8 fusion.32
  199.8 0.8 fusion.32
  200.6 0.8 fusion.32
  201.5 0.8 fusion.32
  202.3 0.8 fusion.32
  203.1 0.8 fusion.32
  203.9 0.8 fusion.32
  204.7 0.8 fusion.32
  205.5 0.8 fusion.32
  206.3 0.8 fusion.32
  207.2 0.8 fusion.32
  208.8 0.8 fusion.32
  210.5 1.4 copy.30
  211.9 6.6 %fusion.15 = f32[4,32,512]{1,0,2:T(4,128)S(1)} fusion(f32[512,4,32]{2,1,0:T(4,128)S(1)} %fusion.1, f32[4,16,512]{1,0,2:T(4,128)} %copy.30, f32[32]{0:T(128)S(1)} %iota_add_fusion, f32[16,512]{0,1:T(8,128)S(1)} %copy.24, f32[16,512]{0,1:T(8,128)} %copy-done.3), kind=kOutput, calls=%fused_computation.20 | convolution fusion | flops 13172736 | bytes 721024 | tf_op jit(solution)/shard_map/tmc,nmc->ntc/dot_general | solution.py:77
  219.0 98.8 %all-gather.6.cloned.1.call-done = bf16[512,8192]{1,0:T(8,128)(2,1)} async-done(((bf16[512,256]{1,0:T(8,128)(2,1)}), bf16[512,8192]{1,0:T(8,128)(2,1)}) %all-gather.6.cloned.1.call-update) | async-done | bytes 8388624 | tf_op jit(solution)/shard_map/all_gather | solution.py:82
  317.8 6.6 %fusion.24 = f32[128,8192]{1,0:T(8,128)} fusion(bf16[128,512]{1,0:T(8,128)(2,1)S(1)} %fusion.21, bf16[512,8192]{1,0:T(8,128)(2,1)} %all-gather.6.cloned.1.call-done), kind=kOutput, calls=%fused_computation.47 | convolution fusion | flops 1073741824 | bytes 12713984 | tf_op jit(solution)/shard_map/dot_general | solution.py:80
  324.4 106.7 %reduce-scatter.2.cloned.1.call-done = f32[128,512]{1,0:T(8,128)} async-done(((f32[128,8192]{1,0:T(8,128)}), f32[128,512]{1,0:T(8,128)}) %reduce-scatter.2.cloned.1.call-update) | async-done | bytes 262160 | tf_op jit(solution)/shard_map/reduce_scatter | solution.py:85
  431.1 1.6 convert_element_type.11
  (57 shorter events, 9.4 us)
Async XLA Ops:
  6.5 11.4 %copy-start.6 = (f32[3,3,512]{2,1,0:T(4,128)S(1)}, f32[3,3,512]{2,1,0:T(4,128)}, u32[]{:S(2)}) copy-start(f32[3,3,512]{2,1,0:T(4,128)} %param.11) | copy-start | bytes 55300
  6.5 93.0 %all-gather.8.cloned.1.call-start = ((), (), s32[]{:S(2)}) async-start(), calls=%async_computation.3 | async-start | bytes 1081344 | tf_op jit(solution)/shard_map/all_gather | solution.py:17
  7.3 17.9 %collective-permute-start = (bf16[2,3,512]{2,0,1:T(2,128)(2,1)S(1)}, bf16[2,3,512]{2,0,1:T(2,128)(2,1)S(1)}, u32[]{:S(2)}, u32[]{:S(2)}) collective-permute-start(bf16[2,3,512]{2,0,1:T(2,128)(2,1)S(1)} %slice.31), channel_id=1, source_target_pairs={{0,16},{16,32},{32,48},{48,64},{64,80},{80,96},{96,112},{112,128},... | collective-permute-start | bytes 18440 | tf_op jit(solution)/shard_map/ppermute | solution.py:12
  10.7 173.7 %all-gather.10.cloned.1.call-start = ((), (), s32[]{:S(2)}) async-start(), calls=%async_computation.4 | async-start | bytes 1081344 | tf_op jit(solution)/shard_map/all_gather | solution.py:17
  11.0 14.3 %copy-start.3 = (f32[16,512]{0,1:T(8,128)}, f32[16,512]{0,1:T(8,128)S(1)}, u32[]{:S(2)}) copy-start(f32[16,512]{0,1:T(8,128)S(1)} %copy.23) | copy-start | bytes 98308
  18.0 7.3 %copy-start.4 = (bf16[128,3,512]{2,0,1:T(8,128)(2,1)S(1)}, bf16[128,3,512]{2,0,1:T(8,128)(2,1)}, u32[]{:S(2)}) copy-start(bf16[128,3,512]{2,0,1:T(8,128)(2,1)} %param.10) | copy-start | bytes 1179652
  25.6 0.9 copy-start
  38.2 0.6 copy-start.2
  38.8 279.0 %all-gather.6.cloned.1.call-start = ((), (), s32[]{:S(2)}) async-start(), calls=%async_computation.1 | async-start | bytes 8650752 | tf_op jit(solution)/shard_map/all_gather | solution.py:82
  39.6 391.6 %reduce-scatter.2.cloned.1.call-start = ((), (), s32[]{:S(2)}) async-start(), calls=%async_computation.2 | async-start | bytes 4456448 | tf_op jit(solution)/shard_map/reduce_scatter | solution.py:85
  51.1 159.3 %copy-start.5 = (f32[4,16,512]{2,1,0:T(8,128)S(1)}, f32[4,16,512]{2,1,0:T(8,128)}, u32[]{:S(2)}) copy-start(f32[4,16,512]{2,1,0:T(8,128)} %get-tuple-element.127) | copy-start | bytes 393220
  211.9 7.0 %copy-start.1 = (f32[128,3,512]{2,0,1:T(8,128)S(1)}, f32[128,3,512]{2,0,1:T(8,128)}, u32[]{:S(2)}) copy-start(f32[128,3,512]{2,0,1:T(8,128)} %copy-done) | copy-start | bytes 2359300
  211.9 7.0 %copy-start.7 = (f32[512]{0:T(512)S(1)}, f32[512]{0:T(512)}, u32[]{:S(2)}) copy-start(f32[512]{0:T(512)} %param.14) | copy-start | bytes 6148
Sparse Core Ops, SparseCore 0:
  10.8 88.6 all-gather.7
  102.9 81.4 all-gather.9
  187.5 130.2 all-gather.5
  324.6 106.5 reduce-scatter.1
where the time goes:
time: 445 us; the launch traced here: 439 us
  waiting for transfers between devices  324 us (73%)
  other arithmetic  38.4 us (9%)
  matrix products  37.1 us (8%)
  local copies, waits for them, and re-layouts  23.4 us (5%)
  between operations  13.4 us (3%)
    all_gather x2, waiting for transfers between devices, carried_in(): everything = jax.tree.map(lambda part: lax.all_gather(part, axis), value)  118 us
    reduce_scatter x1, waiting for transfers between devices, shards(): lax.psum_scatter(partial_sums, 'tp', scatter_dimension=1, tiled=True)  107 us
    all_gather x1, waiting for transfers between devices, shards(): lax.all_gather(out_weight, 'ctx', axis=1, tiled=True)  98.8 us
    select_n x32, other arithmetic, step(): return jax.tree.map(lambda a, b: jnp.where(reached, a, b), new, before)  25.3 us
    dot_general x1, matrix products, shards(): jnp.einsum('tsc,nsc->ntc', toeplitz, blocks, precision=lax.Precision.HIGH...  15.5 us
    gather x2, local copies, waits for them, and re-layouts, shards(): kernel[jnp.clip(lag_table, 0, block_len - 1)]  11.1 us
  transfers between devices with their start and end apart: 5, of which 4 were waited for; matrix products, arithmetic and copies ran while one was open for 20% of the time, Pallas kernels for 0%

commit v1 on v0

v1 whole, which is shorter than its diff:
```python
import functools

import jax
import jax.numpy as jnp
from jax import lax
from jax.experimental import pallas as pl
from jax.experimental.pallas import tpu as pltpu
from jax.sharding import PartitionSpec as P

AXES = ("ctx", "tp")
EVERY = [
    (yh, z, core, x, yl)
    for yh in range(2)
    for z in range(8)
    for core in range(2)
    for x in range(4)
    for yl in range(4)
]


def flat(yh, z, core, x, yl):
    return ((yh * 8 + z) * 2 + core) * 16 + x * 4 + yl


def move(value, axes, target, sends=lambda *place: True):
    pairs = [(flat(*p), flat(*target(*p))) for p in EVERY if sends(*p)]
    return lax.ppermute(value, axes, pairs)


def from_behind(value, axes, by):
    pairs = [(i, i + by * 16) for i in range(512) if i + by * 16 < 512]
    return lax.ppermute(value, axes, pairs)


VMEM = pl.BlockSpec(memory_space=pltpu.VMEM)
SMEM = pl.BlockSpec(memory_space=pltpu.SMEM)


def spread(ref, value):
    rows = value.shape[0]
    for half in range(2):
        for part in range(4):
            ref[pl.ds(half * 4 + part, rows, stride=8), :] = value[:, part * 128 : part * 128 + 128]


def front_kernel(feat_ref, halo_ref, taps_ref, rate_ref, query_ref, drive_ref, half_ref, end_ref, ext, lam):
    filtered = []
    for f in range(3):
        ext[8:136, :] = feat_ref[f].astype(jnp.float32)
        ext[6:8, :] = halo_ref[f].astype(jnp.float32)
        total = taps_ref[0, f : f + 1, :] * ext[8:136, :]
        total = total + taps_ref[1, f : f + 1, :] * ext[7:135, :]
        filtered.append(total + taps_ref[2, f : f + 1, :] * ext[6:134, :])
    query_ref[...] = filtered[0]
    drive = filtered[1] * filtered[2]
    for half in range(2):
        for part in range(4):
            drive_ref[pl.ds(half * 4 + part, 64, stride=8), :] = drive[
                half * 64 : half * 64 + 64, part * 128 : part * 128 + 128
            ]
    spread(lam, jnp.exp(-rate_ref[...]))
    lams = [lam[m * 8 : m * 8 + 8, :] for m in range(16)]

    def step(t, states):
        now = drive_ref[pl.ds(pl.multiple_of(t * 8, 8), 8), :]
        return tuple(a * s + now for a, s in zip(lams, states))

    states = lax.fori_loop(0, 64, step, tuple(jnp.zeros((8, 128), jnp.float32) for _ in range(16)), unroll=4)
    for m in range(16):
        half_ref[m * 8 : m * 8 + 8, :] = states[m]
    spread(lam, jnp.exp(-64.0 * rate_ref[...]))
    for m in range(16):
        lam[m * 8 : m * 8 + 8, :] = states[m] + pltpu.roll(lam[m * 8 : m * 8 + 8, :] * states[m], 4, 0)
    for part in range(4):
        end_ref[:, part * 128 : part * 128 + 128] = lam[pl.ds(4 + part, 16, stride=8), :]


def back_kernel(query_ref, drive_ref, half_ref, in_ref, rate_ref, gain_ref, skip_ref, out_ref, lam, gain, start, skip, resp):
    spread(start, in_ref[...])
    spread(gain, gain_ref[...])
    spread(lam, jnp.exp(-64.0 * rate_ref[...]))
    first = lax.broadcasted_iota(jnp.int32, (8, 128), 0) < 4
    states = []
    for m in range(16):
        rows = slice(m * 8, m * 8 + 8)
        came = start[rows, :]
        later = lam[rows, :] * came + pltpu.roll(half_ref[rows, :], 4, 0)
        states.append(jnp.where(first, came, later))
    spread(lam, jnp.exp(-rate_ref[...]))
    spread(skip, skip_ref[...])
    lams = [lam[m * 8 : m * 8 + 8, :] for m in range(16)]
    gains = [gain[m * 8 : m * 8 + 8, :] for m in range(16)]
    direct = skip[...]

    def step(t, states):
        rows = pl.ds(pl.multiple_of(t * 8, 8), 8)
        now = drive_ref[rows, :]
        states = tuple(a * s + now for a, s in zip(lams, states))
        sums = [direct * now, None, None, None]
        for m in range(16):
            term = gains[m] * states[m]
            sums[m % 4] = term if sums[m % 4] is None else sums[m % 4] + term
        resp[rows, :] = (sums[0] + sums[1]) + (sums[2] + sums[3])
        return states

    lax.fori_loop(0, 64, step, tuple(states), unroll=2)
    for half in range(2):
        for part in range(4):
            rows, cols = slice(half * 64, half * 64 + 64), slice(part * 128, part * 128 + 128)
            out_ref[rows, cols] = (query_ref[rows, cols] * resp[pl.ds(half * 4 + part, 64, stride=8), :]).astype(jnp.bfloat16)


def mix_kernel(table_ref, *refs):
    s, (fwd, bwd, hf, hb), weights = refs[:4], refs[4:8], refs[8:17]
    keep_ref, send_ref, g, w, acc, g_sem, w_sem = refs[17:]
    own = table_ref[0] == 1
    yl = table_ref[1]
    low = table_ref[2] * 4
    high = table_ref[3] * 4

    def spot(base, j):
        return g.at[base + lax.rem(yl - j + 4, 4)]

    from_own = [(s[j], spot(low, j)) for j in range(4)]
    from_own += [(hf.at[pl.ds(j * 256, 256), :], spot(high, j)) for j in range(2)]
    from_own += [(hb.at[pl.ds(j * 256, 256), :], spot(high, 2 + j)) for j in range(2)]
    from_others = [(fwd.at[pl.ds(j * 256, 256), :], spot(low, j)) for j in range(4)]
    from_others += [(bwd.at[pl.ds(j * 256, 256), :], spot(high, j)) for j in range(4)]

    def channel_copies(pairs):
        return [pltpu.make_async_copy(a, b, g_sem.at[i]) for i, (a, b) in enumerate(pairs)]

    @pl.when(own)
    def _():
        for copy in channel_copies(from_own):
            copy.start()

    @pl.when(jnp.logical_not(own))
    def _():
        for copy in channel_copies(from_others):
            copy.start()

    loads = [pltpu.make_async_copy(weights[i], w.at[i], w_sem.at[i]) for i in range(7)]
    loads += [pltpu.make_async_copy(weights[7 + p], w.at[7, pl.ds(p * 512, 512)], w_sem.at[7 + p]) for p in range(2)]
    for copy in loads:
        copy.start()

    @pl.when(own)
    def _():
        for copy in channel_copies(from_own):
            copy.wait()

    @pl.when(jnp.logical_not(own))
    def _():
        for copy in channel_copies(from_others):
            copy.wait()

    for i in range(8):
        loads[i].wait()
        if i == 7:
            loads[8].wait()
        block = g[table_ref[4 + i]]
        for p in range(2):
            part = jnp.dot(block, w[i, p * 512 : p * 512 + 512, :], preferred_element_type=jnp.float32)
            acc[p] = part if i == 0 else acc[p] + part
    for p in range(2):

        @pl.when(table_ref[12] == p)
        def _():
            for half in range(2):
                cols = slice(half * 256, half * 256 + 256)
                keep_ref[:, cols] = acc[half ^ p, :128, :]
                send_ref[:, cols] = acc[half ^ p, 128:, :]


def front(feat, halo, taps, rate):
    f32 = jnp.float32
    return pl.pallas_call(
        front_kernel,
        out_shape=(
            jax.ShapeDtypeStruct((128, 512), f32),
            jax.ShapeDtypeStruct((512, 128), f32),
            jax.ShapeDtypeStruct((128, 128), f32),
            jax.ShapeDtypeStruct((16, 512), f32),
        ),
        in_specs=[VMEM] * 4,
        out_specs=(VMEM,) * 4,
        scratch_shapes=[pltpu.VMEM((136, 512), f32), pltpu.VMEM((128, 128), f32)],
        cost_estimate=pl.CostEstimate(flops=1, bytes_accessed=1, transcendentals=0),
        name="front",
    )(feat, halo, taps, rate)


def back(query, drive, half, incoming, rate, gain, skip):
    f32 = jnp.float32
    return pl.pallas_call(
        back_kernel,
        out_shape=jax.ShapeDtypeStruct((128, 512), jnp.bfloat16),
        in_specs=[VMEM] * 7,
        out_specs=VMEM,
        scratch_shapes=[pltpu.VMEM((128, 128), f32)] * 3 + [pltpu.VMEM((8, 128), f32), pltpu.VMEM((512, 128), f32)],
        cost_estimate=pl.CostEstimate(flops=1, bytes_accessed=1, transcendentals=0),
        name="back",
    )(query, drive, half, incoming, rate, gain, skip)


def mix(table, *operands):
    out = jax.ShapeDtypeStruct((128, 512), jnp.float32)
    return pl.pallas_call(
        mix_kernel,
        out_shape=(out, out),
        in_specs=[SMEM] + [pl.BlockSpec(memory_space=pl.ANY)] * len(operands),
        out_specs=(VMEM, VMEM),
        scratch_shapes=[
            pltpu.VMEM((8, 256, 512), jnp.bfloat16),
            pltpu.VMEM((8, 1024, 256), jnp.bfloat16),
            pltpu.VMEM((2, 256, 256), jnp.float32),
            pltpu.SemaphoreType.DMA((8,)),
            pltpu.SemaphoreType.DMA((9,)),
        ],
        compiler_params=pltpu.CompilerParams(vmem_limit_bytes=60 * 1024 * 1024),
        cost_estimate=pl.CostEstimate(flops=1_100_000_000, bytes_accessed=7_000_000, transcendentals=0),
        name="mix",
    )(table, *operands)


def body(features, short_filter, decay_rate, residue, skip, out_weight, axes, front, back, mix):
    n_modes, channels = decay_rate.shape
    positions = features.shape[0]
    index = lax.axis_index(axes)
    yl, x, core, z, yh = index % 4, index // 4 % 4, index // 16 % 2, index // 32 % 8, index // 256

    halo = from_behind(features[positions - 2 :], axes, 1)

    def tile(p):
        def target(yh, z, core, x, yl):
            t = yh * 8 + z
            return core ^ p, (x // 2) * 4 + yl, x % 2, t // 4, t % 4

        return target

    weight = jnp.concatenate([move(out_weight, axes, tile(p)) for p in range(2)], axis=0)
    rows = out_weight.shape[0]

    def along(axis, by):
        def target(yh, z, core, x, yl):
            if axis == "z":
                return yh, (z + by) % 8, core, x, yl
            if axis == "x":
                return yh, z, core, (x + by) % 4, yl
            return yh, z, core, x, (yl + by) % 4

        return target

    def other_core(value):
        return move(value, axes, lambda yh, z, core, x, yl: (yh, z, 1 - core, x, yl))

    tie = lax.optimization_barrier
    ups, downs = [weight], [weight]

    def ring():
        ups.append(move(ups[-1], axes, along("z", 1)))
        downs.append(move(downs[-1], axes, along("z", -1)))

    query, drive, half, end = front(features.transpose(1, 0, 2), halo.transpose(1, 0, 2), short_filter, decay_rate)

    incoming = from_behind(end, axes, 1)
    for k in range(5):
        by = 2**k
        if k == 1:
            incoming, ups[0] = tie((incoming, ups[0]))
            downs[0] = ups[0]
            ring()
        incoming = incoming + jnp.exp(-decay_rate * (positions * by)) * from_behind(incoming, axes, by)

    gain = residue * jnp.sqrt(-jnp.expm1(-2.0 * decay_rate))
    incoming, ups[1], downs[1] = tie((incoming, ups[1], downs[1]))
    ring()
    gated = back(query, drive, half, incoming, decay_rate, gain, skip[None])

    both = jnp.concatenate([gated, other_core(gated)], axis=0)

    def mine(yh, z, core, x, yl):
        return x % 2 == core

    def others(yh, z, core, x, yl):
        return x % 2 != core

    near = [both] + [move(both, axes, along("yl", j), mine) for j in range(1, 4)]
    line = jnp.concatenate(near, axis=0)
    line, ups[2], downs[2] = tie((line, ups[2], downs[2]))
    ring()
    fwd = move(line, axes, along("x", 1), mine)
    bwd = move(line, axes, along("x", -1), mine)
    fwd, bwd, ups[3], downs[3] = tie((fwd, bwd, ups[3], downs[3]))
    up_last = move(ups[3][:rows], axes, along("z", 1))
    down_last = move(downs[3][rows:], axes, along("z", -1))
    weights = [ups[0], ups[1], downs[1], ups[2], downs[2], ups[3], downs[3], up_last, down_last]
    half_rows = line.shape[0] // 2
    hf = move(fwd[:half_rows], axes, along("x", 1), others)
    hb = move(bwd[half_rows:], axes, along("x", -1), others)

    own = x % 2 == core
    low = jnp.where(own, x // 2, (x + 3) % 4 // 2)
    high = jnp.where(own, 1 - x // 2, (x + 1) % 4 // 2)
    places = [(z - d) % 8 for d in (0, 1, -1, 2, -2, 3, -3, 4)]
    table = jnp.stack([own.astype(jnp.int32), yl, low, high] + places + [yh]).astype(jnp.int32)
    keep, send = mix(table, *near, fwd, bwd, hf, hb, *weights)
    return (keep + other_core(send)).astype(jnp.bfloat16)


def shards(*arguments):
    return body(*arguments, AXES, front, back, mix)


def solution(mesh):
    in_specs = (
        P("ctx", None, "tp"),
        P(None, None, "tp"),
        P(None, "tp"),
        P(None, "tp"),
        P("tp"),
        P("tp", "ctx"),
    )
    return jax.shard_map(shards, mesh=mesh, in_specs=in_specs, out_specs=P("ctx", "tp"), check_vma=False)
```

time: 445 us -> 197 us (0.44)
  waiting for transfers between devices: 324 us -> 94.5 us
  starting transfers between devices: 2.22 us -> 76.6 us
  matrix products: 37.1 us -> 0 us
  other arithmetic: 38.4 us -> 3.9 us
  local copies, waits for them, and re-layouts: 23.4 us -> 7.27 us
  between operations: 13.4 us -> 0.8 us
  Pallas kernels: 0 us -> 10.5 us
    all_gather x3 -> x0, waiting for transfers between devices: 217 us -> none  [the longest x2 118 us: carried_in(): everything = jax.tree.map(lambda part: lax.all_gather(part, axis), value)]
    reduce_scatter x1 -> x0, waiting for transfers between devices: 107 us -> none  [shards(): lax.psum_scatter(partial_sums, 'tp', scatter_dimension=1, tiled=True)]
    ppermute x1 -> x26, waiting for transfers between devices: 0.01 us -> 94.5 us  [the longest x7 58.9 us: from_behind(): return lax.ppermute(value, axes, pairs)]
    ppermute x1 -> x26, starting transfers between devices: 1.92 us -> 76.6 us  [the longest x19 63.7 us: move(): return lax.ppermute(value, axes, pairs)]
    dot_general x4 -> x0, matrix products: 37.1 us -> none  [the longest x1 15.5 us: shards(): jnp.einsum('tsc,nsc->ntc', toeplitz, blocks, precision=lax.Precision.HIGH...]
    select_n x33 -> x0, other arithmetic: 25.3 us -> none  [the longest x32 25.3 us: step(): return jax.tree.map(lambda a, b: jnp.where(reached, a, b), new, before)]
    gather x2 -> x0, local copies, waits for them, and re-layouts: 11.1 us -> none  [shards(): kernel[jnp.clip(lag_table, 0, block_len - 1)]]
    pallas_call x0 -> x3, Pallas kernels: none -> 10.5 us  [the longest x1 4.98 us: mix(): pl.pallas_call(mix_kernel, out_shape=(out, out), in_specs=[SMEM] + [pl.Bl...]
  transfers between devices with their start and end apart: 5 -> 26, of which waited for: 4 -> 16; matrix products, arithmetic and copies ran while one was open for 20% -> 1% of each run, Pallas kernels for 0% -> 0%
where the time goes in v1:
time: 197 us; the launch traced here: 194 us
  waiting for transfers between devices  94.5 us (48%)
  starting transfers between devices  76.6 us (39%)
  Pallas kernels  10.5 us (5%)
  local copies, waits for them, and re-layouts  7.27 us (4%)
  other arithmetic  3.9 us (2%)
    ppermute x19, starting transfers between devices, move(): return lax.ppermute(value, axes, pairs)  63.7 us
    ppermute x7, waiting for transfers between devices, from_behind(): return lax.ppermute(value, axes, pairs)  58.9 us
    ppermute x19, waiting for transfers between devices, move(): return lax.ppermute(value, axes, pairs)  35.6 us
    ppermute x7, starting transfers between devices, from_behind(): return lax.ppermute(value, axes, pairs)  12.8 us
    pallas_call x1, Pallas kernels, mix(): pl.pallas_call(mix_kernel, out_shape=(out, out), in_specs=[SMEM] + [pl.Bl...  4.98 us
    unnamed x46, local copies, waits for them, and re-layouts  4.36 us
  transfers between devices with their start and end apart: 26, of which 16 were waited for; matrix products, arithmetic and copies ran while one was open for 1% of the time, Pallas kernels for 0%

profile of v1, /device:TPU:56, one launch (start us, length us, event | category | flops | bytes accessed | tf_op | source)
XLA Modules:
  0.0 193.6 jit_solution(1661842067672855075)
XLA Ops:
  0.0 0.8 slice.15
  0.8 1.9 collective-permute-start
  2.7 12.0 %collective-permute-done = bf16[2,3,512]{2,0,1:T(2,128)(2,1)S(1)} collective-permute-done((bf16[2,3,512]{2,0,1:T(2,128)(2,1)S(1)}, bf16[2,3,512]{2,0,1:T(2,128)(2,1)S(1)}, u32[]{:S(2)}, u32[]{:S(2)}) %collective-permute-start) | collective-permute-done | bytes 6176 | tf_op jit(solution)/shard_map/ppermute | solution.py:32
  15.3 2.6 %front.1 = (f32[128,512]{1,0:T(8,128)}, f32[512,128]{1,0:T(8,128)}, f32[128,128]{1,0:T(8,128)}, f32[16,512]{1,0:T(8,128)}) custom-call(bf16[3,128,512]{2,1,0:T(8,128)(2,1)} %bitcast.16, bf16[3,2,512]{2,1,0:T(2,128)(2,1)} %bitcast.17, f32[3,3,512]{2,1,0:T(4,128)} %taps_ref.1, f32[16,512]{1,0:T(8,128)} %rate_ref.3), custom_call_target="tpu_custom_call" | custom-call | flops 1 | bytes 1 | tf_op jit(solution)/shard_map/front/pallas_call | solution.py:178
  18.0 1.9 collective-permute-start.1
  19.9 2.0 %collective-permute-start.3 = (bf16[512,256]{1,0:T(8,128)(2,1)S(1)}, bf16[512,256]{1,0:T(8,128)(2,1)S(1)}, u32[]{:S(2)}, u32[]{:S(2)}) collective-permute-start(bf16[512,256]{1,0:T(8,128)(2,1)S(1)} %copy-done.20), channel_id=1, source_target_pairs={{0,0},{1,32},{2,64},{3,96},{4,16},{5,48},{6,80},{7,112},{8,128},{9... | collective-permute-start | bytes 786440 | tf_op jit(solution)/shard_map/ppermute | solution.py:27
  21.9 8.3 %collective-permute-start.4 = (bf16[512,256]{1,0:T(8,128)(2,1)S(1)}, bf16[512,256]{1,0:T(8,128)(2,1)S(1)}, u32[]{:S(2)}, u32[]{:S(2)}) collective-permute-start(bf16[512,256]{1,0:T(8,128)(2,1)S(1)} %copy-done.20), channel_id=1, source_target_pairs={{0,256},{1,288},{2,320},{3,352},{4,272},{5,304},{6,336},{7,368},{8... | collective-permute-start | bytes 786440 | tf_op jit(solution)/shard_map/ppermute | solution.py:27
  30.2 2.0 %collective-permute-start.2 = (f32[16,512]{1,0:T(8,128)S(1)}, f32[16,512]{1,0:T(8,128)S(1)}, u32[]{:S(2)}, u32[]{:S(2)}) collective-permute-start(f32[16,512]{1,0:T(8,128)S(1)} %collective-permute-done.1), channel_id=1, source_target_pairs={{0,16},{1,17},{2,18},{3,19},{4,20},{5,21},{6,22},{7,23},{8,24},{9,... | collective-permute-start | bytes 98312 | tf_op jit(solution)/shard_map/ppermute | solution.py:32
  32.2 10.3 %collective-permute-done.2 = f32[16,512]{1,0:T(8,128)S(1)} collective-permute-done((f32[16,512]{1,0:T(8,128)S(1)}, f32[16,512]{1,0:T(8,128)S(1)}, u32[]{:S(2)}, u32[]{:S(2)}) %collective-permute-start.2) | collective-permute-done | bytes 32800 | tf_op jit(solution)/shard_map/ppermute | solution.py:32
  42.5 14.2 %collective-permute-done.3 = bf16[512,256]{1,0:T(8,128)(2,1)S(1)} collective-permute-done((bf16[512,256]{1,0:T(8,128)(2,1)S(1)}, bf16[512,256]{1,0:T(8,128)(2,1)S(1)}, u32[]{:S(2)}, u32[]{:S(2)}) %collective-permute-start.3) | collective-permute-done | bytes 262176 | tf_op jit(solution)/shard_map/ppermute | solution.py:27
  56.9 1.9 collective-permute-start.5
  58.8 9.9 %collective-permute-done.5 = f32[16,512]{1,0:T(8,128)S(1)} collective-permute-done((f32[16,512]{1,0:T(8,128)S(1)}, f32[16,512]{1,0:T(8,128)S(1)}, u32[]{:S(2)}, u32[]{:S(2)}) %collective-permute-start.5) | collective-permute-done | bytes 32800 | tf_op jit(solution)/shard_map/ppermute | solution.py:32
  69.4 1.9 collective-permute-start.6
  71.3 1.9 collective-permute-start.10
  73.2 3.9 %collective-permute-start.9 = (bf16[1024,256]{1,0:T(8,128)(2,1)S(1)}, bf16[1024,256]{1,0:T(8,128)(2,1)S(1)}, u32[]{:S(2)}, u32[]{:S(2)}) collective-permute-start(bf16[1024,256]{1,0:T(8,128)(2,1)S(1)} %pad_maximum_fusion.refs_8_), channel_id=1, source_target_pairs={{0,32},{1,33},{2,34},{3,35},{4,36},{5,37},{6,38},{7,39},{8,40},{9,... | collective-permute-start | bytes 1572872 | tf_op jit(solution)/shard_map/ppermute | solution.py:27
  77.1 5.7 %collective-permute-done.6 = f32[16,512]{1,0:T(8,128)S(1)} collective-permute-done((f32[16,512]{1,0:T(8,128)S(1)}, f32[16,512]{1,0:T(8,128)S(1)}, u32[]{:S(2)}, u32[]{:S(2)}) %collective-permute-start.6) | collective-permute-done | bytes 32800 | tf_op jit(solution)/shard_map/ppermute | solution.py:32
  82.9 1.9 collective-permute-start.7
  84.8 12.6 %collective-permute-done.7 = f32[16,512]{1,0:T(8,128)S(1)} collective-permute-done((f32[16,512]{1,0:T(8,128)S(1)}, f32[16,512]{1,0:T(8,128)S(1)}, u32[]{:S(2)}, u32[]{:S(2)}) %collective-permute-start.7) | collective-permute-done | bytes 32800 | tf_op jit(solution)/shard_map/ppermute | solution.py:32
  97.4 1.3 collective-permute-start.8
  98.7 8.4 %collective-permute-done.8 = f32[16,512]{1,0:T(8,128)S(1)} collective-permute-done((f32[16,512]{1,0:T(8,128)S(1)}, f32[16,512]{1,0:T(8,128)S(1)}, u32[]{:S(2)}, u32[]{:S(2)}) %collective-permute-start.8) | collective-permute-done | bytes 32800 | tf_op jit(solution)/shard_map/ppermute | solution.py:32
  107.8 2.9 %back.1 = bf16[128,512]{1,0:T(8,128)(2,1)} custom-call(f32[128,512]{1,0:T(8,128)} %get-tuple-element.23.query_ref, f32[512,128]{1,0:T(8,128)} %get-tuple-element.24.drive_ref, f32[128,128]{1,0:T(8,128)} %get-tuple-element.25.half_ref, f32[16,512]{1,0:T(8,128)} %multiply_add_fusion.in_ref, f32[16,512]{1,0:T(8,128)} %rate_ref.3, ...), custom_call_target="tpu_custom_call" | custom-call | flops 1 | bytes 1 | tf_op jit(solution)/shard_map/back/pallas_call | solution.py:196
  110.7 2.0 %collective-permute-start.11 = (bf16[128,512]{1,0:T(8,128)(2,1)}, bf16[128,512]{1,0:T(8,128)(2,1)S(1)}, u32[]{:S(2)}, u32[]{:S(2)}) collective-permute-start(bf16[128,512]{1,0:T(8,128)(2,1)} %back.1), channel_id=1, source_target_pairs={{0,16},{1,17},{2,18},{3,19},{4,20},{5,21},{6,22},{7,23},{8,24},{9,... | collective-permute-start | bytes 393224 | tf_op jit(solution)/shard_map/ppermute | solution.py:27
  112.7 1.5 collective-permute-done.11
  114.3 0.9 pad_maximum_fusion.1.refs_0_
  115.2 1.9 collective-permute-start.12
  117.1 2.1 %collective-permute-start.15 = (bf16[1024,256]{1,0:T(8,128)(2,1)S(1)}, bf16[1024,256]{1,0:T(8,128)(2,1)S(1)}, u32[]{:S(2)}, u32[]{:S(2)}) collective-permute-start(bf16[1024,256]{1,0:T(8,128)(2,1)S(1)} %collective-permute-done.9.refs_9_), channel_id=1, source_target_pairs={{0,32},{1,33},{2,34},{3,35},{4,36},{5,37},{6,38},{7,39},{8,40},{9,... | collective-permute-start | bytes 1572872 | tf_op jit(solution)/shard_map/ppermute | solution.py:27
  119.3 4.9 %collective-permute-start.16 = (bf16[1024,256]{1,0:T(8,128)(2,1)S(1)}, bf16[1024,256]{1,0:T(8,128)(2,1)S(1)}, u32[]{:S(2)}, u32[]{:S(2)}) collective-permute-start(bf16[1024,256]{1,0:T(8,128)(2,1)S(1)} %collective-permute-done.10.refs_10_), channel_id=1, source_target_pairs={{0,224},{1,225},{2,226},{3,227},{4,228},{5,229},{6,230},{7,231},{8... | collective-permute-start | bytes 1572872 | tf_op jit(solution)/shard_map/ppermute | solution.py:27
  124.2 10.7 %collective-permute-start.13 = (bf16[256,512]{1,0:T(8,128)(2,1)S(1)}, bf16[256,512]{1,0:T(8,128)(2,1)S(1)}, u32[]{:S(2)}, u32[]{:S(2)}) collective-permute-start(bf16[256,512]{1,0:T(8,128)(2,1)S(1)} %pad_maximum_fusion.1.refs_0_), channel_id=1, source_target_pairs={{0,2},{1,3},{2,0},{3,1},{8,10},{9,11},{10,8},{11,9},{20,22},{21,23... | collective-permute-start | bytes 786440 | tf_op jit(solution)/shard_map/ppermute | solution.py:27
  134.9 1.9 collective-permute-start.14
  137.6 4.4 %collective-permute-done.13.refs_2_ = bf16[256,512]{1,0:T(8,128)(2,1)S(1)} collective-permute-done((bf16[256,512]{1,0:T(8,128)(2,1)S(1)}, bf16[256,512]{1,0:T(8,128)(2,1)S(1)}, u32[]{:S(2)}, u32[]{:S(2)}) %collective-permute-start.13) | collective-permute-done | bytes 262176 | tf_op jit(solution)/shard_map/ppermute | solution.py:27
  142.8 2.2 %collective-permute-done.14.refs_3_ = bf16[256,512]{1,0:T(8,128)(2,1)S(1)} collective-permute-done((bf16[256,512]{1,0:T(8,128)(2,1)S(1)}, bf16[256,512]{1,0:T(8,128)(2,1)S(1)}, u32[]{:S(2)}, u32[]{:S(2)}) %collective-permute-start.14) | collective-permute-done | bytes 262176 | tf_op jit(solution)/shard_map/ppermute | solution.py:27
  145.8 1.4 collective-permute-start.17
  147.1 1.4 collective-permute-start.18
  148.5 1.9 collective-permute-start.19
  150.4 5.1 %collective-permute-start.20 = (bf16[1024,256]{1,0:T(8,128)(2,1)S(1)}, bf16[1024,256]{1,0:T(8,128)(2,1)S(1)}, u32[]{:S(2)}, u32[]{:S(2)}) collective-permute-start(bf16[1024,256]{1,0:T(8,128)(2,1)S(1)} %collective-permute-done.16.refs_12_), channel_id=1, source_target_pairs={{0,224},{1,225},{2,226},{3,227},{4,228},{5,229},{6,230},{7,231},{8... | collective-permute-start | bytes 1572872 | tf_op jit(solution)/shard_map/ppermute | solution.py:27
  155.6 5.2 %collective-permute-done.19.refs_13_ = bf16[1024,256]{1,0:T(8,128)(2,1)S(1)} collective-permute-done((bf16[1024,256]{1,0:T(8,128)(2,1)S(1)}, bf16[1024,256]{1,0:T(8,128)(2,1)S(1)}, u32[]{:S(2)}, u32[]{:S(2)}) %collective-permute-start.19) | collective-permute-done | bytes 524320 | tf_op jit(solution)/shard_map/ppermute | solution.py:27
  160.8 1.5 collective-permute-done.20.refs_14_
  162.3 1.3 collective-permute-start.21
  163.6 1.3 collective-permute-start.22
  165.7 1.9 collective-permute-start.23
  168.3 5.6 %collective-permute-start.24 = (bf16[512,256]{1,0:T(8,128)(2,1)}, bf16[512,256]{1,0:T(8,128)(2,1)}, u32[]{:S(2)}, u32[]{:S(2)}) collective-permute-start(bf16[512,256]{1,0:T(8,128)(2,1)} %slice.19), channel_id=1, source_target_pairs={{0,224},{1,225},{2,226},{3,227},{4,228},{5,229},{6,230},{7,231},{8... | collective-permute-start | bytes 786440 | tf_op jit(solution)/shard_map/ppermute | solution.py:27
  174.9 2.4 %collective-permute-done.23.refs_15_ = bf16[512,256]{1,0:T(8,128)(2,1)S(1)} collective-permute-done((bf16[512,256]{1,0:T(8,128)(2,1)}, bf16[512,256]{1,0:T(8,128)(2,1)S(1)}, u32[]{:S(2)}, u32[]{:S(2)}) %collective-permute-start.23) | collective-permute-done | bytes 262176 | tf_op jit(solution)/shard_map/ppermute | solution.py:27
  177.3 2.6 %collective-permute-done.24.refs_16_ = bf16[512,256]{1,0:T(8,128)(2,1)} collective-permute-done((bf16[512,256]{1,0:T(8,128)(2,1)}, bf16[512,256]{1,0:T(8,128)(2,1)}, u32[]{:S(2)}, u32[]{:S(2)}) %collective-permute-start.24) | collective-permute-done | bytes 262176 | tf_op jit(solution)/shard_map/ppermute | solution.py:27
  179.9 0.8 copy-done.15
  181.5 5.0 %mix.1 = (f32[128,512]{1,0:T(8,128)}, f32[128,512]{1,0:T(8,128)}) custom-call(s32[13]{0:T(128)} %stack.59.table_ref, bf16[256,512]{1,0:T(8,128)(2,1)} %copy-done.7, bf16[256,512]{1,0:T(8,128)(2,1)} %copy-done.8, bf16[256,512]{1,0:T(8,128)(2,1)} %copy-done.9, bf16[256,512]{1,0:T(8,128)(2,1)} %copy-done.10, bf16[1024,512]{1,0:T(8,128)(2,1)} %copy-done, ...), custom_call_target="tpu_custom_call" | custom-call | flops 1100000000 | bytes 7000000 | tf_op jit(solution)/shard_map/mix/pallas_call | solution.py:209
  186.5 4.1 %collective-permute-start.25 = (f32[128,512]{1,0:T(8,128)}, f32[128,512]{1,0:T(8,128)S(1)}, u32[]{:S(2)}, u32[]{:S(2)}) collective-permute-start(f32[128,512]{1,0:T(8,128)} %get-tuple-element.40), channel_id=1, source_target_pairs={{0,16},{1,17},{2,18},{3,19},{4,20},{5,21},{6,22},{7,23},{8,24},{9,... | collective-permute-start | bytes 786440 | tf_op jit(solution)/shard_map/ppermute | solution.py:27
  190.6 1.4 collective-permute-done.25
  191.9 1.6 add_convert_fusion
  (68 shorter events, 7.2 us)
Async XLA Ops:
  0.0 19.9 %copy-start.20 = (bf16[512,256]{1,0:T(8,128)(2,1)S(1)}, bf16[512,256]{1,0:T(8,128)(2,1)}, u32[]{:S(2)}) copy-start(bf16[512,256]{1,0:T(8,128)(2,1)} %param.11) | copy-start | bytes 786436
  0.8 13.9 %collective-permute-start = (bf16[2,3,512]{2,0,1:T(2,128)(2,1)S(1)}, bf16[2,3,512]{2,0,1:T(2,128)(2,1)S(1)}, u32[]{:S(2)}, u32[]{:S(2)}) collective-permute-start(bf16[2,3,512]{2,0,1:T(2,128)(2,1)S(1)} %slice.15), channel_id=1, source_target_pairs={{0,16},{1,17},{2,18},{3,19},{4,20},{5,21},{6,22},{7,23},{8,24},{9,... | collective-permute-start | bytes 18440 | tf_op jit(solution)/shard_map/ppermute | solution.py:32
  14.7 0.6 copy-start.19
  15.3 27.2 %copy-start.3 = (f32[16,512]{1,0:T(8,128)S(1)}, f32[16,512]{1,0:T(8,128)}, u32[]{:S(2)}) copy-start(f32[16,512]{1,0:T(8,128)} %rate_ref.3) | copy-start | bytes 98308
  18.0 12.3 %collective-permute-start.1 = (f32[16,512]{1,0:T(8,128)}, f32[16,512]{1,0:T(8,128)S(1)}, u32[]{:S(2)}, u32[]{:S(2)}) collective-permute-start(f32[16,512]{1,0:T(8,128)} %get-tuple-element.26), channel_id=1, source_target_pairs={{0,16},{1,17},{2,18},{3,19},{4,20},{5,21},{6,22},{7,23},{8,24},{9,... | collective-permute-start | bytes 98312 | tf_op jit(solution)/shard_map/ppermute | solution.py:32
  19.9 36.8 %collective-permute-start.3 = (bf16[512,256]{1,0:T(8,128)(2,1)S(1)}, bf16[512,256]{1,0:T(8,128)(2,1)S(1)}, u32[]{:S(2)}, u32[]{:S(2)}) collective-permute-start(bf16[512,256]{1,0:T(8,128)(2,1)S(1)} %copy-done.20), channel_id=1, source_target_pairs={{0,0},{1,32},{2,64},{3,96},{4,16},{5,48},{6,80},{7,112},{8,128},{9... | collective-permute-start | bytes 786440 | tf_op jit(solution)/shard_map/ppermute | solution.py:27
  21.9 35.0 %collective-permute-start.4 = (bf16[512,256]{1,0:T(8,128)(2,1)S(1)}, bf16[512,256]{1,0:T(8,128)(2,1)S(1)}, u32[]{:S(2)}, u32[]{:S(2)}) collective-permute-start(bf16[512,256]{1,0:T(8,128)(2,1)S(1)} %copy-done.20), channel_id=1, source_target_pairs={{0,256},{1,288},{2,320},{3,352},{4,272},{5,304},{6,336},{7,368},{8... | collective-permute-start | bytes 786440 | tf_op jit(solution)/shard_map/ppermute | solution.py:27
  30.2 12.3 %collective-permute-start.2 = (f32[16,512]{1,0:T(8,128)S(1)}, f32[16,512]{1,0:T(8,128)S(1)}, u32[]{:S(2)}, u32[]{:S(2)}) collective-permute-start(f32[16,512]{1,0:T(8,128)S(1)} %collective-permute-done.1), channel_id=1, source_target_pairs={{0,16},{1,17},{2,18},{3,19},{4,20},{5,21},{6,22},{7,23},{8,24},{9,... | collective-permute-start | bytes 98312 | tf_op jit(solution)/shard_map/ppermute | solution.py:32
  42.5 26.2 %copy-start.18 = (f32[16,512]{1,0:T(8,128)S(1)}, f32[16,512]{1,0:T(8,128)}, u32[]{:S(2)}) copy-start(f32[16,512]{1,0:T(8,128)} %param.9) | copy-start | bytes 98308
  56.9 53.8 %copy-start.2 = (bf16[1024,256]{1,0:T(8,128)(2,1)}, bf16[1024,256]{1,0:T(8,128)(2,1)S(1)}, u32[]{:S(2)}) copy-start(bf16[1024,256]{1,0:T(8,128)(2,1)S(1)} %pad_maximum_fusion.refs_8_) | copy-start | bytes 1572868
  56.9 11.8 %collective-permute-start.5 = (f32[16,512]{1,0:T(8,128)S(1)}, f32[16,512]{1,0:T(8,128)S(1)}, u32[]{:S(2)}, u32[]{:S(2)}) collective-permute-start(f32[16,512]{1,0:T(8,128)S(1)} %multiply_add_fusion.4), channel_id=1, source_target_pairs={{0,32},{1,33},{2,34},{3,35},{4,36},{5,37},{6,38},{7,39},{8,40},{9,... | collective-permute-start | bytes 98312 | tf_op jit(solution)/shard_map/ppermute | solution.py:32
  69.4 13.5 %collective-permute-start.6 = (f32[16,512]{1,0:T(8,128)S(1)}, f32[16,512]{1,0:T(8,128)S(1)}, u32[]{:S(2)}, u32[]{:S(2)}) collective-permute-start(f32[16,512]{1,0:T(8,128)S(1)} %get-tuple-element.42), channel_id=1, source_target_pairs={{0,64},{1,65},{2,66},{3,67},{4,68},{5,69},{6,70},{7,71},{8,72},{9,... | collective-permute-start | bytes 98312 | tf_op jit(solution)/shard_map/ppermute | solution.py:32
  71.3 36.5 %collective-permute-start.10 = (bf16[1024,256]{1,0:T(8,128)(2,1)S(1)}, bf16[1024,256]{1,0:T(8,128)(2,1)S(1)}, u32[]{:S(2)}, u32[]{:S(2)}) collective-permute-start(bf16[1024,256]{1,0:T(8,128)(2,1)S(1)} %pad_maximum_fusion.refs_8_), channel_id=1, source_target_pairs={{0,224},{1,225},{2,226},{3,227},{4,228},{5,229},{6,230},{7,231},{8... | collective-permute-start | bytes 1572872 | tf_op jit(solution)/shard_map/ppermute | solution.py:27
  73.2 34.6 %collective-permute-start.9 = (bf16[1024,256]{1,0:T(8,128)(2,1)S(1)}, bf16[1024,256]{1,0:T(8,128)(2,1)S(1)}, u32[]{:S(2)}, u32[]{:S(2)}) collective-permute-start(bf16[1024,256]{1,0:T(8,128)(2,1)S(1)} %pad_maximum_fusion.refs_8_), channel_id=1, source_target_pairs={{0,32},{1,33},{2,34},{3,35},{4,36},{5,37},{6,38},{7,39},{8,40},{9,... | collective-permute-start | bytes 1572872 | tf_op jit(solution)/shard_map/ppermute | solution.py:27
  82.9 14.5 %collective-permute-start.7 = (f32[16,512]{1,0:T(8,128)S(1)}, f32[16,512]{1,0:T(8,128)S(1)}, u32[]{:S(2)}, u32[]{:S(2)}) collective-permute-start(f32[16,512]{1,0:T(8,128)S(1)} %multiply_add_fusion.2), channel_id=1, source_target_pairs={{0,128},{1,129},{2,130},{3,131},{4,132},{5,133},{6,134},{7,135},{8... | collective-permute-start | bytes 98312 | tf_op jit(solution)/shard_map/ppermute | solution.py:32
  97.4 9.7 %collective-permute-start.8 = (f32[16,512]{1,0:T(8,128)S(1)}, f32[16,512]{1,0:T(8,128)S(1)}, u32[]{:S(2)}, u32[]{:S(2)}) collective-permute-start(f32[16,512]{1,0:T(8,128)S(1)} %multiply_add_fusion.1), channel_id=1, source_target_pairs={{0,256},{1,257},{2,258},{3,259},{4,260},{5,261},{6,262},{7,263},{8... | collective-permute-start | bytes 98312 | tf_op jit(solution)/shard_map/ppermute | solution.py:32
  107.8 11.5 %copy-start.11 = (bf16[1024,256]{1,0:T(8,128)(2,1)}, bf16[1024,256]{1,0:T(8,128)(2,1)S(1)}, u32[]{:S(2)}) copy-start(bf16[1024,256]{1,0:T(8,128)(2,1)S(1)} %collective-permute-done.10.refs_10_) | copy-start | bytes 1572868
  107.8 9.4 %copy-start.12 = (bf16[1024,256]{1,0:T(8,128)(2,1)}, bf16[1024,256]{1,0:T(8,128)(2,1)S(1)}, u32[]{:S(2)}) copy-start(bf16[1024,256]{1,0:T(8,128)(2,1)S(1)} %collective-permute-done.9.refs_9_) | copy-start | bytes 1572868
  110.7 24.2 %copy-start.6 = (bf16[128,512]{1,0:T(8,128)(2,1)S(1)}, bf16[128,512]{1,0:T(8,128)(2,1)}, u32[]{:S(2)}) copy-start(bf16[128,512]{1,0:T(8,128)(2,1)} %back.1) | copy-start | bytes 393220
  110.7 3.6 %collective-permute-start.11 = (bf16[128,512]{1,0:T(8,128)(2,1)}, bf16[128,512]{1,0:T(8,128)(2,1)S(1)}, u32[]{:S(2)}, u32[]{:S(2)}) collective-permute-start(bf16[128,512]{1,0:T(8,128)(2,1)} %back.1), channel_id=1, source_target_pairs={{0,16},{1,17},{2,18},{3,19},{4,20},{5,21},{6,22},{7,23},{8,24},{9,... | collective-permute-start | bytes 393224 | tf_op jit(solution)/shard_map/ppermute | solution.py:27
  115.2 21.7 %copy-start.7 = (bf16[256,512]{1,0:T(8,128)(2,1)}, bf16[256,512]{1,0:T(8,128)(2,1)S(1)}, u32[]{:S(2)}) copy-start(bf16[256,512]{1,0:T(8,128)(2,1)S(1)} %pad_maximum_fusion.1.refs_0_) | copy-start | bytes 786436
  115.2 21.7 %collective-permute-start.12 = (bf16[256,512]{1,0:T(8,128)(2,1)S(1)}, bf16[256,512]{1,0:T(8,128)(2,1)S(1)}, u32[]{:S(2)}, u32[]{:S(2)}) collective-permute-start(bf16[256,512]{1,0:T(8,128)(2,1)S(1)} %pad_maximum_fusion.1.refs_0_), channel_id=1, source_target_pairs={{0,1},{1,2},{2,3},{3,0},{8,9},{9,10},{10,11},{11,8},{20,21},{21,22... | collective-permute-start | bytes 786440 | tf_op jit(solution)/shard_map/ppermute | solution.py:27
  117.1 28.6 %collective-permute-start.15 = (bf16[1024,256]{1,0:T(8,128)(2,1)S(1)}, bf16[1024,256]{1,0:T(8,128)(2,1)S(1)}, u32[]{:S(2)}, u32[]{:S(2)}) collective-permute-start(bf16[1024,256]{1,0:T(8,128)(2,1)S(1)} %collective-permute-done.9.refs_9_), channel_id=1, source_target_pairs={{0,32},{1,33},{2,34},{3,35},{4,36},{5,37},{6,38},{7,39},{8,40},{9,... | collective-permute-start | bytes 1572872 | tf_op jit(solution)/shard_map/ppermute | solution.py:27
  119.3 26.5 %collective-permute-start.16 = (bf16[1024,256]{1,0:T(8,128)(2,1)S(1)}, bf16[1024,256]{1,0:T(8,128)(2,1)S(1)}, u32[]{:S(2)}, u32[]{:S(2)}) collective-permute-start(bf16[1024,256]{1,0:T(8,128)(2,1)S(1)} %collective-permute-done.10.refs_10_), channel_id=1, source_target_pairs={{0,224},{1,225},{2,226},{3,227},{4,228},{5,229},{6,230},{7,231},{8... | collective-permute-start | bytes 1572872 | tf_op jit(solution)/shard_map/ppermute | solution.py:27
  124.2 17.8 %collective-permute-start.13 = (bf16[256,512]{1,0:T(8,128)(2,1)S(1)}, bf16[256,512]{1,0:T(8,128)(2,1)S(1)}, u32[]{:S(2)}, u32[]{:S(2)}) collective-permute-start(bf16[256,512]{1,0:T(8,128)(2,1)S(1)} %pad_maximum_fusion.1.refs_0_), channel_id=1, source_target_pairs={{0,2},{1,3},{2,0},{3,1},{8,10},{9,11},{10,8},{11,9},{20,22},{21,23... | collective-permute-start | bytes 786440 | tf_op jit(solution)/shard_map/ppermute | solution.py:27
  134.9 10.1 %collective-permute-start.14 = (bf16[256,512]{1,0:T(8,128)(2,1)S(1)}, bf16[256,512]{1,0:T(8,128)(2,1)S(1)}, u32[]{:S(2)}, u32[]{:S(2)}) collective-permute-start(bf16[256,512]{1,0:T(8,128)(2,1)S(1)} %pad_maximum_fusion.1.refs_0_), channel_id=1, source_target_pairs={{0,3},{1,0},{2,1},{3,2},{8,11},{9,8},{10,9},{11,10},{20,23},{21,20... | collective-permute-start | bytes 786440 | tf_op jit(solution)/shard_map/ppermute | solution.py:27
  136.9 0.7 copy-start.8
  142.1 0.7 copy-start.9
  145.0 0.7 copy-start.10
  145.7 22.6 %copy-start.13 = (bf16[1024,256]{1,0:T(8,128)(2,1)}, bf16[1024,256]{1,0:T(8,128)(2,1)S(1)}, u32[]{:S(2)}) copy-start(bf16[1024,256]{1,0:T(8,128)(2,1)S(1)} %collective-permute-done.15.refs_11_) | copy-start | bytes 1572868
  145.7 22.6 %copy-start.14 = (bf16[1024,256]{1,0:T(8,128)(2,1)}, bf16[1024,256]{1,0:T(8,128)(2,1)S(1)}, u32[]{:S(2)}) copy-start(bf16[1024,256]{1,0:T(8,128)(2,1)S(1)} %collective-permute-done.16.refs_12_) | copy-start | bytes 1572868
  145.8 16.5 %collective-permute-start.17 = (bf16[1024,512]{1,0:T(8,128)(2,1)S(1)}, bf16[1024,512]{1,0:T(8,128)(2,1)S(1)}, u32[]{:S(2)}, u32[]{:S(2)}) collective-permute-start(bf16[1024,512]{1,0:T(8,128)(2,1)S(1)} %constant_dynamic-update-slice_fusion), channel_id=1, source_target_pairs={{0,4},{1,5},{2,6},{3,7},{8,12},{9,13},{10,14},{11,15},{20,24},{21,... | collective-permute-start | bytes 3145736 | tf_op jit(solution)/shard_map/ppermute | solution.py:27
  147.1 15.1 %collective-permute-start.18 = (bf16[1024,512]{1,0:T(8,128)(2,1)S(1)}, bf16[1024,512]{1,0:T(8,128)(2,1)S(1)}, u32[]{:S(2)}, u32[]{:S(2)}) collective-permute-start(bf16[1024,512]{1,0:T(8,128)(2,1)S(1)} %constant_dynamic-update-slice_fusion), channel_id=1, source_target_pairs={{0,12},{1,13},{2,14},{3,15},{8,4},{9,5},{10,6},{11,7},{20,16},{21,... | collective-permute-start | bytes 3145736 | tf_op jit(solution)/shard_map/ppermute | solution.py:27
  148.5 12.3 %collective-permute-start.19 = (bf16[1024,256]{1,0:T(8,128)(2,1)S(1)}, bf16[1024,256]{1,0:T(8,128)(2,1)S(1)}, u32[]{:S(2)}, u32[]{:S(2)}) collective-permute-start(bf16[1024,256]{1,0:T(8,128)(2,1)S(1)} %collective-permute-done.15.refs_11_), channel_id=1, source_target_pairs={{0,32},{1,33},{2,34},{3,35},{4,36},{5,37},{6,38},{7,39},{8,40},{9,... | collective-permute-start | bytes 1572872 | tf_op jit(solution)/shard_map/ppermute | solution.py:27
  150.4 11.8 %collective-permute-start.20 = (bf16[1024,256]{1,0:T(8,128)(2,1)S(1)}, bf16[1024,256]{1,0:T(8,128)(2,1)S(1)}, u32[]{:S(2)}, u32[]{:S(2)}) collective-permute-start(bf16[1024,256]{1,0:T(8,128)(2,1)S(1)} %collective-permute-done.16.refs_12_), channel_id=1, source_target_pairs={{0,224},{1,225},{2,226},{3,227},{4,228},{5,229},{6,230},{7,231},{8... | collective-permute-start | bytes 1572872 | tf_op jit(solution)/shard_map/ppermute | solution.py:27
  160.8 4.2 %copy-start.4 = (bf16[1024,256]{1,0:T(8,128)(2,1)}, bf16[1024,256]{1,0:T(8,128)(2,1)S(1)}, u32[]{:S(2)}) copy-start(bf16[1024,256]{1,0:T(8,128)(2,1)S(1)} %collective-permute-done.19.refs_13_) | copy-start | bytes 1572868
  162.2 6.1 %copy-start.5 = (bf16[1024,256]{1,0:T(8,128)(2,1)}, bf16[1024,256]{1,0:T(8,128)(2,1)S(1)}, u32[]{:S(2)}) copy-start(bf16[1024,256]{1,0:T(8,128)(2,1)S(1)} %collective-permute-done.20.refs_14_) | copy-start | bytes 1572868
  162.2 3.5 %copy-start = (bf16[1024,512]{1,0:T(8,128)(2,1)}, bf16[1024,512]{1,0:T(8,128)(2,1)S(1)}, u32[]{:S(2)}) copy-start(bf16[1024,512]{1,0:T(8,128)(2,1)S(1)} %collective-permute-done.17.refs_4_) | copy-start | bytes 3145732
  162.2 3.5 %copy-start.1 = (bf16[1024,512]{1,0:T(8,128)(2,1)}, bf16[1024,512]{1,0:T(8,128)(2,1)S(1)}, u32[]{:S(2)}) copy-start(bf16[1024,512]{1,0:T(8,128)(2,1)S(1)} %collective-permute-done.18.refs_5_) | copy-start | bytes 3145732
  162.3 17.6 %collective-permute-start.21 = (bf16[512,512]{1,0:T(8,128)(2,1)S(1)}, bf16[512,512]{1,0:T(8,128)(2,1)S(1)}, u32[]{:S(2)}, u32[]{:S(2)}) collective-permute-start(bf16[512,512]{1,0:T(8,128)(2,1)S(1)} %slice.16), channel_id=1, source_target_pairs={{4,8},{5,9},{6,10},{7,11},{12,0},{13,1},{14,2},{15,3},{16,20},{17,... | collective-permute-start | bytes 1572872 | tf_op jit(solution)/shard_map/ppermute | solution.py:27
  163.6 16.2 %collective-permute-start.22 = (bf16[512,512]{1,0:T(8,128)(2,1)S(1)}, bf16[512,512]{1,0:T(8,128)(2,1)S(1)}, u32[]{:S(2)}, u32[]{:S(2)}) collective-permute-start(bf16[512,512]{1,0:T(8,128)(2,1)S(1)} %slice.17), channel_id=1, source_target_pairs={{4,0},{5,1},{6,2},{7,3},{12,8},{13,9},{14,10},{15,11},{16,28},{17,... | collective-permute-start | bytes 1572872 | tf_op jit(solution)/shard_map/ppermute | solution.py:27
  165.7 11.6 %collective-permute-start.23 = (bf16[512,256]{1,0:T(8,128)(2,1)}, bf16[512,256]{1,0:T(8,128)(2,1)S(1)}, u32[]{:S(2)}, u32[]{:S(2)}) collective-permute-start(bf16[512,256]{1,0:T(8,128)(2,1)} %slice.18), channel_id=1, source_target_pairs={{0,32},{1,33},{2,34},{3,35},{4,36},{5,37},{6,38},{7,39},{8,40},{9,... | collective-permute-start | bytes 786440 | tf_op jit(solution)/shard_map/ppermute | solution.py:27
  168.3 11.5 %collective-permute-start.24 = (bf16[512,256]{1,0:T(8,128)(2,1)}, bf16[512,256]{1,0:T(8,128)(2,1)}, u32[]{:S(2)}, u32[]{:S(2)}) collective-permute-start(bf16[512,256]{1,0:T(8,128)(2,1)} %slice.19), channel_id=1, source_target_pairs={{0,224},{1,225},{2,226},{3,227},{4,228},{5,229},{6,230},{7,231},{8... | collective-permute-start | bytes 786440 | tf_op jit(solution)/shard_map/ppermute | solution.py:27
  177.3 2.6 %copy-start.17 = (bf16[512,256]{1,0:T(8,128)(2,1)}, bf16[512,256]{1,0:T(8,128)(2,1)S(1)}, u32[]{:S(2)}) copy-start(bf16[512,256]{1,0:T(8,128)(2,1)S(1)} %collective-permute-done.23.refs_15_) | copy-start | bytes 786436
  179.9 0.8 copy-start.15
  180.7 0.8 copy-start.16
  186.5 5.5 %collective-permute-start.25 = (f32[128,512]{1,0:T(8,128)}, f32[128,512]{1,0:T(8,128)S(1)}, u32[]{:S(2)}, u32[]{:S(2)}) collective-permute-start(f32[128,512]{1,0:T(8,128)} %get-tuple-element.40), channel_id=1, source_target_pairs={{0,16},{1,17},{2,18},{3,19},{4,20},{5,21},{6,22},{7,23},{8,24},{9,... | collective-permute-start | bytes 786440 | tf_op jit(solution)/shard_map/ppermute | solution.py:27

commit v2 on v1

--- a/solution.py
+++ b/solution.py
@@ -111,66 +111,65 @@
 
 
 def mix_kernel(table_ref, *refs):
-    s, (fwd, bwd, hf, hb), weights = refs[:4], refs[4:8], refs[8:17]
-    keep_ref, send_ref, g, w, acc, g_sem, w_sem = refs[17:]
+    line, fwd, bwd, hf, hb = refs[:5]
+    weights = refs[5:14]
+    keep_ref, send_ref, g, w, acc, g_sem, w_sem = refs[14:]
     own = table_ref[0] == 1
     yl = table_ref[1]
-    low = table_ref[2] * 4
-    high = table_ref[3] * 4
-
-    def spot(base, j):
-        return g.at[base + lax.rem(yl - j + 4, 4)]
-
-    from_own = [(s[j], spot(low, j)) for j in range(4)]
-    from_own += [(hf.at[pl.ds(j * 256, 256), :], spot(high, j)) for j in range(2)]
-    from_own += [(hb.at[pl.ds(j * 256, 256), :], spot(high, 2 + j)) for j in range(2)]
-    from_others = [(fwd.at[pl.ds(j * 256, 256), :], spot(low, j)) for j in range(4)]
-    from_others += [(bwd.at[pl.ds(j * 256, 256), :], spot(high, j)) for j in range(4)]
-
-    def channel_copies(pairs):
-        return [pltpu.make_async_copy(a, b, g_sem.at[i]) for i, (a, b) in enumerate(pairs)]
+    low, high = table_ref[2], table_ref[3]
+
+    def from_own():
+        return [
+            pltpu.make_async_copy(line, g.at[low], g_sem.at[0]),
+            pltpu.make_async_copy(hf, g.at[high, pl.ds(0, 256)], g_sem.at[1]),
+            pltpu.make_async_copy(hb, g.at[high, pl.ds(256, 256)], g_sem.at[2]),
+        ]
+
+    def from_others():
+        return [
+            pltpu.make_async_copy(fwd, g.at[low], g_sem.at[0]),
+            pltpu.make_async_copy(bwd, g.at[high], g_sem.at[1]),
+        ]
 
     @pl.when(own)
     def _():
-        for copy in channel_copies(from_own):
+        for copy in from_own():
             copy.start()
 
     @pl.when(jnp.logical_not(own))
     def _():
-        for copy in channel_copies(from_others):
+        for copy in from_others():
             copy.start()
 
     loads = [pltpu.make_async_copy(weights[i], w.at[i], w_sem.at[i]) for i in range(7)]
-    loads += [pltpu.make_async_copy(weights[7 + p], w.at[7, pl.ds(p * 512, 512)], w_sem.at[7 + p]) for p in range(2)]
+    loads += [pltpu.make_async_copy(weights[7 + p], w.at[7, pl.ds(p * 256, 256)], w_sem.at[7 + p]) for p in range(2)]
     for copy in loads:
         copy.start()
+    acc[...] = jnp.zeros_like(acc)
 
     @pl.when(own)
     def _():
-        for copy in channel_copies(from_own):
+        for copy in from_own():
             copy.wait()
 
     @pl.when(jnp.logical_not(own))
     def _():
-        for copy in channel_copies(from_others):
+        for copy in from_others():
             copy.wait()
 
     for i in range(8):
         loads[i].wait()
         if i == 7:
             loads[8].wait()
-        block = g[table_ref[4 + i]]
-        for p in range(2):
-            part = jnp.dot(block, w[i, p * 512 : p * 512 + 512, :], preferred_element_type=jnp.float32)
-            acc[p] = part if i == 0 else acc[p] + part
-    for p in range(2):
-
-        @pl.when(table_ref[12] == p)
-        def _():
-            for half in range(2):
-                cols = slice(half * 256, half * 256 + 256)
-                keep_ref[:, cols] = acc[half ^ p, :128, :]
-                send_ref[:, cols] = acc[half ^ p, 128:, :]
+        place = table_ref[4 + i]
+        part = jnp.dot(g[lax.rem(place, 2)], w[i], preferred_element_type=jnp.float32)
+        acc[place // 2] += part.reshape(4, 128, 256)
+    for d in range(4):
+        block = lax.rem(yl + d, 4)
+        for half in range(2):
+            cols = slice(half * 256, half * 256 + 256)
+            keep_ref[d, :, cols] = acc[lax.rem(block, 2) * 2 + half, block // 2 * 2]
+            send_ref[d, :, cols] = acc[lax.rem(block, 2) * 2 + half, block // 2 * 2 + 1]
 
 
 def front(feat, halo, taps, rate):
@@ -205,17 +204,17 @@
 
 
 def mix(table, *operands):
-    out = jax.ShapeDtypeStruct((128, 512), jnp.float32)
+    out = jax.ShapeDtypeStruct((4, 128, 512), jnp.float32)
     return pl.pallas_call(
         mix_kernel,
         out_shape=(out, out),
         in_specs=[SMEM] + [pl.BlockSpec(memory_space=pl.ANY)] * len(operands),
         out_specs=(VMEM, VMEM),
         scratch_shapes=[
-            pltpu.VMEM((8, 256, 512), jnp.bfloat16),
-            pltpu.VMEM((8, 1024, 256), jnp.bfloat16),
-            pltpu.VMEM((2, 256, 256), jnp.float32),
-            pltpu.SemaphoreType.DMA((8,)),
+            pltpu.VMEM((2, 512, 512), jnp.bfloat16),
+            pltpu.VMEM((8, 512, 256), jnp.bfloat16),
+            pltpu.VMEM((4, 4, 128, 256), jnp.float32),
+            pltpu.SemaphoreType.DMA((3,)),
             pltpu.SemaphoreType.DMA((9,)),
         ],
         compiler_params=pltpu.CompilerParams(vmem_limit_bytes=60 * 1024 * 1024),
@@ -228,19 +227,15 @@
     n_modes, channels = decay_rate.shape
     positions = features.shape[0]
     index = lax.axis_index(axes)
-    yl, x, core, z, yh = index % 4, index // 4 % 4, index // 16 % 2, index // 32 % 8, index // 256
+    yl, x, core, z = index % 4, index // 4 % 4, index // 16 % 2, index // 32 % 8
 
     halo = from_behind(features[positions - 2 :], axes, 1)
 
-    def tile(p):
-        def target(yh, z, core, x, yl):
-            t = yh * 8 + z
-            return core ^ p, (x // 2) * 4 + yl, x % 2, t // 4, t % 4
-
-        return target
-
-    weight = jnp.concatenate([move(out_weight, axes, tile(p)) for p in range(2)], axis=0)
+    tie = lax.optimization_barrier
     rows = out_weight.shape[0]
+
+    def place(yh, z, core, x, yl):
+        return yh, z // 4 * 4 + core * 2 + x // 2, x % 2, z % 4, yl
 
     def along(axis, by):
         def target(yh, z, core, x, yl):
@@ -252,10 +247,16 @@
 
         return target
 
-    def other_core(value):
-        return move(value, axes, lambda yh, z, core, x, yl: (yh, z, 1 - core, x, yl))
-
-    tie = lax.optimization_barrier
+    def mine(yh, z, core, x, yl):
+        return x % 2 == core
+
+    def others(yh, z, core, x, yl):
+        return x % 2 != core
+
+    def other_core(value, sends=lambda *place: True):
+        return move(value, axes, lambda yh, z, core, x, yl: (yh, z, 1 - core, x, yl), sends)
+
+    weight = move(out_weight, axes, place)
     ups, downs = [weight], [weight]
 
     def ring():
@@ -263,38 +264,31 @@
         downs.append(move(downs[-1], axes, along("z", -1)))
 
     query, drive, half, end = front(features.transpose(1, 0, 2), halo.transpose(1, 0, 2), short_filter, decay_rate)
+    end, weight = tie((end, weight))
 
     incoming = from_behind(end, axes, 1)
     for k in range(5):
         by = 2**k
-        if k == 1:
-            incoming, ups[0] = tie((incoming, ups[0]))
-            downs[0] = ups[0]
-            ring()
         incoming = incoming + jnp.exp(-decay_rate * (positions * by)) * from_behind(incoming, axes, by)
 
     gain = residue * jnp.sqrt(-jnp.expm1(-2.0 * decay_rate))
-    incoming, ups[1], downs[1] = tie((incoming, ups[1], downs[1]))
+    incoming, weight = tie((incoming, weight))
+    ups[0] = downs[0] = weight
     ring()
     gated = back(query, drive, half, incoming, decay_rate, gain, skip[None])
 
-    both = jnp.concatenate([gated, other_core(gated)], axis=0)
-
-    def mine(yh, z, core, x, yl):
-        return x % 2 == core
-
-    def others(yh, z, core, x, yl):
-        return x % 2 != core
-
-    near = [both] + [move(both, axes, along("yl", j), mine) for j in range(1, 4)]
-    line = jnp.concatenate(near, axis=0)
+    both = jnp.concatenate([gated, other_core(gated, others)], axis=0)
+    both, ups[1], downs[1] = tie((both, ups[1], downs[1]))
+    ring()
+    beyond = move(both, axes, lambda yh, z, core, x, yl: (1 - yh, z, core, x, yl), mine)
+    line = jnp.concatenate([both, beyond], axis=0)
     line, ups[2], downs[2] = tie((line, ups[2], downs[2]))
     ring()
     fwd = move(line, axes, along("x", 1), mine)
     bwd = move(line, axes, along("x", -1), mine)
     fwd, bwd, ups[3], downs[3] = tie((fwd, bwd, ups[3], downs[3]))
-    up_last = move(ups[3][:rows], axes, along("z", 1))
-    down_last = move(downs[3][rows:], axes, along("z", -1))
+    up_last = move(ups[3][: rows // 2], axes, along("z", 1))
+    down_last = move(downs[3][rows // 2 :], axes, along("z", -1))
     weights = [ups[0], ups[1], downs[1], ups[2], downs[2], ups[3], downs[3], up_last, down_last]
     half_rows = line.shape[0] // 2
     hf = move(fwd[:half_rows], axes, along("x", 1), others)
@@ -304,9 +298,15 @@
     low = jnp.where(own, x // 2, (x + 3) % 4 // 2)
     high = jnp.where(own, 1 - x // 2, (x + 1) % 4 // 2)
     places = [(z - d) % 8 for d in (0, 1, -1, 2, -2, 3, -3, 4)]
-    table = jnp.stack([own.astype(jnp.int32), yl, low, high] + places + [yh]).astype(jnp.int32)
-    keep, send = mix(table, *near, fwd, bwd, hf, hb, *weights)
-    return (keep + other_core(send)).astype(jnp.bfloat16)
+    table = jnp.stack([own.astype(jnp.int32), yl, low, high] + places).astype(jnp.int32)
+    keep, send = mix(table, line, fwd, bwd, hf, hb, *weights)
+
+    blocks = keep + other_core(send)
+    parts = [move(blocks[d].astype(jnp.bfloat16), axes, along("yl", d)) for d in range(1, 4)]
+    total = blocks[0] + sum(part.astype(jnp.float32) for part in parts)
+    return move(
+        total.astype(jnp.bfloat16), axes, lambda yh, z, core, x, yl: (yh ^ (yl // 2), z, core, yh * 2 + yl % 2, x)
+    )
 
 
 def shards(*arguments):

time: 197 us -> 205 us (1.041); the launches traced: 194 us -> 204 us
  waiting for transfers between devices: 94.5 us -> 110 us
  starting transfers between devices: 76.6 us -> 72.2 us
  local copies, waits for them, and re-layouts: 7.27 us -> 4.96 us
    ppermute x7, waiting for transfers between devices: 58.9 us -> 71.5 us  [from_behind(): return lax.ppermute(value, axes, pairs)]
    ppermute x19 -> x20, starting transfers between devices: 63.7 us -> 54.6 us  [move(): return lax.ppermute(value, axes, pairs)]
    ppermute x7, starting transfers between devices: 12.8 us -> 17.5 us  [from_behind(): return lax.ppermute(value, axes, pairs)]
    ppermute x19 -> x20, waiting for transfers between devices: 35.6 us -> 38.4 us  [move(): return lax.ppermute(value, axes, pairs)]
    pallas_call x1, Pallas kernels: 4.98 us -> 7.21 us  [mix(): pl.pallas_call(mix_kernel, out_shape=(out, out), in_specs=[SMEM] + [pl.Bl...]
    unnamed x46 -> x35, local copies, waits for them, and re-layouts: 4.36 us -> 3.48 us
  transfers between devices with their start and end apart: 26 -> 27, of which waited for: 16 -> 18; matrix products, arithmetic and copies ran while one was open for 1% -> 1% of each run, Pallas kernels for 0% -> 3%
where the time goes in v2:
time: 205 us; the launch traced here: 204 us
  waiting for transfers between devices  110 us (54%)
  starting transfers between devices  72.2 us (35%)
  Pallas kernels  12.4 us (6%)
  local copies, waits for them, and re-layouts  4.96 us (2%)
  other arithmetic  3.82 us (2%)
    ppermute x7, waiting for transfers between devices, from_behind(): return lax.ppermute(value, axes, pairs)  71.5 us
    ppermute x20, starting transfers between devices, move(): return lax.ppermute(value, axes, pairs)  54.6 us
    ppermute x20, waiting for transfers between devices, move(): return lax.ppermute(value, axes, pairs)  38.4 us
    ppermute x7, starting transfers between devices, from_behind(): return lax.ppermute(value, axes, pairs)  17.5 us
    pallas_call x1, Pallas kernels, mix(): pl.pallas_call(mix_kernel, out_shape=(out, out), in_specs=[SMEM] + [pl.Bl...  7.21 us
  transfers between devices with their start and end apart: 27, of which 18 were waited for; matrix products, arithmetic and copies ran while one was open for 1% of the time, Pallas kernels for 3%

profile of v2, /device:TPU:56, one launch (start us, length us, event | category | flops | bytes accessed | tf_op | source)
XLA Modules:
  0.0 204.1 jit_solution(6248114083798421225)
XLA Ops:
  0.0 1.6 collective-permute-start.1
  2.3 6.5 %collective-permute-start = (bf16[2,3,512]{2,0,1:T(2,128)(2,1)S(1)}, bf16[2,3,512]{2,0,1:T(2,128)(2,1)S(1)}, u32[]{:S(2)}, u32[]{:S(2)}) collective-permute-start(bf16[2,3,512]{2,0,1:T(2,128)(2,1)S(1)} %slice.30), channel_id=1, source_target_pairs={{0,16},{1,17},{2,18},{3,19},{4,20},{5,21},{6,22},{7,23},{8,24},{9,... | collective-permute-start | bytes 18440 | tf_op jit(solution)/shard_map/ppermute | solution.py:32
  8.9 10.8 %collective-permute-done = bf16[2,3,512]{2,0,1:T(2,128)(2,1)S(1)} collective-permute-done((bf16[2,3,512]{2,0,1:T(2,128)(2,1)S(1)}, bf16[2,3,512]{2,0,1:T(2,128)(2,1)S(1)}, u32[]{:S(2)}, u32[]{:S(2)}) %collective-permute-start) | collective-permute-done | bytes 6176 | tf_op jit(solution)/shard_map/ppermute | solution.py:32
  20.2 2.6 %front.1 = (f32[128,512]{1,0:T(8,128)}, f32[512,128]{1,0:T(8,128)}, f32[128,128]{1,0:T(8,128)}, f32[16,512]{1,0:T(8,128)}) custom-call(bf16[3,128,512]{2,1,0:T(8,128)(2,1)} %bitcast.27, bf16[3,2,512]{2,1,0:T(2,128)(2,1)} %bitcast.28, f32[3,3,512]{2,1,0:T(4,128)} %taps_ref.1, f32[16,512]{1,0:T(8,128)} %rate_ref.3), custom_call_target="tpu_custom_call" | custom-call | flops 1 | bytes 1 | tf_op jit(solution)/shard_map/front/pallas_call | solution.py:177
  22.9 2.1 %collective-permute-start.2 = (f32[16,512]{1,0:T(8,128)}, f32[16,512]{1,0:T(8,128)S(1)}, u32[]{:S(2)}, u32[]{:S(2)}) collective-permute-start(f32[16,512]{1,0:T(8,128)} %get-tuple-element.29), channel_id=1, source_target_pairs={{0,16},{1,17},{2,18},{3,19},{4,20},{5,21},{6,22},{7,23},{8,24},{9,... | collective-permute-start | bytes 98312 | tf_op jit(solution)/shard_map/ppermute | solution.py:32
  24.9 9.5 %collective-permute-done.2 = f32[16,512]{1,0:T(8,128)S(1)} collective-permute-done((f32[16,512]{1,0:T(8,128)}, f32[16,512]{1,0:T(8,128)S(1)}, u32[]{:S(2)}, u32[]{:S(2)}) %collective-permute-start.2) | collective-permute-done | bytes 32800 | tf_op jit(solution)/shard_map/ppermute | solution.py:32
  34.5 1.9 collective-permute-start.3
  36.4 9.3 %collective-permute-done.3 = f32[16,512]{1,0:T(8,128)S(1)} collective-permute-done((f32[16,512]{1,0:T(8,128)S(1)}, f32[16,512]{1,0:T(8,128)S(1)}, u32[]{:S(2)}, u32[]{:S(2)}) %collective-permute-start.3) | collective-permute-done | bytes 32800 | tf_op jit(solution)/shard_map/ppermute | solution.py:32
  45.7 1.9 collective-permute-start.4
  47.7 10.0 %collective-permute-done.4 = f32[16,512]{1,0:T(8,128)S(1)} collective-permute-done((f32[16,512]{1,0:T(8,128)S(1)}, f32[16,512]{1,0:T(8,128)S(1)}, u32[]{:S(2)}, u32[]{:S(2)}) %collective-permute-start.4) | collective-permute-done | bytes 32800 | tf_op jit(solution)/shard_map/ppermute | solution.py:32
  58.3 1.9 collective-permute-start.5
  60.2 10.8 %collective-permute-done.5 = f32[16,512]{1,0:T(8,128)S(1)} collective-permute-done((f32[16,512]{1,0:T(8,128)S(1)}, f32[16,512]{1,0:T(8,128)S(1)}, u32[]{:S(2)}, u32[]{:S(2)}) %collective-permute-start.5) | collective-permute-done | bytes 32800 | tf_op jit(solution)/shard_map/ppermute | solution.py:32
  71.0 1.9 collective-permute-start.6
  73.0 12.7 %collective-permute-done.6 = f32[16,512]{1,0:T(8,128)S(1)} collective-permute-done((f32[16,512]{1,0:T(8,128)S(1)}, f32[16,512]{1,0:T(8,128)S(1)}, u32[]{:S(2)}, u32[]{:S(2)}) %collective-permute-start.6) | collective-permute-done | bytes 32800 | tf_op jit(solution)/shard_map/ppermute | solution.py:32
  85.7 1.3 collective-permute-start.7
  87.0 8.4 %collective-permute-done.7 = f32[16,512]{1,0:T(8,128)S(1)} collective-permute-done((f32[16,512]{1,0:T(8,128)S(1)}, f32[16,512]{1,0:T(8,128)S(1)}, u32[]{:S(2)}, u32[]{:S(2)}) %collective-permute-start.7) | collective-permute-done | bytes 32800 | tf_op jit(solution)/shard_map/ppermute | solution.py:32
  96.1 1.9 collective-permute-start.10
  98.0 3.9 %collective-permute-start.9 = (bf16[512,256]{1,0:T(8,128)(2,1)S(1)}, bf16[512,256]{1,0:T(8,128)(2,1)S(1)}, u32[]{:S(2)}, u32[]{:S(2)}) collective-permute-start(bf16[512,256]{1,0:T(8,128)(2,1)S(1)} %collective-permute-done.1.refs_5_), channel_id=1, source_target_pairs={{0,32},{1,33},{2,34},{3,35},{4,36},{5,37},{6,38},{7,39},{8,40},{9,... | collective-permute-start | bytes 786440 | tf_op jit(solution)/shard_map/ppermute | solution.py:27
  101.9 2.5 %back.1 = bf16[128,512]{1,0:T(8,128)(2,1)} custom-call(f32[128,512]{1,0:T(8,128)} %get-tuple-element.25.query_ref, f32[512,128]{1,0:T(8,128)} %get-tuple-element.26.drive_ref, f32[128,128]{1,0:T(8,128)} %get-tuple-element.27.half_ref, f32[16,512]{1,0:T(8,128)} %multiply_add_fusion.in_ref, f32[16,512]{1,0:T(8,128)} %rate_ref.3, ...), custom_call_target="tpu_custom_call" | custom-call | flops 1 | bytes 1 | tf_op jit(solution)/shard_map/back/pallas_call | solution.py:195
  104.4 1.3 collective-permute-start.8
  105.7 2.2 %collective-permute-done.8 = bf16[128,512]{1,0:T(8,128)(2,1)S(1)} collective-permute-done((bf16[128,512]{1,0:T(8,128)(2,1)}, bf16[128,512]{1,0:T(8,128)(2,1)S(1)}, u32[]{:S(2)}, u32[]{:S(2)}) %collective-permute-start.8) | collective-permute-done | bytes 131104 | tf_op jit(solution)/shard_map/ppermute | solution.py:27
  107.9 0.9 pad_maximum_fusion.1
  108.9 1.9 collective-permute-start.11
  110.8 1.9 collective-permute-start.12
  112.7 5.1 %collective-permute-start.13 = (bf16[512,256]{1,0:T(8,128)(2,1)S(1)}, bf16[512,256]{1,0:T(8,128)(2,1)S(1)}, u32[]{:S(2)}, u32[]{:S(2)}) collective-permute-start(bf16[512,256]{1,0:T(8,128)(2,1)S(1)} %collective-permute-done.10.refs_7_), channel_id=1, source_target_pairs={{0,224},{1,225},{2,226},{3,227},{4,228},{5,229},{6,230},{7,231},{8... | collective-permute-start | bytes 786440 | tf_op jit(solution)/shard_map/ppermute | solution.py:27
  117.8 3.9 %collective-permute-done.11 = bf16[256,512]{1,0:T(8,128)(2,1)S(1)} collective-permute-done((bf16[256,512]{1,0:T(8,128)(2,1)S(1)}, bf16[256,512]{1,0:T(8,128)(2,1)S(1)}, u32[]{:S(2)}, u32[]{:S(2)}) %collective-permute-start.11) | collective-permute-done | bytes 262176 | tf_op jit(solution)/shard_map/ppermute | solution.py:27
  122.2 1.3 collective-permute-start.15
  123.5 2.1 %collective-permute-start.14 = (bf16[512,512]{1,0:T(8,128)(2,1)S(1)}, bf16[512,512]{1,0:T(8,128)(2,1)S(1)}, u32[]{:S(2)}, u32[]{:S(2)}) collective-permute-start(bf16[512,512]{1,0:T(8,128)(2,1)S(1)} %pad_maximum_fusion.refs_0_), channel_id=1, source_target_pairs={{0,4},{1,5},{2,6},{3,7},{8,12},{9,13},{10,14},{11,15},{20,24},{21,... | collective-permute-start | bytes 1572872 | tf_op jit(solution)/shard_map/ppermute | solution.py:27
  125.6 1.9 collective-permute-start.16
  127.5 5.6 %collective-permute-start.17 = (bf16[512,256]{1,0:T(8,128)(2,1)S(1)}, bf16[512,256]{1,0:T(8,128)(2,1)S(1)}, u32[]{:S(2)}, u32[]{:S(2)}) collective-permute-start(bf16[512,256]{1,0:T(8,128)(2,1)S(1)} %collective-permute-done.13.refs_9_), channel_id=1, source_target_pairs={{0,224},{1,225},{2,226},{3,227},{4,228},{5,229},{6,230},{7,231},{8... | collective-permute-start | bytes 786440 | tf_op jit(solution)/shard_map/ppermute | solution.py:27
  133.1 2.4 %collective-permute-done.16.refs_10_ = bf16[512,256]{1,0:T(8,128)(2,1)S(1)} collective-permute-done((bf16[512,256]{1,0:T(8,128)(2,1)S(1)}, bf16[512,256]{1,0:T(8,128)(2,1)S(1)}, u32[]{:S(2)}, u32[]{:S(2)}) %collective-permute-start.16) | collective-permute-done | bytes 262176 | tf_op jit(solution)/shard_map/ppermute | solution.py:27
  135.5 1.5 collective-permute-done.17.refs_11_
  137.8 1.3 collective-permute-start.19
  139.1 1.3 collective-permute-start.18
  140.5 5.6 %collective-permute-start.21 = (bf16[256,256]{1,0:T(8,128)(2,1)S(1)}, bf16[256,256]{1,0:T(8,128)(2,1)S(1)}, u32[]{:S(2)}, u32[]{:S(2)}) collective-permute-start(bf16[256,256]{1,0:T(8,128)(2,1)S(1)} %slice.34), channel_id=1, source_target_pairs={{0,224},{1,225},{2,226},{3,227},{4,228},{5,229},{6,230},{7,231},{8... | collective-permute-start | bytes 393224 | tf_op jit(solution)/shard_map/ppermute | solution.py:27
  146.1 1.9 collective-permute-start.20
  149.6 5.8 %collective-permute-done.20.refs_12_ = bf16[256,256]{1,0:T(8,128)(2,1)S(1)} collective-permute-done((bf16[256,256]{1,0:T(8,128)(2,1)S(1)}, bf16[256,256]{1,0:T(8,128)(2,1)S(1)}, u32[]{:S(2)}, u32[]{:S(2)}) %collective-permute-start.20) | collective-permute-done | bytes 131104 | tf_op jit(solution)/shard_map/ppermute | solution.py:27
  156.9 7.2 %mix.1 = (f32[4,128,512]{2,1,0:T(8,128)}, f32[4,128,512]{2,1,0:T(8,128)}) custom-call(s32[12]{0:T(128)} %stack.55.table_ref, bf16[512,512]{1,0:T(8,128)(2,1)} %copy-done, bf16[512,512]{1,0:T(8,128)(2,1)} %copy-done.3, bf16[512,512]{1,0:T(8,128)(2,1)} %copy-done.2, bf16[256,512]{1,0:T(8,128)(2,1)} %copy-done.12, bf16[256,512]{1,0:T(8,128)(2,1)} %copy-done.11, ...), custom_call_target="tpu_custom_call" | custom-call | flops 1100000000 | bytes 7000000 | tf_op jit(solution)/shard_map/mix/pallas_call | solution.py:208
  164.1 2.2 %collective-permute-start.22 = (f32[4,128,512]{2,1,0:T(8,128)}, f32[4,128,512]{2,1,0:T(8,128)S(1)}, u32[]{:S(2)}, u32[]{:S(2)}) collective-permute-start(f32[4,128,512]{2,1,0:T(8,128)} %get-tuple-element.44), channel_id=1, source_target_pairs={{0,16},{1,17},{2,18},{3,19},{4,20},{5,21},{6,22},{7,23},{8,24},{9,... | collective-permute-start | bytes 3145736 | tf_op jit(solution)/shard_map/ppermute | solution.py:27
  166.2 2.6 %collective-permute-done.22 = f32[4,128,512]{2,1,0:T(8,128)S(1)} collective-permute-done((f32[4,128,512]{2,1,0:T(8,128)}, f32[4,128,512]{2,1,0:T(8,128)S(1)}, u32[]{:S(2)}, u32[]{:S(2)}) %collective-permute-start.22) | collective-permute-done | bytes 1048608 | tf_op jit(solution)/shard_map/ppermute | solution.py:27
  168.8 1.5 fusion.2
  170.4 3.1 %collective-permute-start.23 = (bf16[128,512]{1,0:T(8,128)(2,1)S(1)}, bf16[128,512]{1,0:T(8,128)(2,1)S(1)}, u32[]{:S(2)}, u32[]{:S(2)}) collective-permute-start(bf16[128,512]{1,0:T(8,128)(2,1)S(1)} %get-tuple-element.47), channel_id=1, source_target_pairs={{0,1},{1,2},{2,3},{3,0},{4,5},{5,6},{6,7},{7,4},{8,9},{9,10},{10,1... | collective-permute-start | bytes 393224 | tf_op jit(solution)/shard_map/ppermute | solution.py:27
  173.5 2.7 %collective-permute-start.25 = (bf16[128,512]{1,0:T(8,128)(2,1)S(1)}, bf16[128,512]{1,0:T(8,128)(2,1)S(1)}, u32[]{:S(2)}, u32[]{:S(2)}) collective-permute-start(bf16[128,512]{1,0:T(8,128)(2,1)S(1)} %get-tuple-element.48), channel_id=1, source_target_pairs={{0,3},{1,0},{2,1},{3,2},{4,7},{5,4},{6,5},{7,6},{8,11},{9,8},{10,9... | collective-permute-start | bytes 393224 | tf_op jit(solution)/shard_map/ppermute | solution.py:27
  176.2 2.1 %collective-permute-start.24 = (bf16[128,512]{1,0:T(8,128)(2,1)S(1)}, bf16[128,512]{1,0:T(8,128)(2,1)S(1)}, u32[]{:S(2)}, u32[]{:S(2)}) collective-permute-start(bf16[128,512]{1,0:T(8,128)(2,1)S(1)} %get-tuple-element.49), channel_id=1, source_target_pairs={{0,2},{1,3},{2,0},{3,1},{4,6},{5,7},{6,4},{7,5},{8,10},{9,11},{10,... | collective-permute-start | bytes 393224 | tf_op jit(solution)/shard_map/ppermute | solution.py:27
  178.4 5.2 %collective-permute-done.25 = bf16[128,512]{1,0:T(8,128)(2,1)S(1)} collective-permute-done((bf16[128,512]{1,0:T(8,128)(2,1)S(1)}, bf16[128,512]{1,0:T(8,128)(2,1)S(1)}, u32[]{:S(2)}, u32[]{:S(2)}) %collective-permute-start.25) | collective-permute-done | bytes 131104 | tf_op jit(solution)/shard_map/ppermute | solution.py:27
  183.5 4.6 %collective-permute-done.24 = bf16[128,512]{1,0:T(8,128)(2,1)S(1)} collective-permute-done((bf16[128,512]{1,0:T(8,128)(2,1)S(1)}, bf16[128,512]{1,0:T(8,128)(2,1)S(1)}, u32[]{:S(2)}, u32[]{:S(2)}) %collective-permute-start.24) | collective-permute-done | bytes 131104 | tf_op jit(solution)/shard_map/ppermute | solution.py:27
  188.2 5.8 %collective-permute-start.26 = (bf16[128,512]{1,0:T(8,128)(2,1)S(1)}, bf16[128,512]{1,0:T(8,128)(2,1)S(1)}, u32[]{:S(2)}, u32[]{:S(2)}) collective-permute-start(bf16[128,512]{1,0:T(8,128)(2,1)S(1)} %fusion.1), channel_id=1, source_target_pairs={{0,0},{1,4},{2,256},{3,260},{4,1},{5,5},{6,257},{7,261},{8,2},{9,6... | collective-permute-start | bytes 393224 | tf_op jit(solution)/shard_map/ppermute | solution.py:27
  194.1 9.4 %collective-permute-done.26 = bf16[128,512]{1,0:T(8,128)(2,1)S(1)} collective-permute-done((bf16[128,512]{1,0:T(8,128)(2,1)S(1)}, bf16[128,512]{1,0:T(8,128)(2,1)S(1)}, u32[]{:S(2)}, u32[]{:S(2)}) %collective-permute-start.26) | collective-permute-done | bytes 131104 | tf_op jit(solution)/shard_map/ppermute | solution.py:27
  (60 shorter events, 7.4 us)
Async XLA Ops:
  0.0 22.9 %collective-permute-start.1 = (bf16[512,256]{1,0:T(8,128)(2,1)}, bf16[512,256]{1,0:T(8,128)(2,1)S(1)}, u32[]{:S(2)}, u32[]{:S(2)}) collective-permute-start(bf16[512,256]{1,0:T(8,128)(2,1)} %param.11), channel_id=1, source_target_pairs={{0,0},{1,1},{2,2},{3,3},{4,16},{5,17},{6,18},{7,19},{8,32},{9,33},... | collective-permute-start | bytes 786440 | tf_op jit(solution)/shard_map/ppermute | solution.py:27
  2.3 17.3 %collective-permute-start = (bf16[2,3,512]{2,0,1:T(2,128)(2,1)S(1)}, bf16[2,3,512]{2,0,1:T(2,128)(2,1)S(1)}, u32[]{:S(2)}, u32[]{:S(2)}) collective-permute-start(bf16[2,3,512]{2,0,1:T(2,128)(2,1)S(1)} %slice.30), channel_id=1, source_target_pairs={{0,16},{1,17},{2,18},{3,19},{4,20},{5,21},{6,22},{7,23},{8,24},{9,... | collective-permute-start | bytes 18440 | tf_op jit(solution)/shard_map/ppermute | solution.py:32
  19.6 0.6 copy-start.16
  20.2 25.5 %copy-start.1 = (f32[16,512]{1,0:T(8,128)S(1)}, f32[16,512]{1,0:T(8,128)}, u32[]{:S(2)}) copy-start(f32[16,512]{1,0:T(8,128)} %rate_ref.3) | copy-start | bytes 98308
  22.9 75.1 %copy-start.6 = (bf16[512,256]{1,0:T(8,128)(2,1)}, bf16[512,256]{1,0:T(8,128)(2,1)S(1)}, u32[]{:S(2)}) copy-start(bf16[512,256]{1,0:T(8,128)(2,1)S(1)} %collective-permute-done.1.refs_5_) | copy-start | bytes 786436
  22.9 34.8 %copy-start.15 = (f32[16,512]{1,0:T(8,128)S(1)}, f32[16,512]{1,0:T(8,128)}, u32[]{:S(2)}) copy-start(f32[16,512]{1,0:T(8,128)} %param.9) | copy-start | bytes 98308
  22.9 11.6 %collective-permute-start.2 = (f32[16,512]{1,0:T(8,128)}, f32[16,512]{1,0:T(8,128)S(1)}, u32[]{:S(2)}, u32[]{:S(2)}) collective-permute-start(f32[16,512]{1,0:T(8,128)} %get-tuple-element.29), channel_id=1, source_target_pairs={{0,16},{1,17},{2,18},{3,19},{4,20},{5,21},{6,22},{7,23},{8,24},{9,... | collective-permute-start | bytes 98312 | tf_op jit(solution)/shard_map/ppermute | solution.py:32
  34.5 11.2 %collective-permute-start.3 = (f32[16,512]{1,0:T(8,128)S(1)}, f32[16,512]{1,0:T(8,128)S(1)}, u32[]{:S(2)}, u32[]{:S(2)}) collective-permute-start(f32[16,512]{1,0:T(8,128)S(1)} %collective-permute-done.2), channel_id=1, source_target_pairs={{0,16},{1,17},{2,18},{3,19},{4,20},{5,21},{6,22},{7,23},{8,24},{9,... | collective-permute-start | bytes 98312 | tf_op jit(solution)/shard_map/ppermute | solution.py:32
  45.7 11.9 %collective-permute-start.4 = (f32[16,512]{1,0:T(8,128)S(1)}, f32[16,512]{1,0:T(8,128)S(1)}, u32[]{:S(2)}, u32[]{:S(2)}) collective-permute-start(f32[16,512]{1,0:T(8,128)S(1)} %multiply_add_fusion.4), channel_id=1, source_target_pairs={{0,32},{1,33},{2,34},{3,35},{4,36},{5,37},{6,38},{7,39},{8,40},{9,... | collective-permute-start | bytes 98312 | tf_op jit(solution)/shard_map/ppermute | solution.py:32
  58.3 12.7 %collective-permute-start.5 = (f32[16,512]{1,0:T(8,128)S(1)}, f32[16,512]{1,0:T(8,128)S(1)}, u32[]{:S(2)}, u32[]{:S(2)}) collective-permute-start(f32[16,512]{1,0:T(8,128)S(1)} %get-tuple-element.51), channel_id=1, source_target_pairs={{0,64},{1,65},{2,66},{3,67},{4,68},{5,69},{6,70},{7,71},{8,72},{9,... | collective-permute-start | bytes 98312 | tf_op jit(solution)/shard_map/ppermute | solution.py:32
  71.0 14.7 %collective-permute-start.6 = (f32[16,512]{1,0:T(8,128)S(1)}, f32[16,512]{1,0:T(8,128)S(1)}, u32[]{:S(2)}, u32[]{:S(2)}) collective-permute-start(f32[16,512]{1,0:T(8,128)S(1)} %multiply_add_fusion.2), channel_id=1, source_target_pairs={{0,128},{1,129},{2,130},{3,131},{4,132},{5,133},{6,134},{7,135},{8... | collective-permute-start | bytes 98312 | tf_op jit(solution)/shard_map/ppermute | solution.py:32
  85.7 9.7 %collective-permute-start.7 = (f32[16,512]{1,0:T(8,128)S(1)}, f32[16,512]{1,0:T(8,128)S(1)}, u32[]{:S(2)}, u32[]{:S(2)}) collective-permute-start(f32[16,512]{1,0:T(8,128)S(1)} %multiply_add_fusion.1), channel_id=1, source_target_pairs={{0,256},{1,257},{2,258},{3,259},{4,260},{5,261},{6,262},{7,263},{8... | collective-permute-start | bytes 98312 | tf_op jit(solution)/shard_map/ppermute | solution.py:32
  96.1 12.8 %collective-permute-start.10 = (bf16[512,256]{1,0:T(8,128)(2,1)S(1)}, bf16[512,256]{1,0:T(8,128)(2,1)S(1)}, u32[]{:S(2)}, u32[]{:S(2)}) collective-permute-start(bf16[512,256]{1,0:T(8,128)(2,1)S(1)} %collective-permute-done.1.refs_5_), channel_id=1, source_target_pairs={{0,224},{1,225},{2,226},{3,227},{4,228},{5,229},{6,230},{7,231},{8... | collective-permute-start | bytes 786440 | tf_op jit(solution)/shard_map/ppermute | solution.py:27
  98.0 10.9 %collective-permute-start.9 = (bf16[512,256]{1,0:T(8,128)(2,1)S(1)}, bf16[512,256]{1,0:T(8,128)(2,1)S(1)}, u32[]{:S(2)}, u32[]{:S(2)}) collective-permute-start(bf16[512,256]{1,0:T(8,128)(2,1)S(1)} %collective-permute-done.1.refs_5_), channel_id=1, source_target_pairs={{0,32},{1,33},{2,34},{3,35},{4,36},{5,37},{6,38},{7,39},{8,40},{9,... | collective-permute-start | bytes 786440 | tf_op jit(solution)/shard_map/ppermute | solution.py:27
  104.4 3.4 %collective-permute-start.8 = (bf16[128,512]{1,0:T(8,128)(2,1)}, bf16[128,512]{1,0:T(8,128)(2,1)S(1)}, u32[]{:S(2)}, u32[]{:S(2)}) collective-permute-start(bf16[128,512]{1,0:T(8,128)(2,1)} %back.1), channel_id=1, source_target_pairs={{4,20},{5,21},{6,22},{7,23},{12,28},{13,29},{14,30},{15,31},{16,0}... | collective-permute-start | bytes 393224 | tf_op jit(solution)/shard_map/ppermute | solution.py:27
  108.8 12.9 %copy-start.7 = (bf16[512,256]{1,0:T(8,128)(2,1)}, bf16[512,256]{1,0:T(8,128)(2,1)S(1)}, u32[]{:S(2)}) copy-start(bf16[512,256]{1,0:T(8,128)(2,1)S(1)} %collective-permute-done.10.refs_7_) | copy-start | bytes 786436
  108.8 12.9 %copy-start.8 = (bf16[512,256]{1,0:T(8,128)(2,1)}, bf16[512,256]{1,0:T(8,128)(2,1)S(1)}, u32[]{:S(2)}) copy-start(bf16[512,256]{1,0:T(8,128)(2,1)S(1)} %collective-permute-done.9.refs_6_) | copy-start | bytes 786436
  108.9 12.9 %collective-permute-start.11 = (bf16[256,512]{1,0:T(8,128)(2,1)S(1)}, bf16[256,512]{1,0:T(8,128)(2,1)S(1)}, u32[]{:S(2)}, u32[]{:S(2)}) collective-permute-start(bf16[256,512]{1,0:T(8,128)(2,1)S(1)} %pad_maximum_fusion.1), channel_id=1, source_target_pairs={{0,256},{1,257},{2,258},{3,259},{8,264},{9,265},{10,266},{11,267},... | collective-permute-start | bytes 786440 | tf_op jit(solution)/shard_map/ppermute | solution.py:27
  110.8 11.0 %collective-permute-start.12 = (bf16[512,256]{1,0:T(8,128)(2,1)S(1)}, bf16[512,256]{1,0:T(8,128)(2,1)S(1)}, u32[]{:S(2)}, u32[]{:S(2)}) collective-permute-start(bf16[512,256]{1,0:T(8,128)(2,1)S(1)} %collective-permute-done.9.refs_6_), channel_id=1, source_target_pairs={{0,32},{1,33},{2,34},{3,35},{4,36},{5,37},{6,38},{7,39},{8,40},{9,... | collective-permute-start | bytes 786440 | tf_op jit(solution)/shard_map/ppermute | solution.py:27
  112.7 9.5 %collective-permute-start.13 = (bf16[512,256]{1,0:T(8,128)(2,1)S(1)}, bf16[512,256]{1,0:T(8,128)(2,1)S(1)}, u32[]{:S(2)}, u32[]{:S(2)}) collective-permute-start(bf16[512,256]{1,0:T(8,128)(2,1)S(1)} %collective-permute-done.10.refs_7_), channel_id=1, source_target_pairs={{0,224},{1,225},{2,226},{3,227},{4,228},{5,229},{6,230},{7,231},{8... | collective-permute-start | bytes 786440 | tf_op jit(solution)/shard_map/ppermute | solution.py:27
  121.8 15.3 %copy-start = (bf16[512,512]{1,0:T(8,128)(2,1)}, bf16[512,512]{1,0:T(8,128)(2,1)S(1)}, u32[]{:S(2)}) copy-start(bf16[512,512]{1,0:T(8,128)(2,1)S(1)} %pad_maximum_fusion.refs_0_) | copy-start | bytes 1572868
  121.8 18.7 %copy-start.9 = (bf16[512,256]{1,0:T(8,128)(2,1)}, bf16[512,256]{1,0:T(8,128)(2,1)S(1)}, u32[]{:S(2)}) copy-start(bf16[512,256]{1,0:T(8,128)(2,1)S(1)} %collective-permute-done.12.refs_8_) | copy-start | bytes 786436
  122.2 18.3 %copy-start.10 = (bf16[512,256]{1,0:T(8,128)(2,1)}, bf16[512,256]{1,0:T(8,128)(2,1)S(1)}, u32[]{:S(2)}) copy-start(bf16[512,256]{1,0:T(8,128)(2,1)S(1)} %collective-permute-done.13.refs_9_) | copy-start | bytes 786436
  122.2 14.8 %collective-permute-start.15 = (bf16[512,512]{1,0:T(8,128)(2,1)S(1)}, bf16[512,512]{1,0:T(8,128)(2,1)S(1)}, u32[]{:S(2)}, u32[]{:S(2)}) collective-permute-start(bf16[512,512]{1,0:T(8,128)(2,1)S(1)} %pad_maximum_fusion.refs_0_), channel_id=1, source_target_pairs={{0,12},{1,13},{2,14},{3,15},{8,4},{9,5},{10,6},{11,7},{20,16},{21,... | collective-permute-start | bytes 1572872 | tf_op jit(solution)/shard_map/ppermute | solution.py:27
  123.5 13.5 %collective-permute-start.14 = (bf16[512,512]{1,0:T(8,128)(2,1)S(1)}, bf16[512,512]{1,0:T(8,128)(2,1)S(1)}, u32[]{:S(2)}, u32[]{:S(2)}) collective-permute-start(bf16[512,512]{1,0:T(8,128)(2,1)S(1)} %pad_maximum_fusion.refs_0_), channel_id=1, source_target_pairs={{0,4},{1,5},{2,6},{3,7},{8,12},{9,13},{10,14},{11,15},{20,24},{21,... | collective-permute-start | bytes 1572872 | tf_op jit(solution)/shard_map/ppermute | solution.py:27
  125.6 9.9 %collective-permute-start.16 = (bf16[512,256]{1,0:T(8,128)(2,1)S(1)}, bf16[512,256]{1,0:T(8,128)(2,1)S(1)}, u32[]{:S(2)}, u32[]{:S(2)}) collective-permute-start(bf16[512,256]{1,0:T(8,128)(2,1)S(1)} %collective-permute-done.12.refs_8_), channel_id=1, source_target_pairs={{0,32},{1,33},{2,34},{3,35},{4,36},{5,37},{6,38},{7,39},{8,40},{9,... | collective-permute-start | bytes 786440 | tf_op jit(solution)/shard_map/ppermute | solution.py:27
  127.5 9.5 %collective-permute-start.17 = (bf16[512,256]{1,0:T(8,128)(2,1)S(1)}, bf16[512,256]{1,0:T(8,128)(2,1)S(1)}, u32[]{:S(2)}, u32[]{:S(2)}) collective-permute-start(bf16[512,256]{1,0:T(8,128)(2,1)S(1)} %collective-permute-done.13.refs_9_), channel_id=1, source_target_pairs={{0,224},{1,225},{2,226},{3,227},{4,228},{5,229},{6,230},{7,231},{8... | collective-permute-start | bytes 786440 | tf_op jit(solution)/shard_map/ppermute | solution.py:27
  135.5 4.9 %copy-start.4 = (bf16[512,256]{1,0:T(8,128)(2,1)}, bf16[512,256]{1,0:T(8,128)(2,1)S(1)}, u32[]{:S(2)}) copy-start(bf16[512,256]{1,0:T(8,128)(2,1)S(1)} %collective-permute-done.16.refs_10_) | copy-start | bytes 786436
  137.0 3.5 %copy-start.5 = (bf16[512,256]{1,0:T(8,128)(2,1)}, bf16[512,256]{1,0:T(8,128)(2,1)S(1)}, u32[]{:S(2)}) copy-start(bf16[512,256]{1,0:T(8,128)(2,1)S(1)} %collective-permute-done.17.refs_11_) | copy-start | bytes 786436
  137.0 0.8 copy-start.2
  137.0 18.4 %copy-start.3 = (bf16[512,512]{1,0:T(8,128)(2,1)}, bf16[512,512]{1,0:T(8,128)(2,1)S(1)}, u32[]{:S(2)}) copy-start(bf16[512,512]{1,0:T(8,128)(2,1)S(1)} %collective-permute-done.14.refs_1_) | copy-start | bytes 1572868
  137.8 17.6 %collective-permute-start.19 = (bf16[256,512]{1,0:T(8,128)(2,1)S(1)}, bf16[256,512]{1,0:T(8,128)(2,1)S(1)}, u32[]{:S(2)}, u32[]{:S(2)}) collective-permute-start(bf16[256,512]{1,0:T(8,128)(2,1)S(1)} %slice.32), channel_id=1, source_target_pairs={{4,0},{5,1},{6,2},{7,3},{12,8},{13,9},{14,10},{15,11},{16,28},{17,... | collective-permute-start | bytes 786440 | tf_op jit(solution)/shard_map/ppermute | solution.py:27
  139.1 16.3 %collective-permute-start.18 = (bf16[256,512]{1,0:T(8,128)(2,1)S(1)}, bf16[256,512]{1,0:T(8,128)(2,1)S(1)}, u32[]{:S(2)}, u32[]{:S(2)}) collective-permute-start(bf16[256,512]{1,0:T(8,128)(2,1)S(1)} %slice.31), channel_id=1, source_target_pairs={{4,8},{5,9},{6,10},{7,11},{12,0},{13,1},{14,2},{15,3},{16,20},{17,... | collective-permute-start | bytes 786440 | tf_op jit(solution)/shard_map/ppermute | solution.py:27
  140.5 9.1 %collective-permute-start.21 = (bf16[256,256]{1,0:T(8,128)(2,1)S(1)}, bf16[256,256]{1,0:T(8,128)(2,1)S(1)}, u32[]{:S(2)}, u32[]{:S(2)}) collective-permute-start(bf16[256,256]{1,0:T(8,128)(2,1)S(1)} %slice.34), channel_id=1, source_target_pairs={{0,224},{1,225},{2,226},{3,227},{4,228},{5,229},{6,230},{7,231},{8... | collective-permute-start | bytes 393224 | tf_op jit(solution)/shard_map/ppermute | solution.py:27
  146.1 9.3 %collective-permute-start.20 = (bf16[256,256]{1,0:T(8,128)(2,1)S(1)}, bf16[256,256]{1,0:T(8,128)(2,1)S(1)}, u32[]{:S(2)}, u32[]{:S(2)}) collective-permute-start(bf16[256,256]{1,0:T(8,128)(2,1)S(1)} %slice.33), channel_id=1, source_target_pairs={{0,32},{1,33},{2,34},{3,35},{4,36},{5,37},{6,38},{7,39},{8,40},{9,... | collective-permute-start | bytes 393224 | tf_op jit(solution)/shard_map/ppermute | solution.py:27
  149.6 5.8 %copy-start.13 = (bf16[256,256]{1,0:T(8,128)(2,1)}, bf16[256,256]{1,0:T(8,128)(2,1)S(1)}, u32[]{:S(2)}) copy-start(bf16[256,256]{1,0:T(8,128)(2,1)S(1)} %collective-permute-done.21.refs_13_) | copy-start | bytes 393220
  155.4 0.7 copy-start.14
  155.4 0.7 copy-start.11
  156.1 0.7 copy-start.12
  164.1 4.8 %collective-permute-start.22 = (f32[4,128,512]{2,1,0:T(8,128)}, f32[4,128,512]{2,1,0:T(8,128)S(1)}, u32[]{:S(2)}, u32[]{:S(2)}) collective-permute-start(f32[4,128,512]{2,1,0:T(8,128)} %get-tuple-element.44), channel_id=1, source_target_pairs={{0,16},{1,17},{2,18},{3,19},{4,20},{5,21},{6,22},{7,23},{8,24},{9,... | collective-permute-start | bytes 3145736 | tf_op jit(solution)/shard_map/ppermute | solution.py:27
  170.4 8.0 %collective-permute-start.23 = (bf16[128,512]{1,0:T(8,128)(2,1)S(1)}, bf16[128,512]{1,0:T(8,128)(2,1)S(1)}, u32[]{:S(2)}, u32[]{:S(2)}) collective-permute-start(bf16[128,512]{1,0:T(8,128)(2,1)S(1)} %get-tuple-element.47), channel_id=1, source_target_pairs={{0,1},{1,2},{2,3},{3,0},{4,5},{5,6},{6,7},{7,4},{8,9},{9,10},{10,1... | collective-permute-start | bytes 393224 | tf_op jit(solution)/shard_map/ppermute | solution.py:27
  173.5 10.0 %collective-permute-start.25 = (bf16[128,512]{1,0:T(8,128)(2,1)S(1)}, bf16[128,512]{1,0:T(8,128)(2,1)S(1)}, u32[]{:S(2)}, u32[]{:S(2)}) collective-permute-start(bf16[128,512]{1,0:T(8,128)(2,1)S(1)} %get-tuple-element.48), channel_id=1, source_target_pairs={{0,3},{1,0},{2,1},{3,2},{4,7},{5,4},{6,5},{7,6},{8,11},{9,8},{10,9... | collective-permute-start | bytes 393224 | tf_op jit(solution)/shard_map/ppermute | solution.py:27
  176.2 11.9 %collective-permute-start.24 = (bf16[128,512]{1,0:T(8,128)(2,1)S(1)}, bf16[128,512]{1,0:T(8,128)(2,1)S(1)}, u32[]{:S(2)}, u32[]{:S(2)}) collective-permute-start(bf16[128,512]{1,0:T(8,128)(2,1)S(1)} %get-tuple-element.49), channel_id=1, source_target_pairs={{0,2},{1,3},{2,0},{3,1},{4,6},{5,7},{6,4},{7,5},{8,10},{9,11},{10,... | collective-permute-start | bytes 393224 | tf_op jit(solution)/shard_map/ppermute | solution.py:27
  188.2 15.2 %collective-permute-start.26 = (bf16[128,512]{1,0:T(8,128)(2,1)S(1)}, bf16[128,512]{1,0:T(8,128)(2,1)S(1)}, u32[]{:S(2)}, u32[]{:S(2)}) collective-permute-start(bf16[128,512]{1,0:T(8,128)(2,1)S(1)} %fusion.1), channel_id=1, source_target_pairs={{0,0},{1,4},{2,256},{3,260},{4,1},{5,5},{6,257},{7,261},{8,2},{9,6... | collective-permute-start | bytes 393224 | tf_op jit(solution)/shard_map/ppermute | solution.py:27

commit v3 on v2

v3 whole, which is shorter than its diff:
```python
import functools

import jax
import jax.numpy as jnp
from jax import lax
from jax.experimental import pallas as pl
from jax.experimental.pallas import tpu as pltpu
from jax.sharding import PartitionSpec as P

AXES = ("ctx", "tp")
EVERY = [
    (yh, z, core, x, yl)
    for yh in range(2)
    for z in range(8)
    for core in range(2)
    for x in range(4)
    for yl in range(4)
]


def flat(yh, z, core, x, yl):
    return ((yh * 8 + z) * 2 + core) * 16 + x * 4 + yl


def move(value, axes, target, sends=lambda *place: True):
    pairs = [(flat(*p), flat(*target(*p))) for p in EVERY if sends(*p)]
    return lax.ppermute(value, axes, pairs)


def from_behind(value, axes, by):
    pairs = [(i, i + by * 16) for i in range(512) if i + by * 16 < 512]
    return lax.ppermute(value, axes, pairs)


VMEM = pl.BlockSpec(memory_space=pltpu.VMEM)
SMEM = pl.BlockSpec(memory_space=pltpu.SMEM)


def spread(ref, value):
    rows = value.shape[0]
    for half in range(2):
        for part in range(4):
            ref[pl.ds(half * 4 + part, rows, stride=8), :] = value[:, part * 128 : part * 128 + 128]


def first_kernel(feat_ref, taps_ref, rate_ref, out_ref, ext, drive_ref, lam):
    both = []
    sides = []
    for f in (1, 2):
        taps = [taps_ref[j, f : f + 1, :] for j in range(3)]
        ext[8:136, :] = feat_ref[f].astype(jnp.float32)
        ext[0:8, :] = jnp.zeros((8, 512), jnp.float32)
        total = taps[0] * ext[8:136, :] + taps[1] * ext[7:135, :] + taps[2] * ext[6:134, :]
        both.append(total)
        last = ext[135:136, :]
        sides.append((total[0:1], total[1:2], taps[1] * last + taps[2] * ext[134:135, :], taps[2] * last))
    drive = both[0] * both[1]
    side = jnp.concatenate([sides[0][0], sides[1][0], sides[0][1], sides[1][1], sides[0][2], sides[1][2], sides[0][3], sides[1][3]], axis=0)
    pack_positions(drive_ref, drive)
    spread(lam, jnp.exp(-rate_ref[...]))
    lams = [lam[m * 8 : m * 8 + 8, :] for m in range(16)]

    def step(t, states):
        now = drive_ref[pl.ds(pl.multiple_of(t * 8, 8), 8), :]
        return tuple(a * s + now for a, s in zip(lams, states))

    states = lax.fori_loop(0, 64, step, tuple(jnp.zeros((8, 128), jnp.float32) for _ in range(16)), unroll=4)
    spread(lam, jnp.exp(-64.0 * rate_ref[...]))
    for part in range(4):
        for pair in range(8):
            out_ref[pair * 4 + part, 8:16, :] = side[:, part * 128 : part * 128 + 128]
    for m in range(16):
        end = states[m] + pltpu.roll(lam[m * 8 : m * 8 + 8, :] * states[m], 4, 0)
        for part in range(4):
            out_ref[m // 2 * 4 + part, m % 2 : m % 2 + 1, :] = end[4 + part : 5 + part]


def carry_kernel(ends_ref, rate_ref, out_ref):
    rate = rate_ref[...]
    whole, late, later = jnp.exp(-128.0 * rate), jnp.exp(-127.0 * rate), jnp.exp(-126.0 * rate)
    state = jnp.zeros((2, 128), jnp.float32)
    for k in range(32):
        out_ref[k] = state
        end = ends_ref[k, 0:2, :]
        if k > 0:
            here, before = ends_ref[k, 8:12, :], ends_ref[k - 1, 12:16, :]
            full = here + before
            end = end + late * (full[0:1] * full[1:2] - here[0:1] * here[1:2])
            end = end + later * (full[2:3] * full[3:4] - here[2:3] * here[3:4])
        state = whole * state + end


def pack_positions(ref, drive):
    for half in range(2):
        for part in range(4):
            ref[pl.ds(half * 4 + part, 64, stride=8), :] = drive[
                half * 64 : half * 64 + 64, part * 128 : part * 128 + 128
            ]


def middle_kernel(feat_ref, halo_ref, taps_ref, rate_ref, query_ref, drive_ref, half_ref, ext, lam):
    filtered = []
    for f in range(3):
        ext[8:136, :] = feat_ref[f].astype(jnp.float32)
        ext[6:8, :] = halo_ref[f].astype(jnp.float32)
        total = taps_ref[0, f : f + 1, :] * ext[8:136, :]
        total = total + taps_ref[1, f : f + 1, :] * ext[7:135, :]
        filtered.append(total + taps_ref[2, f : f + 1, :] * ext[6:134, :])
    query_ref[...] = filtered[0]
    pack_positions(drive_ref, filtered[1] * filtered[2])
    spread(lam, jnp.exp(-rate_ref[...]))
    lams = [lam[m * 8 : m * 8 + 8, :] for m in range(16)]

    def step(t, states):
        now = drive_ref[pl.ds(pl.multiple_of(t * 8, 8), 8), :]
        return tuple(a * s + now for a, s in zip(lams, states))

    states = lax.fori_loop(0, 64, step, tuple(jnp.zeros((8, 128), jnp.float32) for _ in range(16)), unroll=4)
    for m in range(16):
        half_ref[m * 8 : m * 8 + 8, :] = states[m]


def back_kernel(query_ref, drive_ref, half_ref, in_ref, rate_ref, gain_ref, skip_ref, out_ref, lam, gain, skip, resp):
    spread(gain, gain_ref[...])
    spread(lam, jnp.exp(-64.0 * rate_ref[...]))
    states = []
    for m in range(16):
        rows = slice(m * 8, m * 8 + 8)
        came = in_ref[pl.ds(m // 2 * 8 + m % 2, 4, stride=2), :]
        later = lam[m * 8 : m * 8 + 4, :] * came + half_ref[m * 8 : m * 8 + 4, :]
        states.append(jnp.concatenate([came, later], axis=0))
    spread(lam, jnp.exp(-rate_ref[...]))
    spread(skip, skip_ref[...])
    lams = [lam[m * 8 : m * 8 + 8, :] for m in range(16)]
    gains = [gain[m * 8 : m * 8 + 8, :] for m in range(16)]
    direct = skip[...]

    def step(t, states):
        rows = pl.ds(pl.multiple_of(t * 8, 8), 8)
        now = drive_ref[rows, :]
        states = tuple(a * s + now for a, s in zip(lams, states))
        sums = [direct * now, None, None, None]
        for m in range(16):
            term = gains[m] * states[m]
            sums[m % 4] = term if sums[m % 4] is None else sums[m % 4] + term
        resp[rows, :] = (sums[0] + sums[1]) + (sums[2] + sums[3])
        return states

    lax.fori_loop(0, 64, step, tuple(states), unroll=2)
    for half in range(2):
        for part in range(4):
            rows, cols = slice(half * 64, half * 64 + 64), slice(part * 128, part * 128 + 128)
            out_ref[rows, cols] = (query_ref[rows, cols] * resp[pl.ds(half * 4 + part, 64, stride=8), :]).astype(jnp.bfloat16)


def mix_kernel(table_ref, *refs):
    line, fwd, bwd, hf, hb, weights = refs[:6]
    keep_ref, send_ref, g, w, acc, g_sem, w_sem = refs[6:]
    own = table_ref[0] == 1
    yl = table_ref[1]
    low, high = table_ref[2], table_ref[3]

    def from_own():
        return [
            pltpu.make_async_copy(line, g.at[low], g_sem.at[0]),
            pltpu.make_async_copy(hf, g.at[high, pl.ds(0, 256)], g_sem.at[1]),
            pltpu.make_async_copy(hb, g.at[high, pl.ds(256, 256)], g_sem.at[2]),
        ]

    def from_others():
        return [
            pltpu.make_async_copy(fwd, g.at[low], g_sem.at[0]),
            pltpu.make_async_copy(bwd, g.at[high], g_sem.at[1]),
        ]

    @pl.when(own)
    def _():
        for copy in from_own():
            copy.start()

    @pl.when(jnp.logical_not(own))
    def _():
        for copy in from_others():
            copy.start()

    loads = [pltpu.make_async_copy(weights.at[i], w.at[i], w_sem.at[i]) for i in range(8)]
    for copy in loads:
        copy.start()

    @pl.when(own)
    def _():
        for copy in from_own():
            copy.wait()

    @pl.when(jnp.logical_not(own))
    def _():
        for copy in from_others():
            copy.wait()

    for i in range(8):
        loads[i].wait()
        part = jnp.dot(g[i % 2], w[i], preferred_element_type=jnp.float32).reshape(4, 128, 256)
        acc[i // 2] = part if i % 2 == 0 else acc[i // 2] + part
    for d in range(4):
        block = lax.rem(yl + d, 4)
        for half in range(2):
            cols = slice(half * 256, half * 256 + 256)
            keep_ref[d, :, cols] = acc[lax.rem(block, 2) * 2 + half, block // 2 * 2]
            send_ref[d, :, cols] = acc[lax.rem(block, 2) * 2 + half, block // 2 * 2 + 1]


TINY = pl.CostEstimate(flops=1, bytes_accessed=1, transcendentals=0)
F32 = jnp.float32


def first(feat, taps, rate):
    return pl.pallas_call(
        first_kernel,
        out_shape=jax.ShapeDtypeStruct((32, 16, 128), F32),
        in_specs=[VMEM] * 3,
        out_specs=VMEM,
        scratch_shapes=[pltpu.VMEM((136, 512), F32), pltpu.VMEM((512, 128), F32), pltpu.VMEM((128, 128), F32)],
        cost_estimate=TINY,
        name="first",
    )(feat, taps, rate)


def carry(ends, rate):
    return pl.pallas_call(
        carry_kernel,
        out_shape=jax.ShapeDtypeStruct((32, 2, 128), F32),
        in_specs=[VMEM] * 2,
        out_specs=VMEM,
        cost_estimate=TINY,
        name="carry",
    )(ends, rate)


def middle(feat, halo, taps, rate):
    return pl.pallas_call(
        middle_kernel,
        out_shape=(
            jax.ShapeDtypeStruct((128, 512), F32),
            jax.ShapeDtypeStruct((512, 128), F32),
            jax.ShapeDtypeStruct((128, 128), F32),
        ),
        in_specs=[VMEM] * 4,
        out_specs=(VMEM,) * 3,
        scratch_shapes=[pltpu.VMEM((136, 512), F32), pltpu.VMEM((128, 128), F32)],
        cost_estimate=TINY,
        name="middle",
    )(feat, halo, taps, rate)


def back(query, drive, half, incoming, rate, gain, skip):
    return pl.pallas_call(
        back_kernel,
        out_shape=jax.ShapeDtypeStruct((128, 512), jnp.bfloat16),
        in_specs=[VMEM] * 7,
        out_specs=VMEM,
        scratch_shapes=[pltpu.VMEM((128, 128), F32)] * 2 + [pltpu.VMEM((8, 128), F32), pltpu.VMEM((512, 128), F32)],
        cost_estimate=TINY,
        name="back",
    )(query, drive, half, incoming, rate, gain, skip)


def mix(table, *operands):
    out = jax.ShapeDtypeStruct((4, 128, 512), jnp.float32)
    return pl.pallas_call(
        mix_kernel,
        out_shape=(out, out),
        in_specs=[SMEM] + [pl.BlockSpec(memory_space=pl.ANY)] * len(operands),
        out_specs=(VMEM, VMEM),
        scratch_shapes=[
            pltpu.VMEM((2, 512, 512), jnp.bfloat16),
            pltpu.VMEM((8, 512, 256), jnp.bfloat16),
            pltpu.VMEM((4, 4, 128, 256), jnp.float32),
            pltpu.SemaphoreType.DMA((3,)),
            pltpu.SemaphoreType.DMA((8,)),
        ],
        compiler_params=pltpu.CompilerParams(vmem_limit_bytes=60 * 1024 * 1024),
        cost_estimate=pl.CostEstimate(flops=1_100_000_000, bytes_accessed=7_000_000, transcendentals=0),
        name="mix",
    )(table, *operands)


def body(features, short_filter, decay_rate, residue, skip, out_weight, axes, first, carry, middle, back, mix):
    positions = features.shape[0]
    index = lax.axis_index(axes)
    yl, x, core = index % 4, index // 4 % 4, index // 16 % 2

    halo = from_behind(features[positions - 2 :], axes, 1)

    tie = lax.optimization_barrier
    def place(yh, z, core, x, yl):
        return yh, z // 4 * 4 + core * 2 + x // 2, x % 2, z % 4, yl

    def along(axis, by):
        def target(yh, z, core, x, yl):
            if axis == "z":
                return yh, (z + by) % 8, core, x, yl
            if axis == "x":
                return yh, z, core, (x + by) % 4, yl
            return yh, z, core, x, (yl + by) % 4

        return target

    def mine(yh, z, core, x, yl):
        return x % 2 == core

    def others(yh, z, core, x, yl):
        return x % 2 != core

    def other_core(value, sends=lambda *place: True):
        return move(value, axes, lambda yh, z, core, x, yl: (yh, z, 1 - core, x, yl), sends)

    weight = move(out_weight, axes, place)
    along_z = [[(yh * 8 + z) * 2 + core for z in range(8)] for yh in range(2) for core in range(2)]

    feat = features.transpose(1, 0, 2)
    ends = first(feat, short_filter, decay_rate)
    ends, weight = tie((ends, weight))
    weights = lax.all_gather(weight, "ctx", axis_index_groups=along_z)
    ends = lax.all_to_all(ends, "ctx", 0, 0, tiled=True)
    ctx = index // 16
    rate = lax.dynamic_slice(decay_rate, (ctx // 4 * 2, ctx % 4 * 128), (2, 128))
    incoming = lax.all_to_all(carry(ends, rate), "ctx", 0, 0, tiled=True).reshape(64, 128)

    query, drive, half = middle(feat, halo.transpose(1, 0, 2), short_filter, decay_rate)
    gain = residue * jnp.sqrt(-jnp.expm1(-2.0 * decay_rate))
    gated = back(query, drive, half, incoming, decay_rate, gain, skip[None])

    both = jnp.concatenate([gated, other_core(gated, others)], axis=0)
    beyond = move(both, axes, lambda yh, z, core, x, yl: (1 - yh, z, core, x, yl), mine)
    line = jnp.concatenate([both, beyond], axis=0)
    fwd = move(line, axes, along("x", 1), mine)
    bwd = move(line, axes, along("x", -1), mine)
    half_rows = line.shape[0] // 2
    hf = move(fwd[:half_rows], axes, along("x", 1), others)
    hb = move(bwd[half_rows:], axes, along("x", -1), others)

    own = x % 2 == core
    low = jnp.where(own, x // 2, (x + 3) % 4 // 2)
    high = jnp.where(own, 1 - x // 2, (x + 1) % 4 // 2)
    table = jnp.stack([own.astype(jnp.int32), yl, low, high]).astype(jnp.int32)
    keep, send = mix(table, line, fwd, bwd, hf, hb, weights)

    blocks = keep + other_core(send)
    parts = [move(blocks[d].astype(jnp.bfloat16), axes, along("yl", d)) for d in range(1, 4)]
    total = blocks[0] + sum(part.astype(jnp.float32) for part in parts)
    return move(
        total.astype(jnp.bfloat16), axes, lambda yh, z, core, x, yl: (yh ^ (yl // 2), z, core, yh * 2 + yl % 2, x)
    )


def shards(*arguments):
    return body(*arguments, AXES, first, carry, middle, back, mix)


def solution(mesh):
    in_specs = (
        P("ctx", None, "tp"),
        P(None, None, "tp"),
        P(None, "tp"),
        P(None, "tp"),
        P("tp"),
        P("tp", "ctx"),
    )
    return jax.shard_map(shards, mesh=mesh, in_specs=in_specs, out_specs=P("ctx", "tp"), check_vma=False)
```

time: 205 us -> 166 us (0.81)
  waiting for transfers between devices: 110 us -> 51.1 us
  between operations: 0.82 us -> 13.8 us
  Pallas kernels: 12.4 us -> 15.9 us
    ppermute x7 -> x1, waiting for transfers between devices: 71.5 us -> 0.01 us  [from_behind(): return lax.ppermute(value, axes, pairs)]
    all_to_all x0 -> x2, starting transfers between devices: none -> 35.4 us  [the longest x1 26.5 us: body(): ends = lax.all_to_all(ends, 'ctx', 0, 0, tiled=True)]
    ppermute x20 -> x12, starting transfers between devices: 54.6 us -> 34.8 us  [move(): return lax.ppermute(value, axes, pairs)]
    ppermute x7 -> x1, starting transfers between devices: 17.5 us -> 2.06 us  [from_behind(): return lax.ppermute(value, axes, pairs)]
    all_to_all x0 -> x2, waiting for transfers between devices: none -> 10.4 us  [the longest x1 7.85 us: body(): ends = lax.all_to_all(ends, 'ctx', 0, 0, tiled=True)]
    pallas_call x1 -> x3, Pallas kernels: 2.63 us -> 6.71 us  [the longest x1 2.61 us: middle(): pl.pallas_call(middle_kernel, out_shape=(jax.ShapeDtypeStruct((128, 512),...]
    ppermute x20 -> x12, waiting for transfers between devices: 38.4 us -> 40.6 us  [move(): return lax.ppermute(value, axes, pairs)]
  transfers between devices with their start and end apart: 27 -> 16, of which waited for: 18 -> 11; matrix products, arithmetic and copies ran while one was open for 1% -> 4% of each run, Pallas kernels for 3% -> 6%
where the time goes in v3:
time: 166 us; the launch traced here: 165 us
  starting transfers between devices  72.3 us (44%)
  waiting for transfers between devices  51.1 us (31%)
  Pallas kernels  15.9 us (10%)
  between operations  13.8 us (8%)
  local copies, waits for them, and re-layouts  6.12 us (4%)
  other arithmetic  5.42 us (3%)
    ppermute x12, waiting for transfers between devices, move(): return lax.ppermute(value, axes, pairs)  40.6 us
    ppermute x12, starting transfers between devices, move(): return lax.ppermute(value, axes, pairs)  34.8 us
    all_to_all x1, starting transfers between devices, body(): ends = lax.all_to_all(ends, 'ctx', 0, 0, tiled=True)  26.5 us
    all_to_all x1, starting transfers between devices, body(): lax.all_to_all(carry(ends, rate), 'ctx', 0, 0, tiled=True).reshape(64, 128)  8.85 us
    all_to_all x1, waiting for transfers between devices, body(): ends = lax.all_to_all(ends, 'ctx', 0, 0, tiled=True)  7.85 us
    pallas_call x1, Pallas kernels, mix(): pl.pallas_call(mix_kernel, out_shape=(out, out), in_specs=[SMEM] + [pl.Bl...  6.64 us
    unnamed x19, local copies, waits for them, and re-layouts  4 us
  transfers between devices with their start and end apart: 16, of which 11 were waited for; matrix products, arithmetic and copies ran while one was open for 4% of the time, Pallas kernels for 6%

profile of v3, /device:TPU:56, one launch (start us, length us, event | category | flops | bytes accessed | tf_op | source)
XLA Modules:
  0.0 164.6 jit_solution(4545894541539541273)
XLA Ops:
  6.5 1.6 collective-permute-start.1
  8.1 2.5 %first.1 = f32[32,16,128]{2,1,0:T(8,128)} custom-call(bf16[3,128,512]{2,1,0:T(8,128)(2,1)} %bitcast.22, f32[3,3,512]{2,1,0:T(4,128)} %taps_ref.3, f32[16,512]{1,0:T(8,128)} %rate_ref.5), custom_call_target="tpu_custom_call" | custom-call | flops 1 | bytes 1 | tf_op jit(solution)/shard_map/first/pallas_call | solution.py:217
  10.6 0.0 collective-permute-done.1
  10.6 0.7 copy-done.6
  11.3 0.0 all-gather.3.cloned.1.call-update
  11.3 26.5 %all-to-all-start = ((f32[32,16,128]{2,1,0:T(8,128)}), f32[32,16,128]{2,1,0:T(8,128)S(1)}, u32[]{:S(2)}, u32[]{:S(2)}) async-start(f32[32,16,128]{2,1,0:T(8,128)} %first.1), calls=%async_computation | async-start | bytes 524288 | tf_op jit(solution)/shard_map/all_to_all | solution.py:324
  37.9 0.8 slice.24
  38.6 2.1 %collective-permute-start = (bf16[2,3,512]{2,0,1:T(2,128)(2,1)S(1)}, bf16[2,3,512]{2,0,1:T(2,128)(2,1)S(1)}, u32[]{:S(2)}, u32[]{:S(2)}) collective-permute-start(bf16[2,3,512]{2,0,1:T(2,128)(2,1)S(1)} %slice.24), channel_id=1, source_target_pairs={{0,16},{1,17},{2,18},{3,19},{4,20},{5,21},{6,22},{7,23},{8,24},{9,... | collective-permute-start | bytes 18440 | tf_op jit(solution)/shard_map/ppermute | solution.py:32
  40.7 1.3 dynamic_slice.3.rate_ref
  42.0 7.8 %all-to-all-done.ends_ref = f32[32,16,128]{2,1,0:T(8,128)S(1)} async-done(((f32[32,16,128]{2,1,0:T(8,128)}), f32[32,16,128]{2,1,0:T(8,128)S(1)}, u32[]{:S(2)}, u32[]{:S(2)}) %all-to-all-start) | async-done | bytes 262176 | tf_op jit(solution)/shard_map/all_to_all | solution.py:324
  49.9 0.7 copy-done.3
  50.6 1.6 carry.1
  52.3 8.8 %all-to-all-start.1 = ((f32[32,2,128]{2,1,0:T(2,128)}), f32[32,2,128]{2,1,0:T(2,128)S(1)}, u32[]{:S(2)}, u32[]{:S(2)}) async-start(f32[32,2,128]{2,1,0:T(2,128)} %carry.1), calls=%async_computation.1 | async-start | bytes 65536 | tf_op jit(solution)/shard_map/all_to_all | solution.py:327
  61.1 1.4 sqrt_multiply_fusion.gain_ref
  62.5 0.6 copy-done.8
  63.1 2.6 %middle.1 = (f32[128,512]{1,0:T(8,128)}, f32[512,128]{1,0:T(8,128)}, f32[128,128]{1,0:T(8,128)}) custom-call(bf16[3,128,512]{2,1,0:T(8,128)(2,1)} %bitcast.23, bf16[3,2,512]{2,1,0:T(2,128)(2,1)} %bitcast.25, f32[3,3,512]{2,1,0:T(4,128)} %taps_ref.3, f32[16,512]{1,0:T(8,128)} %rate_ref.5), custom_call_target="tpu_custom_call" | custom-call | flops 1 | bytes 1 | tf_op jit(solution)/shard_map/middle/pallas_call | solution.py:240
  65.7 2.6 %all-to-all-done.1 = f32[32,2,128]{2,1,0:T(2,128)S(1)} async-done(((f32[32,2,128]{2,1,0:T(2,128)}), f32[32,2,128]{2,1,0:T(2,128)S(1)}, u32[]{:S(2)}, u32[]{:S(2)}) %all-to-all-start.1) | async-done | bytes 32800 | tf_op jit(solution)/shard_map/all_to_all | solution.py:327
  68.3 0.6 copy-done.7
  68.9 2.5 %back.1 = bf16[128,512]{1,0:T(8,128)(2,1)} custom-call(f32[128,512]{1,0:T(8,128)} %get-tuple-element.12.query_ref, f32[512,128]{1,0:T(8,128)} %get-tuple-element.13.drive_ref, f32[128,128]{1,0:T(8,128)} %get-tuple-element.14.half_ref, f32[64,128]{1,0:T(8,128)} %bitcast.24, f32[16,512]{1,0:T(8,128)} %rate_ref.5, f32[16,512]{1,0:T(8,128)} %sqrt_multiply_fusion.gain_ref, ...), custom_call_target="tpu_custom_call" | custom-call | flops 1 | bytes 1 | tf_op jit(solution)/shard_map/back/pallas_call | solution.py:256
  71.5 1.3 collective-permute-start.2
  72.7 2.2 %collective-permute-done.2 = bf16[128,512]{1,0:T(8,128)(2,1)S(1)} collective-permute-done((bf16[128,512]{1,0:T(8,128)(2,1)}, bf16[128,512]{1,0:T(8,128)(2,1)S(1)}, u32[]{:S(2)}, u32[]{:S(2)}) %collective-permute-start.2) | collective-permute-done | bytes 131104 | tf_op jit(solution)/shard_map/ppermute | solution.py:27
  74.9 0.9 pad_maximum_fusion.1
  75.8 7.4 %collective-permute-start.3 = (bf16[256,512]{1,0:T(8,128)(2,1)S(1)}, bf16[256,512]{1,0:T(8,128)(2,1)S(1)}, u32[]{:S(2)}, u32[]{:S(2)}) collective-permute-start(bf16[256,512]{1,0:T(8,128)(2,1)S(1)} %pad_maximum_fusion.1), channel_id=1, source_target_pairs={{0,256},{1,257},{2,258},{3,259},{8,264},{9,265},{10,266},{11,267},... | collective-permute-start | bytes 786440 | tf_op jit(solution)/shard_map/ppermute | solution.py:27
  83.2 4.8 %collective-permute-done.3 = bf16[256,512]{1,0:T(8,128)(2,1)S(1)} collective-permute-done((bf16[256,512]{1,0:T(8,128)(2,1)S(1)}, bf16[256,512]{1,0:T(8,128)(2,1)S(1)}, u32[]{:S(2)}, u32[]{:S(2)}) %collective-permute-start.3) | collective-permute-done | bytes 262176 | tf_op jit(solution)/shard_map/ppermute | solution.py:27
  88.1 0.9 pad_maximum_fusion.refs_0_
  89.0 1.3 collective-permute-start.5
  90.4 1.3 collective-permute-start.4
  91.7 5.3 %collective-permute-done.5.refs_2_ = bf16[512,512]{1,0:T(8,128)(2,1)S(1)} collective-permute-done((bf16[512,512]{1,0:T(8,128)(2,1)S(1)}, bf16[512,512]{1,0:T(8,128)(2,1)S(1)}, u32[]{:S(2)}, u32[]{:S(2)}) %collective-permute-start.5) | collective-permute-done | bytes 524320 | tf_op jit(solution)/shard_map/ppermute | solution.py:27
  97.0 1.3 collective-permute-start.7
  98.3 0.0 collective-permute-done.4.refs_1_
  98.4 1.3 collective-permute-start.6
  99.8 0.6 pad_add_fusion.table_ref
  100.4 5.0 %collective-permute-done.7.refs_4_ = bf16[256,512]{1,0:T(8,128)(2,1)S(1)} collective-permute-done((bf16[256,512]{1,0:T(8,128)(2,1)S(1)}, bf16[256,512]{1,0:T(8,128)(2,1)S(1)}, u32[]{:S(2)}, u32[]{:S(2)}) %collective-permute-start.7) | collective-permute-done | bytes 262176 | tf_op jit(solution)/shard_map/ppermute | solution.py:27
  105.4 2.5 %collective-permute-done.6.refs_3_ = bf16[256,512]{1,0:T(8,128)(2,1)S(1)} collective-permute-done((bf16[256,512]{1,0:T(8,128)(2,1)S(1)}, bf16[256,512]{1,0:T(8,128)(2,1)S(1)}, u32[]{:S(2)}, u32[]{:S(2)}) %collective-permute-start.6) | collective-permute-done | bytes 262176 | tf_op jit(solution)/shard_map/ppermute | solution.py:27
  107.9 0.7 copy-done.5
  108.6 6.6 %mix.1 = (f32[4,128,512]{2,1,0:T(8,128)}, f32[4,128,512]{2,1,0:T(8,128)}) custom-call(s32[4]{0:T(128)} %pad_add_fusion.table_ref, bf16[512,512]{1,0:T(8,128)(2,1)} %copy-done, bf16[512,512]{1,0:T(8,128)(2,1)} %copy-done.2, bf16[512,512]{1,0:T(8,128)(2,1)} %copy-done.1, bf16[256,512]{1,0:T(8,128)(2,1)} %copy-done.5, bf16[256,512]{1,0:T(8,128)(2,1)} %copy-done.4, ...), custom_call_target="tpu_custom_call" | custom-call | flops 1100000000 | bytes 7000000 | tf_op jit(solution)/shard_map/mix/pallas_call | solution.py:269
  115.2 1.9 %collective-permute-start.8 = (f32[4,128,512]{2,1,0:T(8,128)}, f32[4,128,512]{2,1,0:T(8,128)S(1)}, u32[]{:S(2)}, u32[]{:S(2)}) collective-permute-start(f32[4,128,512]{2,1,0:T(8,128)} %get-tuple-element.18), channel_id=1, source_target_pairs={{0,16},{1,17},{2,18},{3,19},{4,20},{5,21},{6,22},{7,23},{8,24},{9,... | collective-permute-start | bytes 3145736 | tf_op jit(solution)/shard_map/ppermute | solution.py:27
  117.2 2.8 %collective-permute-done.8 = f32[4,128,512]{2,1,0:T(8,128)S(1)} collective-permute-done((f32[4,128,512]{2,1,0:T(8,128)}, f32[4,128,512]{2,1,0:T(8,128)S(1)}, u32[]{:S(2)}, u32[]{:S(2)}) %collective-permute-start.8) | collective-permute-done | bytes 1048608 | tf_op jit(solution)/shard_map/ppermute | solution.py:27
  120.0 1.5 fusion.2
  121.5 4.8 %collective-permute-start.9 = (bf16[128,512]{1,0:T(8,128)(2,1)S(1)}, bf16[128,512]{1,0:T(8,128)(2,1)S(1)}, u32[]{:S(2)}, u32[]{:S(2)}) collective-permute-start(bf16[128,512]{1,0:T(8,128)(2,1)S(1)} %get-tuple-element.21), channel_id=1, source_target_pairs={{0,1},{1,2},{2,3},{3,0},{4,5},{5,6},{6,7},{7,4},{8,9},{9,10},{10,1... | collective-permute-start | bytes 393224 | tf_op jit(solution)/shard_map/ppermute | solution.py:27
  126.3 3.4 %collective-permute-start.11 = (bf16[128,512]{1,0:T(8,128)(2,1)S(1)}, bf16[128,512]{1,0:T(8,128)(2,1)S(1)}, u32[]{:S(2)}, u32[]{:S(2)}) collective-permute-start(bf16[128,512]{1,0:T(8,128)(2,1)S(1)} %get-tuple-element.22), channel_id=1, source_target_pairs={{0,3},{1,0},{2,1},{3,2},{4,7},{5,4},{6,5},{7,6},{8,11},{9,8},{10,9... | collective-permute-start | bytes 393224 | tf_op jit(solution)/shard_map/ppermute | solution.py:27
  129.7 4.7 %collective-permute-start.10 = (bf16[128,512]{1,0:T(8,128)(2,1)S(1)}, bf16[128,512]{1,0:T(8,128)(2,1)S(1)}, u32[]{:S(2)}, u32[]{:S(2)}) collective-permute-start(bf16[128,512]{1,0:T(8,128)(2,1)S(1)} %get-tuple-element.23), channel_id=1, source_target_pairs={{0,2},{1,3},{2,0},{3,1},{4,6},{5,7},{6,4},{7,5},{8,10},{9,11},{10,... | collective-permute-start | bytes 393224 | tf_op jit(solution)/shard_map/ppermute | solution.py:27
  134.5 2.2 %collective-permute-done.11 = bf16[128,512]{1,0:T(8,128)(2,1)S(1)} collective-permute-done((bf16[128,512]{1,0:T(8,128)(2,1)S(1)}, bf16[128,512]{1,0:T(8,128)(2,1)S(1)}, u32[]{:S(2)}, u32[]{:S(2)}) %collective-permute-start.11) | collective-permute-done | bytes 131104 | tf_op jit(solution)/shard_map/ppermute | solution.py:27
  136.6 5.4 %collective-permute-done.10 = bf16[128,512]{1,0:T(8,128)(2,1)S(1)} collective-permute-done((bf16[128,512]{1,0:T(8,128)(2,1)S(1)}, bf16[128,512]{1,0:T(8,128)(2,1)S(1)}, u32[]{:S(2)}, u32[]{:S(2)}) %collective-permute-start.10) | collective-permute-done | bytes 131104 | tf_op jit(solution)/shard_map/ppermute | solution.py:27
  142.0 0.1 fusion.1
  142.1 4.5 %collective-permute-start.12 = (bf16[128,512]{1,0:T(8,128)(2,1)S(1)}, bf16[128,512]{1,0:T(8,128)(2,1)S(1)}, u32[]{:S(2)}, u32[]{:S(2)}) collective-permute-start(bf16[128,512]{1,0:T(8,128)(2,1)S(1)} %fusion.1), channel_id=1, source_target_pairs={{0,0},{1,4},{2,256},{3,260},{4,1},{5,5},{6,257},{7,261},{8,2},{9,6... | collective-permute-start | bytes 393224 | tf_op jit(solution)/shard_map/ppermute | solution.py:27
  146.5 10.5 %collective-permute-done.12 = bf16[128,512]{1,0:T(8,128)(2,1)S(1)} collective-permute-done((bf16[128,512]{1,0:T(8,128)(2,1)S(1)}, bf16[128,512]{1,0:T(8,128)(2,1)S(1)}, u32[]{:S(2)}, u32[]{:S(2)}) %collective-permute-start.12) | collective-permute-done | bytes 131104 | tf_op jit(solution)/shard_map/ppermute | solution.py:27
  157.1 0.7 copy.8
  (20 shorter events, 0.1 us)
Async XLA Ops:
  6.5 101.3 %all-gather.3.cloned.1.call-start = ((), (), s32[]{:S(2)}) async-start(), calls=%async_computation.2 | async-start | bytes 2359296 | tf_op jit(solution)/shard_map/all_gather | solution.py:323
  6.5 4.1 %collective-permute-start.1 = (bf16[512,256]{1,0:T(8,128)(2,1)}, bf16[512,256]{1,0:T(8,128)(2,1)S(1)}, u32[]{:S(2)}, u32[]{:S(2)}) collective-permute-start(bf16[512,256]{1,0:T(8,128)(2,1)} %param.11), channel_id=1, source_target_pairs={{0,0},{1,1},{2,2},{3,3},{4,16},{5,17},{6,18},{7,19},{8,32},{9,33},... | collective-permute-start | bytes 786440 | tf_op jit(solution)/shard_map/ppermute | solution.py:27
  10.6 0.7 copy-start.6
  11.3 38.6 %all-to-all-start = ((f32[32,16,128]{2,1,0:T(8,128)}), f32[32,16,128]{2,1,0:T(8,128)S(1)}, u32[]{:S(2)}, u32[]{:S(2)}) async-start(f32[32,16,128]{2,1,0:T(8,128)} %first.1), calls=%async_computation | async-start | bytes 524288 | tf_op jit(solution)/shard_map/all_to_all | solution.py:324
  38.6 23.9 %collective-permute-start = (bf16[2,3,512]{2,0,1:T(2,128)(2,1)S(1)}, bf16[2,3,512]{2,0,1:T(2,128)(2,1)S(1)}, u32[]{:S(2)}, u32[]{:S(2)}) collective-permute-start(bf16[2,3,512]{2,0,1:T(2,128)(2,1)S(1)} %slice.24), channel_id=1, source_target_pairs={{0,16},{1,17},{2,18},{3,19},{4,20},{5,21},{6,22},{7,23},{8,24},{9,... | collective-permute-start | bytes 18440 | tf_op jit(solution)/shard_map/ppermute | solution.py:32
  49.9 0.7 copy-start.3
  52.3 16.1 %all-to-all-start.1 = ((f32[32,2,128]{2,1,0:T(2,128)}), f32[32,2,128]{2,1,0:T(2,128)S(1)}, u32[]{:S(2)}, u32[]{:S(2)}) async-start(f32[32,2,128]{2,1,0:T(2,128)} %carry.1), calls=%async_computation.1 | async-start | bytes 65536 | tf_op jit(solution)/shard_map/all_to_all | solution.py:327
  62.5 0.6 copy-start.8
  68.3 0.6 copy-start.7
  71.5 3.4 %collective-permute-start.2 = (bf16[128,512]{1,0:T(8,128)(2,1)}, bf16[128,512]{1,0:T(8,128)(2,1)S(1)}, u32[]{:S(2)}, u32[]{:S(2)}) collective-permute-start(bf16[128,512]{1,0:T(8,128)(2,1)} %back.1), channel_id=1, source_target_pairs={{4,20},{5,21},{6,22},{7,23},{12,28},{13,29},{14,30},{15,31},{16,0}... | collective-permute-start | bytes 393224 | tf_op jit(solution)/shard_map/ppermute | solution.py:27
  75.8 12.3 %collective-permute-start.3 = (bf16[256,512]{1,0:T(8,128)(2,1)S(1)}, bf16[256,512]{1,0:T(8,128)(2,1)S(1)}, u32[]{:S(2)}, u32[]{:S(2)}) collective-permute-start(bf16[256,512]{1,0:T(8,128)(2,1)S(1)} %pad_maximum_fusion.1), channel_id=1, source_target_pairs={{0,256},{1,257},{2,258},{3,259},{8,264},{9,265},{10,266},{11,267},... | collective-permute-start | bytes 786440 | tf_op jit(solution)/shard_map/ppermute | solution.py:27
  89.0 18.8 %copy-start = (bf16[512,512]{1,0:T(8,128)(2,1)}, bf16[512,512]{1,0:T(8,128)(2,1)S(1)}, u32[]{:S(2)}) copy-start(bf16[512,512]{1,0:T(8,128)(2,1)S(1)} %pad_maximum_fusion.refs_0_) | copy-start | bytes 1572868
  89.0 8.0 %collective-permute-start.5 = (bf16[512,512]{1,0:T(8,128)(2,1)S(1)}, bf16[512,512]{1,0:T(8,128)(2,1)S(1)}, u32[]{:S(2)}, u32[]{:S(2)}) collective-permute-start(bf16[512,512]{1,0:T(8,128)(2,1)S(1)} %pad_maximum_fusion.refs_0_), channel_id=1, source_target_pairs={{0,12},{1,13},{2,14},{3,15},{8,4},{9,5},{10,6},{11,7},{20,16},{21,... | collective-permute-start | bytes 1572872 | tf_op jit(solution)/shard_map/ppermute | solution.py:27
  90.4 8.0 %collective-permute-start.4 = (bf16[512,512]{1,0:T(8,128)(2,1)S(1)}, bf16[512,512]{1,0:T(8,128)(2,1)S(1)}, u32[]{:S(2)}, u32[]{:S(2)}) collective-permute-start(bf16[512,512]{1,0:T(8,128)(2,1)S(1)} %pad_maximum_fusion.refs_0_), channel_id=1, source_target_pairs={{0,4},{1,5},{2,6},{3,7},{8,12},{9,13},{10,14},{11,15},{20,24},{21,... | collective-permute-start | bytes 1572872 | tf_op jit(solution)/shard_map/ppermute | solution.py:27
  97.0 10.9 %copy-start.1 = (bf16[512,512]{1,0:T(8,128)(2,1)}, bf16[512,512]{1,0:T(8,128)(2,1)S(1)}, u32[]{:S(2)}) copy-start(bf16[512,512]{1,0:T(8,128)(2,1)S(1)} %collective-permute-done.5.refs_2_) | copy-start | bytes 1572868
  97.0 8.4 %collective-permute-start.7 = (bf16[256,512]{1,0:T(8,128)(2,1)S(1)}, bf16[256,512]{1,0:T(8,128)(2,1)S(1)}, u32[]{:S(2)}, u32[]{:S(2)}) collective-permute-start(bf16[256,512]{1,0:T(8,128)(2,1)S(1)} %slice.32), channel_id=1, source_target_pairs={{4,0},{5,1},{6,2},{7,3},{12,8},{13,9},{14,10},{15,11},{16,28},{17,... | collective-permute-start | bytes 786440 | tf_op jit(solution)/shard_map/ppermute | solution.py:27
  98.4 9.5 %copy-start.2 = (bf16[512,512]{1,0:T(8,128)(2,1)}, bf16[512,512]{1,0:T(8,128)(2,1)S(1)}, u32[]{:S(2)}) copy-start(bf16[512,512]{1,0:T(8,128)(2,1)S(1)} %collective-permute-done.4.refs_1_) | copy-start | bytes 1572868
  98.4 9.5 %collective-permute-start.6 = (bf16[256,512]{1,0:T(8,128)(2,1)S(1)}, bf16[256,512]{1,0:T(8,128)(2,1)S(1)}, u32[]{:S(2)}, u32[]{:S(2)}) collective-permute-start(bf16[256,512]{1,0:T(8,128)(2,1)S(1)} %slice.31), channel_id=1, source_target_pairs={{4,8},{5,9},{6,10},{7,11},{12,0},{13,1},{14,2},{15,3},{16,20},{17,... | collective-permute-start | bytes 786440 | tf_op jit(solution)/shard_map/ppermute | solution.py:27
  105.4 2.5 %copy-start.4 = (bf16[256,512]{1,0:T(8,128)(2,1)}, bf16[256,512]{1,0:T(8,128)(2,1)S(1)}, u32[]{:S(2)}) copy-start(bf16[256,512]{1,0:T(8,128)(2,1)S(1)} %collective-permute-done.7.refs_4_) | copy-start | bytes 786436
  107.9 0.7 copy-start.5
  115.2 4.8 %collective-permute-start.8 = (f32[4,128,512]{2,1,0:T(8,128)}, f32[4,128,512]{2,1,0:T(8,128)S(1)}, u32[]{:S(2)}, u32[]{:S(2)}) collective-permute-start(f32[4,128,512]{2,1,0:T(8,128)} %get-tuple-element.18), channel_id=1, source_target_pairs={{0,16},{1,17},{2,18},{3,19},{4,20},{5,21},{6,22},{7,23},{8,24},{9,... | collective-permute-start | bytes 3145736 | tf_op jit(solution)/shard_map/ppermute | solution.py:27
  121.5 12.9 %collective-permute-start.9 = (bf16[128,512]{1,0:T(8,128)(2,1)S(1)}, bf16[128,512]{1,0:T(8,128)(2,1)S(1)}, u32[]{:S(2)}, u32[]{:S(2)}) collective-permute-start(bf16[128,512]{1,0:T(8,128)(2,1)S(1)} %get-tuple-element.21), channel_id=1, source_target_pairs={{0,1},{1,2},{2,3},{3,0},{4,5},{5,6},{6,7},{7,4},{8,9},{9,10},{10,1... | collective-permute-start | bytes 393224 | tf_op jit(solution)/shard_map/ppermute | solution.py:27
  126.3 10.3 %collective-permute-start.11 = (bf16[128,512]{1,0:T(8,128)(2,1)S(1)}, bf16[128,512]{1,0:T(8,128)(2,1)S(1)}, u32[]{:S(2)}, u32[]{:S(2)}) collective-permute-start(bf16[128,512]{1,0:T(8,128)(2,1)S(1)} %get-tuple-element.22), channel_id=1, source_target_pairs={{0,3},{1,0},{2,1},{3,2},{4,7},{5,4},{6,5},{7,6},{8,11},{9,8},{10,9... | collective-permute-start | bytes 393224 | tf_op jit(solution)/shard_map/ppermute | solution.py:27
  129.7 12.3 %collective-permute-start.10 = (bf16[128,512]{1,0:T(8,128)(2,1)S(1)}, bf16[128,512]{1,0:T(8,128)(2,1)S(1)}, u32[]{:S(2)}, u32[]{:S(2)}) collective-permute-start(bf16[128,512]{1,0:T(8,128)(2,1)S(1)} %get-tuple-element.23), channel_id=1, source_target_pairs={{0,2},{1,3},{2,0},{3,1},{4,6},{5,7},{6,4},{7,5},{8,10},{9,11},{10,... | collective-permute-start | bytes 393224 | tf_op jit(solution)/shard_map/ppermute | solution.py:27
  142.1 15.0 %collective-permute-start.12 = (bf16[128,512]{1,0:T(8,128)(2,1)S(1)}, bf16[128,512]{1,0:T(8,128)(2,1)S(1)}, u32[]{:S(2)}, u32[]{:S(2)}) collective-permute-start(bf16[128,512]{1,0:T(8,128)(2,1)S(1)} %fusion.1), channel_id=1, source_target_pairs={{0,0},{1,4},{2,256},{3,260},{4,1},{5,5},{6,257},{7,261},{8,2},{9,6... | collective-permute-start | bytes 393224 | tf_op jit(solution)/shard_map/ppermute | solution.py:27
Sparse Core Ops, SparseCore 0:
  11.5 62.1 all-gather.2

commit v4 on v3

--- a/solution.py
+++ b/solution.py
@@ -155,7 +155,7 @@
 
 def mix_kernel(table_ref, *refs):
     line, fwd, bwd, hf, hb, weights = refs[:6]
-    keep_ref, send_ref, g, w, acc, g_sem, w_sem = refs[6:]
+    keep_ref, send_ref, g, w, g_sem, w_sem = refs[6:]
     own = table_ref[0] == 1
     yl = table_ref[1]
     low, high = table_ref[2], table_ref[3]
@@ -197,16 +197,16 @@
         for copy in from_others():
             copy.wait()
 
-    for i in range(8):
-        loads[i].wait()
-        part = jnp.dot(g[i % 2], w[i], preferred_element_type=jnp.float32).reshape(4, 128, 256)
-        acc[i // 2] = part if i % 2 == 0 else acc[i // 2] + part
-    for d in range(4):
-        block = lax.rem(yl + d, 4)
-        for half in range(2):
-            cols = slice(half * 256, half * 256 + 256)
-            keep_ref[d, :, cols] = acc[lax.rem(block, 2) * 2 + half, block // 2 * 2]
-            send_ref[d, :, cols] = acc[lax.rem(block, 2) * 2 + half, block // 2 * 2 + 1]
+    for i in range(4):
+        loads[2 * i].wait()
+        loads[2 * i + 1].wait()
+        part = jnp.dot(g[0], w[2 * i], preferred_element_type=jnp.float32)
+        part = part + jnp.dot(g[1], w[2 * i + 1], preferred_element_type=jnp.float32)
+        cols = slice(i % 2 * 256, i % 2 * 256 + 256)
+        for far in range(2):
+            d = lax.rem(far * 2 + i // 2 - yl + 4, 4)
+            keep_ref[d, :, cols] = part[far * 256 : far * 256 + 128]
+            send_ref[d, :, cols] = part[far * 256 + 128 : far * 256 + 256]
 
 
 TINY = pl.CostEstimate(flops=1, bytes_accessed=1, transcendentals=0)
@@ -274,7 +274,6 @@
         scratch_shapes=[
             pltpu.VMEM((2, 512, 512), jnp.bfloat16),
             pltpu.VMEM((8, 512, 256), jnp.bfloat16),
-            pltpu.VMEM((4, 4, 128, 256), jnp.float32),
             pltpu.SemaphoreType.DMA((3,)),
             pltpu.SemaphoreType.DMA((8,)),
         ],
@@ -319,11 +318,11 @@
 
     feat = features.transpose(1, 0, 2)
     ends = first(feat, short_filter, decay_rate)
-    ends, weight = tie((ends, weight))
-    weights = lax.all_gather(weight, "ctx", axis_index_groups=along_z)
     ends = lax.all_to_all(ends, "ctx", 0, 0, tiled=True)
     ctx = index // 16
     rate = lax.dynamic_slice(decay_rate, (ctx // 4 * 2, ctx % 4 * 128), (2, 128))
+    ends, weight, halo, rate = tie((ends, weight, halo, rate))
+    weights = lax.all_gather(weight, "ctx", axis_index_groups=along_z)
     incoming = lax.all_to_all(carry(ends, rate), "ctx", 0, 0, tiled=True).reshape(64, 128)
 
     query, drive, half = middle(feat, halo.transpose(1, 0, 2), short_filter, decay_rate)

time: 166 us -> 160 us (0.964)
  starting transfers between devices: 72.3 us -> 68.8 us
    all_to_all x1, starting transfers between devices: 26.5 us -> 15.8 us  [body(): ends = lax.all_to_all(ends, 'ctx', 0, 0, tiled=True)]
    all_to_all x1, waiting for transfers between devices: 7.85 us -> 0.01 us  [body(): ends = lax.all_to_all(ends, 'ctx', 0, 0, tiled=True)]
    ppermute x1, waiting for transfers between devices: 0.01 us -> 5.49 us  [from_behind(): return lax.ppermute(value, axes, pairs)]
    all_to_all x1, starting transfers between devices: 8.85 us -> 14 us  [body(): lax.all_to_all(carry(ends, rate), 'ctx', 0, 0, tiled=True).reshape(64, 128)]
    ppermute x1, starting transfers between devices: 2.06 us -> 4.71 us  [from_behind(): return lax.ppermute(value, axes, pairs)]
  transfers between devices with their start and end apart: 16 -> 16, of which waited for: 11 -> 11; matrix products, arithmetic and copies ran while one was open for 4% -> 4% of each run, Pallas kernels for 6% -> 4%
where the time goes in v4:
time: 160 us; the launch traced here: 159 us
  starting transfers between devices  68.8 us (43%)
  waiting for transfers between devices  50.1 us (31%)
  Pallas kernels  15.6 us (10%)
  between operations  13.8 us (9%)
  other arithmetic  5.43 us (3%)
  local copies, waits for them, and re-layouts  4.85 us (3%)
    ppermute x12, waiting for transfers between devices, move(): return lax.ppermute(value, axes, pairs)  41.4 us
    ppermute x12, starting transfers between devices, move(): return lax.ppermute(value, axes, pairs)  34.2 us
    all_to_all x1, starting transfers between devices, body(): ends = lax.all_to_all(ends, 'ctx', 0, 0, tiled=True)  15.8 us
    all_to_all x1, starting transfers between devices, body(): lax.all_to_all(carry(ends, rate), 'ctx', 0, 0, tiled=True).reshape(64, 128)  14 us
    pallas_call x1, Pallas kernels, mix(): pl.pallas_call(mix_kernel, out_shape=(out, out), in_specs=[SMEM] + [pl.Bl...  6.4 us
    ppermute x1, waiting for transfers between devices, from_behind(): return lax.ppermute(value, axes, pairs)  5.49 us
    ppermute x1, starting transfers between devices, from_behind(): return lax.ppermute(value, axes, pairs)  4.71 us
  transfers between devices with their start and end apart: 16, of which 11 were waited for; matrix products, arithmetic and copies ran while one was open for 4% of the time, Pallas kernels for 4%

profile of v4, /device:TPU:56, one launch (start us, length us, event | category | flops | bytes accessed | tf_op | source)
XLA Modules:
  0.0 158.6 jit_solution(10466426451271269133)
XLA Ops:
  6.5 2.4 %first.1 = f32[32,16,128]{2,1,0:T(8,128)} custom-call(bf16[3,128,512]{2,1,0:T(8,128)(2,1)} %bitcast.22, f32[3,3,512]{2,1,0:T(4,128)} %taps_ref.3, f32[16,512]{1,0:T(8,128)} %rate_ref.5), custom_call_target="tpu_custom_call" | custom-call | flops 1 | bytes 1 | tf_op jit(solution)/shard_map/first/pallas_call | solution.py:217
  9.0 15.8 %all-to-all-start = ((f32[32,16,128]{2,1,0:T(8,128)}), f32[32,16,128]{2,1,0:T(8,128)S(1)}, u32[]{:S(2)}, u32[]{:S(2)}) async-start(f32[32,16,128]{2,1,0:T(8,128)} %first.1), calls=%async_computation | async-start | bytes 524288 | tf_op jit(solution)/shard_map/all_to_all | solution.py:321
  24.8 0.0 all-gather.3.cloned.1.call-start
  24.9 1.6 %collective-permute-start = (bf16[512,256]{1,0:T(8,128)(2,1)}, bf16[512,256]{1,0:T(8,128)(2,1)S(1)}, u32[]{:S(2)}, u32[]{:S(2)}) collective-permute-start(bf16[512,256]{1,0:T(8,128)(2,1)} %param.11), channel_id=1, source_target_pairs={{0,0},{1,1},{2,2},{3,3},{4,16},{5,17},{6,18},{7,19},{8,32},{9,33},... | collective-permute-start | bytes 786440 | tf_op jit(solution)/shard_map/ppermute | solution.py:27
  26.5 0.7 slice.24
  27.2 4.7 %collective-permute-start.1 = (bf16[2,3,512]{2,0,1:T(2,128)(2,1)S(1)}, bf16[2,3,512]{2,0,1:T(2,128)(2,1)S(1)}, u32[]{:S(2)}, u32[]{:S(2)}) collective-permute-start(bf16[2,3,512]{2,0,1:T(2,128)(2,1)S(1)} %slice.24), channel_id=1, source_target_pairs={{0,16},{1,17},{2,18},{3,19},{4,20},{5,21},{6,22},{7,23},{8,24},{9,... | collective-permute-start | bytes 18440 | tf_op jit(solution)/shard_map/ppermute | solution.py:32
  32.0 1.3 dynamic_slice.3.rate_ref
  33.3 5.5 %collective-permute-done.1 = bf16[2,3,512]{2,0,1:T(2,128)(2,1)S(1)} collective-permute-done((bf16[2,3,512]{2,0,1:T(2,128)(2,1)S(1)}, bf16[2,3,512]{2,0,1:T(2,128)(2,1)S(1)}, u32[]{:S(2)}, u32[]{:S(2)}) %collective-permute-start.1) | collective-permute-done | bytes 6176 | tf_op jit(solution)/shard_map/ppermute | solution.py:32
  38.8 0.0 collective-permute-done
  38.8 0.7 copy-done.6
  39.5 0.0 all-gather.3.cloned.1.call-update
  39.5 0.1 copy-done.3
  39.6 1.6 %carry.1 = f32[32,2,128]{2,1,0:T(2,128)} custom-call(f32[32,16,128]{2,1,0:T(8,128)} %copy-done.3, f32[2,128]{1,0:T(2,128)} %dynamic_slice.3.rate_ref), custom_call_target="tpu_custom_call" | custom-call | flops 1 | bytes 1 | tf_op jit(solution)/shard_map/carry/pallas_call | solution.py:229
  41.2 14.0 %all-to-all-start.1 = ((f32[32,2,128]{2,1,0:T(2,128)}), f32[32,2,128]{2,1,0:T(2,128)S(1)}, u32[]{:S(2)}, u32[]{:S(2)}) async-start(f32[32,2,128]{2,1,0:T(2,128)} %carry.1), calls=%async_computation.1 | async-start | bytes 65536 | tf_op jit(solution)/shard_map/all_to_all | solution.py:326
  55.3 1.4 sqrt_multiply_fusion.gain_ref
  56.7 2.6 %middle.1 = (f32[128,512]{1,0:T(8,128)}, f32[512,128]{1,0:T(8,128)}, f32[128,128]{1,0:T(8,128)}) custom-call(bf16[3,128,512]{2,1,0:T(8,128)(2,1)} %bitcast.23, bf16[3,2,512]{2,1,0:T(2,128)(2,1)} %bitcast.25, f32[3,3,512]{2,1,0:T(4,128)} %taps_ref.3, f32[16,512]{1,0:T(8,128)} %rate_ref.5), custom_call_target="tpu_custom_call" | custom-call | flops 1 | bytes 1 | tf_op jit(solution)/shard_map/middle/pallas_call | solution.py:240
  59.3 3.2 %all-to-all-done.1 = f32[32,2,128]{2,1,0:T(2,128)S(1)} async-done(((f32[32,2,128]{2,1,0:T(2,128)}), f32[32,2,128]{2,1,0:T(2,128)S(1)}, u32[]{:S(2)}, u32[]{:S(2)}) %all-to-all-start.1) | async-done | bytes 32800 | tf_op jit(solution)/shard_map/all_to_all | solution.py:326
  62.5 0.6 copy-done.7
  63.1 2.5 %back.1 = bf16[128,512]{1,0:T(8,128)(2,1)} custom-call(f32[128,512]{1,0:T(8,128)} %get-tuple-element.15.query_ref, f32[512,128]{1,0:T(8,128)} %get-tuple-element.16.drive_ref, f32[128,128]{1,0:T(8,128)} %get-tuple-element.17.half_ref, f32[64,128]{1,0:T(8,128)} %bitcast.24, f32[16,512]{1,0:T(8,128)} %rate_ref.5, f32[16,512]{1,0:T(8,128)} %sqrt_multiply_fusion.gain_ref, ...), custom_call_target="tpu_custom_call" | custom-call | flops 1 | bytes 1 | tf_op jit(solution)/shard_map/back/pallas_call | solution.py:256
  65.6 1.3 collective-permute-start.2
  66.9 2.2 %collective-permute-done.2 = bf16[128,512]{1,0:T(8,128)(2,1)S(1)} collective-permute-done((bf16[128,512]{1,0:T(8,128)(2,1)}, bf16[128,512]{1,0:T(8,128)(2,1)S(1)}, u32[]{:S(2)}, u32[]{:S(2)}) %collective-permute-start.2) | collective-permute-done | bytes 131104 | tf_op jit(solution)/shard_map/ppermute | solution.py:27
  69.1 0.9 pad_maximum_fusion.1
  70.0 7.3 %collective-permute-start.3 = (bf16[256,512]{1,0:T(8,128)(2,1)S(1)}, bf16[256,512]{1,0:T(8,128)(2,1)S(1)}, u32[]{:S(2)}, u32[]{:S(2)}) collective-permute-start(bf16[256,512]{1,0:T(8,128)(2,1)S(1)} %pad_maximum_fusion.1), channel_id=1, source_target_pairs={{0,256},{1,257},{2,258},{3,259},{8,264},{9,265},{10,266},{11,267},... | collective-permute-start | bytes 786440 | tf_op jit(solution)/shard_map/ppermute | solution.py:27
  77.3 5.0 %collective-permute-done.3 = bf16[256,512]{1,0:T(8,128)(2,1)S(1)} collective-permute-done((bf16[256,512]{1,0:T(8,128)(2,1)S(1)}, bf16[256,512]{1,0:T(8,128)(2,1)S(1)}, u32[]{:S(2)}, u32[]{:S(2)}) %collective-permute-start.3) | collective-permute-done | bytes 262176 | tf_op jit(solution)/shard_map/ppermute | solution.py:27
  82.3 0.9 pad_maximum_fusion.refs_0_
  83.2 1.3 collective-permute-start.5
  84.5 1.3 collective-permute-start.4
  85.9 5.3 %collective-permute-done.5.refs_2_ = bf16[512,512]{1,0:T(8,128)(2,1)S(1)} collective-permute-done((bf16[512,512]{1,0:T(8,128)(2,1)S(1)}, bf16[512,512]{1,0:T(8,128)(2,1)S(1)}, u32[]{:S(2)}, u32[]{:S(2)}) %collective-permute-start.5) | collective-permute-done | bytes 524320 | tf_op jit(solution)/shard_map/ppermute | solution.py:27
  91.2 1.3 collective-permute-start.7
  92.5 0.0 collective-permute-done.4.refs_1_
  92.6 1.3 collective-permute-start.6
  94.0 0.6 pad_add_fusion.table_ref
  94.6 5.3 %collective-permute-done.7.refs_4_ = bf16[256,512]{1,0:T(8,128)(2,1)S(1)} collective-permute-done((bf16[256,512]{1,0:T(8,128)(2,1)S(1)}, bf16[256,512]{1,0:T(8,128)(2,1)S(1)}, u32[]{:S(2)}, u32[]{:S(2)}) %collective-permute-start.7) | collective-permute-done | bytes 262176 | tf_op jit(solution)/shard_map/ppermute | solution.py:27
  99.9 2.1 %collective-permute-done.6.refs_3_ = bf16[256,512]{1,0:T(8,128)(2,1)S(1)} collective-permute-done((bf16[256,512]{1,0:T(8,128)(2,1)S(1)}, bf16[256,512]{1,0:T(8,128)(2,1)S(1)}, u32[]{:S(2)}, u32[]{:S(2)}) %collective-permute-start.6) | collective-permute-done | bytes 262176 | tf_op jit(solution)/shard_map/ppermute | solution.py:27
  102.1 0.7 copy-done.5
  102.8 6.4 %mix.1 = (f32[4,128,512]{2,1,0:T(8,128)}, f32[4,128,512]{2,1,0:T(8,128)}) custom-call(s32[4]{0:T(128)} %pad_add_fusion.table_ref, bf16[512,512]{1,0:T(8,128)(2,1)} %copy-done, bf16[512,512]{1,0:T(8,128)(2,1)} %copy-done.2, bf16[512,512]{1,0:T(8,128)(2,1)} %copy-done.1, bf16[256,512]{1,0:T(8,128)(2,1)} %copy-done.5, bf16[256,512]{1,0:T(8,128)(2,1)} %copy-done.4, ...), custom_call_target="tpu_custom_call" | custom-call | flops 1100000000 | bytes 7000000 | tf_op jit(solution)/shard_map/mix/pallas_call | solution.py:269
  109.2 1.9 %collective-permute-start.8 = (f32[4,128,512]{2,1,0:T(8,128)}, f32[4,128,512]{2,1,0:T(8,128)S(1)}, u32[]{:S(2)}, u32[]{:S(2)}) collective-permute-start(f32[4,128,512]{2,1,0:T(8,128)} %get-tuple-element.22), channel_id=1, source_target_pairs={{0,16},{1,17},{2,18},{3,19},{4,20},{5,21},{6,22},{7,23},{8,24},{9,... | collective-permute-start | bytes 3145736 | tf_op jit(solution)/shard_map/ppermute | solution.py:27
  111.1 2.8 %collective-permute-done.8 = f32[4,128,512]{2,1,0:T(8,128)S(1)} collective-permute-done((f32[4,128,512]{2,1,0:T(8,128)}, f32[4,128,512]{2,1,0:T(8,128)S(1)}, u32[]{:S(2)}, u32[]{:S(2)}) %collective-permute-start.8) | collective-permute-done | bytes 1048608 | tf_op jit(solution)/shard_map/ppermute | solution.py:27
  113.9 1.5 fusion.2
  115.5 4.8 %collective-permute-start.9 = (bf16[128,512]{1,0:T(8,128)(2,1)S(1)}, bf16[128,512]{1,0:T(8,128)(2,1)S(1)}, u32[]{:S(2)}, u32[]{:S(2)}) collective-permute-start(bf16[128,512]{1,0:T(8,128)(2,1)S(1)} %get-tuple-element.25), channel_id=1, source_target_pairs={{0,1},{1,2},{2,3},{3,0},{4,5},{5,6},{6,7},{7,4},{8,9},{9,10},{10,1... | collective-permute-start | bytes 393224 | tf_op jit(solution)/shard_map/ppermute | solution.py:27
  120.3 3.0 %collective-permute-start.11 = (bf16[128,512]{1,0:T(8,128)(2,1)S(1)}, bf16[128,512]{1,0:T(8,128)(2,1)S(1)}, u32[]{:S(2)}, u32[]{:S(2)}) collective-permute-start(bf16[128,512]{1,0:T(8,128)(2,1)S(1)} %get-tuple-element.26), channel_id=1, source_target_pairs={{0,3},{1,0},{2,1},{3,2},{4,7},{5,4},{6,5},{7,6},{8,11},{9,8},{10,9... | collective-permute-start | bytes 393224 | tf_op jit(solution)/shard_map/ppermute | solution.py:27
  123.3 4.7 %collective-permute-start.10 = (bf16[128,512]{1,0:T(8,128)(2,1)S(1)}, bf16[128,512]{1,0:T(8,128)(2,1)S(1)}, u32[]{:S(2)}, u32[]{:S(2)}) collective-permute-start(bf16[128,512]{1,0:T(8,128)(2,1)S(1)} %get-tuple-element.27), channel_id=1, source_target_pairs={{0,2},{1,3},{2,0},{3,1},{4,6},{5,7},{6,4},{7,5},{8,10},{9,11},{10,... | collective-permute-start | bytes 393224 | tf_op jit(solution)/shard_map/ppermute | solution.py:27
  128.0 2.1 %collective-permute-done.11 = bf16[128,512]{1,0:T(8,128)(2,1)S(1)} collective-permute-done((bf16[128,512]{1,0:T(8,128)(2,1)S(1)}, bf16[128,512]{1,0:T(8,128)(2,1)S(1)}, u32[]{:S(2)}, u32[]{:S(2)}) %collective-permute-start.11) | collective-permute-done | bytes 131104 | tf_op jit(solution)/shard_map/ppermute | solution.py:27
  130.2 5.4 %collective-permute-done.10 = bf16[128,512]{1,0:T(8,128)(2,1)S(1)} collective-permute-done((bf16[128,512]{1,0:T(8,128)(2,1)S(1)}, bf16[128,512]{1,0:T(8,128)(2,1)S(1)}, u32[]{:S(2)}, u32[]{:S(2)}) %collective-permute-start.10) | collective-permute-done | bytes 131104 | tf_op jit(solution)/shard_map/ppermute | solution.py:27
  135.6 0.1 fusion.1
  135.6 4.3 %collective-permute-start.12 = (bf16[128,512]{1,0:T(8,128)(2,1)S(1)}, bf16[128,512]{1,0:T(8,128)(2,1)S(1)}, u32[]{:S(2)}, u32[]{:S(2)}) collective-permute-start(bf16[128,512]{1,0:T(8,128)(2,1)S(1)} %fusion.1), channel_id=1, source_target_pairs={{0,0},{1,4},{2,256},{3,260},{4,1},{5,5},{6,257},{7,261},{8,2},{9,6... | collective-permute-start | bytes 393224 | tf_op jit(solution)/shard_map/ppermute | solution.py:27
  140.0 11.2 %collective-permute-done.12 = bf16[128,512]{1,0:T(8,128)(2,1)S(1)} collective-permute-done((bf16[128,512]{1,0:T(8,128)(2,1)S(1)}, bf16[128,512]{1,0:T(8,128)(2,1)S(1)}, u32[]{:S(2)}, u32[]{:S(2)}) %collective-permute-start.12) | collective-permute-done | bytes 131104 | tf_op jit(solution)/shard_map/ppermute | solution.py:27
  151.1 0.7 copy.8
  (20 shorter events, 0.1 us)
Async XLA Ops:
  9.0 29.8 %all-to-all-start = ((f32[32,16,128]{2,1,0:T(8,128)}), f32[32,16,128]{2,1,0:T(8,128)S(1)}, u32[]{:S(2)}, u32[]{:S(2)}) async-start(f32[32,16,128]{2,1,0:T(8,128)} %first.1), calls=%async_computation | async-start | bytes 524288 | tf_op jit(solution)/shard_map/all_to_all | solution.py:321
  24.8 77.2 %all-gather.3.cloned.1.call-start = ((), (), s32[]{:S(2)}) async-start(), calls=%async_computation.2 | async-start | bytes 2359296 | tf_op jit(solution)/shard_map/all_gather | solution.py:325
  24.9 13.9 %collective-permute-start = (bf16[512,256]{1,0:T(8,128)(2,1)}, bf16[512,256]{1,0:T(8,128)(2,1)S(1)}, u32[]{:S(2)}, u32[]{:S(2)}) collective-permute-start(bf16[512,256]{1,0:T(8,128)(2,1)} %param.11), channel_id=1, source_target_pairs={{0,0},{1,1},{2,2},{3,3},{4,16},{5,17},{6,18},{7,19},{8,32},{9,33},... | collective-permute-start | bytes 786440 | tf_op jit(solution)/shard_map/ppermute | solution.py:27
  27.2 11.6 %collective-permute-start.1 = (bf16[2,3,512]{2,0,1:T(2,128)(2,1)S(1)}, bf16[2,3,512]{2,0,1:T(2,128)(2,1)S(1)}, u32[]{:S(2)}, u32[]{:S(2)}) collective-permute-start(bf16[2,3,512]{2,0,1:T(2,128)(2,1)S(1)} %slice.24), channel_id=1, source_target_pairs={{0,16},{1,17},{2,18},{3,19},{4,20},{5,21},{6,22},{7,23},{8,24},{9,... | collective-permute-start | bytes 18440 | tf_op jit(solution)/shard_map/ppermute | solution.py:32
  38.8 17.9 %copy-start.8 = (bf16[2,3,512]{2,0,1:T(2,128)(2,1)}, bf16[2,3,512]{2,0,1:T(2,128)(2,1)S(1)}, u32[]{:S(2)}) copy-start(bf16[2,3,512]{2,0,1:T(2,128)(2,1)S(1)} %collective-permute-done.1) | copy-start | bytes 18436
  38.8 0.7 copy-start.6
  38.8 0.8 copy-start.3
  41.2 21.2 %all-to-all-start.1 = ((f32[32,2,128]{2,1,0:T(2,128)}), f32[32,2,128]{2,1,0:T(2,128)S(1)}, u32[]{:S(2)}, u32[]{:S(2)}) async-start(f32[32,2,128]{2,1,0:T(2,128)} %carry.1), calls=%async_computation.1 | async-start | bytes 65536 | tf_op jit(solution)/shard_map/all_to_all | solution.py:326
  62.5 0.6 copy-start.7
  65.6 3.4 %collective-permute-start.2 = (bf16[128,512]{1,0:T(8,128)(2,1)}, bf16[128,512]{1,0:T(8,128)(2,1)S(1)}, u32[]{:S(2)}, u32[]{:S(2)}) collective-permute-start(bf16[128,512]{1,0:T(8,128)(2,1)} %back.1), channel_id=1, source_target_pairs={{4,20},{5,21},{6,22},{7,23},{12,28},{13,29},{14,30},{15,31},{16,0}... | collective-permute-start | bytes 393224 | tf_op jit(solution)/shard_map/ppermute | solution.py:27
  70.0 12.3 %collective-permute-start.3 = (bf16[256,512]{1,0:T(8,128)(2,1)S(1)}, bf16[256,512]{1,0:T(8,128)(2,1)S(1)}, u32[]{:S(2)}, u32[]{:S(2)}) collective-permute-start(bf16[256,512]{1,0:T(8,128)(2,1)S(1)} %pad_maximum_fusion.1), channel_id=1, source_target_pairs={{0,256},{1,257},{2,258},{3,259},{8,264},{9,265},{10,266},{11,267},... | collective-permute-start | bytes 786440 | tf_op jit(solution)/shard_map/ppermute | solution.py:27
  83.2 18.8 %copy-start = (bf16[512,512]{1,0:T(8,128)(2,1)}, bf16[512,512]{1,0:T(8,128)(2,1)S(1)}, u32[]{:S(2)}) copy-start(bf16[512,512]{1,0:T(8,128)(2,1)S(1)} %pad_maximum_fusion.refs_0_) | copy-start | bytes 1572868
  83.2 8.0 %collective-permute-start.5 = (bf16[512,512]{1,0:T(8,128)(2,1)S(1)}, bf16[512,512]{1,0:T(8,128)(2,1)S(1)}, u32[]{:S(2)}, u32[]{:S(2)}) collective-permute-start(bf16[512,512]{1,0:T(8,128)(2,1)S(1)} %pad_maximum_fusion.refs_0_), channel_id=1, source_target_pairs={{0,12},{1,13},{2,14},{3,15},{8,4},{9,5},{10,6},{11,7},{20,16},{21,... | collective-permute-start | bytes 1572872 | tf_op jit(solution)/shard_map/ppermute | solution.py:27
  84.5 8.0 %collective-permute-start.4 = (bf16[512,512]{1,0:T(8,128)(2,1)S(1)}, bf16[512,512]{1,0:T(8,128)(2,1)S(1)}, u32[]{:S(2)}, u32[]{:S(2)}) collective-permute-start(bf16[512,512]{1,0:T(8,128)(2,1)S(1)} %pad_maximum_fusion.refs_0_), channel_id=1, source_target_pairs={{0,4},{1,5},{2,6},{3,7},{8,12},{9,13},{10,14},{11,15},{20,24},{21,... | collective-permute-start | bytes 1572872 | tf_op jit(solution)/shard_map/ppermute | solution.py:27
  91.2 10.9 %copy-start.1 = (bf16[512,512]{1,0:T(8,128)(2,1)}, bf16[512,512]{1,0:T(8,128)(2,1)S(1)}, u32[]{:S(2)}) copy-start(bf16[512,512]{1,0:T(8,128)(2,1)S(1)} %collective-permute-done.5.refs_2_) | copy-start | bytes 1572868
  91.2 8.7 %collective-permute-start.7 = (bf16[256,512]{1,0:T(8,128)(2,1)S(1)}, bf16[256,512]{1,0:T(8,128)(2,1)S(1)}, u32[]{:S(2)}, u32[]{:S(2)}) collective-permute-start(bf16[256,512]{1,0:T(8,128)(2,1)S(1)} %slice.32), channel_id=1, source_target_pairs={{4,0},{5,1},{6,2},{7,3},{12,8},{13,9},{14,10},{15,11},{16,28},{17,... | collective-permute-start | bytes 786440 | tf_op jit(solution)/shard_map/ppermute | solution.py:27
  92.5 9.5 %copy-start.2 = (bf16[512,512]{1,0:T(8,128)(2,1)}, bf16[512,512]{1,0:T(8,128)(2,1)S(1)}, u32[]{:S(2)}) copy-start(bf16[512,512]{1,0:T(8,128)(2,1)S(1)} %collective-permute-done.4.refs_1_) | copy-start | bytes 1572868
  92.6 9.5 %collective-permute-start.6 = (bf16[256,512]{1,0:T(8,128)(2,1)S(1)}, bf16[256,512]{1,0:T(8,128)(2,1)S(1)}, u32[]{:S(2)}, u32[]{:S(2)}) collective-permute-start(bf16[256,512]{1,0:T(8,128)(2,1)S(1)} %slice.31), channel_id=1, source_target_pairs={{4,8},{5,9},{6,10},{7,11},{12,0},{13,1},{14,2},{15,3},{16,20},{17,... | collective-permute-start | bytes 786440 | tf_op jit(solution)/shard_map/ppermute | solution.py:27
  99.9 2.2 %copy-start.4 = (bf16[256,512]{1,0:T(8,128)(2,1)}, bf16[256,512]{1,0:T(8,128)(2,1)S(1)}, u32[]{:S(2)}) copy-start(bf16[256,512]{1,0:T(8,128)(2,1)S(1)} %collective-permute-done.7.refs_4_) | copy-start | bytes 786436
  102.0 0.7 copy-start.5
  109.2 4.8 %collective-permute-start.8 = (f32[4,128,512]{2,1,0:T(8,128)}, f32[4,128,512]{2,1,0:T(8,128)S(1)}, u32[]{:S(2)}, u32[]{:S(2)}) collective-permute-start(f32[4,128,512]{2,1,0:T(8,128)} %get-tuple-element.22), channel_id=1, source_target_pairs={{0,16},{1,17},{2,18},{3,19},{4,20},{5,21},{6,22},{7,23},{8,24},{9,... | collective-permute-start | bytes 3145736 | tf_op jit(solution)/shard_map/ppermute | solution.py:27
  115.5 12.6 %collective-permute-start.9 = (bf16[128,512]{1,0:T(8,128)(2,1)S(1)}, bf16[128,512]{1,0:T(8,128)(2,1)S(1)}, u32[]{:S(2)}, u32[]{:S(2)}) collective-permute-start(bf16[128,512]{1,0:T(8,128)(2,1)S(1)} %get-tuple-element.25), channel_id=1, source_target_pairs={{0,1},{1,2},{2,3},{3,0},{4,5},{5,6},{6,7},{7,4},{8,9},{9,10},{10,1... | collective-permute-start | bytes 393224 | tf_op jit(solution)/shard_map/ppermute | solution.py:27
  120.3 9.9 %collective-permute-start.11 = (bf16[128,512]{1,0:T(8,128)(2,1)S(1)}, bf16[128,512]{1,0:T(8,128)(2,1)S(1)}, u32[]{:S(2)}, u32[]{:S(2)}) collective-permute-start(bf16[128,512]{1,0:T(8,128)(2,1)S(1)} %get-tuple-element.26), channel_id=1, source_target_pairs={{0,3},{1,0},{2,1},{3,2},{4,7},{5,4},{6,5},{7,6},{8,11},{9,8},{10,9... | collective-permute-start | bytes 393224 | tf_op jit(solution)/shard_map/ppermute | solution.py:27
  123.3 12.2 %collective-permute-start.10 = (bf16[128,512]{1,0:T(8,128)(2,1)S(1)}, bf16[128,512]{1,0:T(8,128)(2,1)S(1)}, u32[]{:S(2)}, u32[]{:S(2)}) collective-permute-start(bf16[128,512]{1,0:T(8,128)(2,1)S(1)} %get-tuple-element.27), channel_id=1, source_target_pairs={{0,2},{1,3},{2,0},{3,1},{4,6},{5,7},{6,4},{7,5},{8,10},{9,11},{10,... | collective-permute-start | bytes 393224 | tf_op jit(solution)/shard_map/ppermute | solution.py:27
  135.6 15.5 %collective-permute-start.12 = (bf16[128,512]{1,0:T(8,128)(2,1)S(1)}, bf16[128,512]{1,0:T(8,128)(2,1)S(1)}, u32[]{:S(2)}, u32[]{:S(2)}) collective-permute-start(bf16[128,512]{1,0:T(8,128)(2,1)S(1)} %fusion.1), channel_id=1, source_target_pairs={{0,0},{1,4},{2,256},{3,260},{4,1},{5,5},{6,257},{7,261},{8,2},{9,6... | collective-permute-start | bytes 393224 | tf_op jit(solution)/shard_map/ppermute | solution.py:27
Sparse Core Ops, SparseCore 0:
  39.6 47.1 all-gather.2

commit v5 on v4

--- a/solution.py
+++ b/solution.py
@@ -157,8 +157,7 @@
     line, fwd, bwd, hf, hb, weights = refs[:6]
     keep_ref, send_ref, g, w, g_sem, w_sem = refs[6:]
     own = table_ref[0] == 1
-    yl = table_ref[1]
-    low, high = table_ref[2], table_ref[3]
+    low, high = table_ref[1], table_ref[2]
 
     def from_own():
         return [
@@ -204,9 +203,8 @@
         part = part + jnp.dot(g[1], w[2 * i + 1], preferred_element_type=jnp.float32)
         cols = slice(i % 2 * 256, i % 2 * 256 + 256)
         for far in range(2):
-            d = lax.rem(far * 2 + i // 2 - yl + 4, 4)
-            keep_ref[d, :, cols] = part[far * 256 : far * 256 + 128]
-            send_ref[d, :, cols] = part[far * 256 + 128 : far * 256 + 256]
+            keep_ref[far * 2 + i // 2, :, cols] = part[far * 256 : far * 256 + 128]
+            send_ref[far * 2 + i // 2, :, cols] = part[far * 256 + 128 : far * 256 + 256]
 
 
 TINY = pl.CostEstimate(flops=1, bytes_accessed=1, transcendentals=0)
@@ -286,7 +284,7 @@
 def body(features, short_filter, decay_rate, residue, skip, out_weight, axes, first, carry, middle, back, mix):
     positions = features.shape[0]
     index = lax.axis_index(axes)
-    yl, x, core = index % 4, index // 4 % 4, index // 16 % 2
+    x, core = index // 4 % 4, index // 16 % 2
 
     halo = from_behind(features[positions - 2 :], axes, 1)
 
@@ -321,12 +319,14 @@
     ends = lax.all_to_all(ends, "ctx", 0, 0, tiled=True)
     ctx = index // 16
     rate = lax.dynamic_slice(decay_rate, (ctx // 4 * 2, ctx % 4 * 128), (2, 128))
-    ends, weight, halo, rate = tie((ends, weight, halo, rate))
-    weights = lax.all_gather(weight, "ctx", axis_index_groups=along_z)
-    incoming = lax.all_to_all(carry(ends, rate), "ctx", 0, 0, tiled=True).reshape(64, 128)
-
     query, drive, half = middle(feat, halo.transpose(1, 0, 2), short_filter, decay_rate)
     gain = residue * jnp.sqrt(-jnp.expm1(-2.0 * decay_rate))
+    ends, rate, query, drive, half, gain = tie((ends, rate, query, drive, half, gain))
+    carried, weight = tie((carry(ends, rate), weight))
+    incoming = lax.all_to_all(carried, "ctx", 0, 0, tiled=True).reshape(64, 128)
+    copies = jnp.broadcast_to(weight[None], (8,) + weight.shape)
+    weights = lax.all_to_all(copies, "ctx", 0, 0, axis_index_groups=along_z, tiled=True)
+
     gated = back(query, drive, half, incoming, decay_rate, gain, skip[None])
 
     both = jnp.concatenate([gated, other_core(gated, others)], axis=0)
@@ -334,6 +334,7 @@
     line = jnp.concatenate([both, beyond], axis=0)
     fwd = move(line, axes, along("x", 1), mine)
     bwd = move(line, axes, along("x", -1), mine)
+    fwd, bwd, weights = tie((fwd, bwd, weights))
     half_rows = line.shape[0] // 2
     hf = move(fwd[:half_rows], axes, along("x", 1), others)
     hb = move(bwd[half_rows:], axes, along("x", -1), others)
@@ -341,12 +342,13 @@
     own = x % 2 == core
     low = jnp.where(own, x // 2, (x + 3) % 4 // 2)
     high = jnp.where(own, 1 - x // 2, (x + 1) % 4 // 2)
-    table = jnp.stack([own.astype(jnp.int32), yl, low, high]).astype(jnp.int32)
+    table = jnp.stack([own.astype(jnp.int32), low, high]).astype(jnp.int32)
     keep, send = mix(table, line, fwd, bwd, hf, hb, weights)
 
-    blocks = keep + other_core(send)
-    parts = [move(blocks[d].astype(jnp.bfloat16), axes, along("yl", d)) for d in range(1, 4)]
-    total = blocks[0] + sum(part.astype(jnp.float32) for part in parts)
+    blocks = (keep + other_core(send)).astype(jnp.bfloat16)
+    along_yl = [[x * 4 + yl for yl in range(4)] for x in range(4)]
+    blocks = lax.all_to_all(blocks, "tp", 0, 0, axis_index_groups=along_yl, tiled=True)
+    total = jnp.sum(blocks.astype(jnp.float32), axis=0)
     return move(
         total.astype(jnp.bfloat16), axes, lambda yh, z, core, x, yl: (yh ^ (yl // 2), z, core, yh * 2 + yl % 2, x)
     )

time: 160 us -> 176 us (1.10)
  blocking collectives: 0 us -> 35.5 us
  starting transfers between devices: 68.8 us -> 44.7 us
  waiting for transfers between devices: 50.1 us -> 64.4 us
  between operations: 13.8 us -> 0.28 us
  local copies, waits for them, and re-layouts: 4.85 us -> 8.06 us
    all_to_all x0 -> x2, blocking collectives: none -> 35.5 us  [the longest x1 18 us: body(): lax.all_to_all(blocks, 'tp', 0, 0, axis_index_groups=along_yl, tiled=True)]
    all_to_all x1, waiting for transfers between devices: 3.18 us -> 22.3 us  [body(): lax.all_to_all(copies, 'ctx', 0, 0, axis_index_groups=along_z, tiled=True)]
    ppermute x12 -> x9, starting transfers between devices: 34.2 us -> 20.5 us  [move(): return lax.ppermute(value, axes, pairs)]
    all_to_all x1, starting transfers between devices: 14 us -> 3.6 us  [body(): lax.all_to_all(copies, 'ctx', 0, 0, axis_index_groups=along_z, tiled=True)]
    ppermute x12 -> x9, waiting for transfers between devices: 41.4 us -> 38 us  [move(): return lax.ppermute(value, axes, pairs)]
    slice x1, local copies, waits for them, and re-layouts: 0.02 us -> 1.83 us  [body(): hf = move(fwd[:half_rows], axes, along('x', 1), others)]
  transfers between devices with their start and end apart: 16 -> 12, of which waited for: 11 -> 10; matrix products, arithmetic and copies ran while one was open for 4% -> 3% of each run, Pallas kernels for 4% -> 4%
where the time goes in v5:
time: 176 us; the launch traced here: 174 us
  waiting for transfers between devices  64.4 us (37%)
  starting transfers between devices  44.7 us (25%)
  blocking collectives  35.5 us (20%)
  Pallas kernels  15.5 us (9%)
  local copies, waits for them, and re-layouts  8.06 us (5%)
  other arithmetic  5.33 us (3%)
    ppermute x9, waiting for transfers between devices, move(): return lax.ppermute(value, axes, pairs)  38 us
    all_to_all x1, waiting for transfers between devices, body(): lax.all_to_all(copies, 'ctx', 0, 0, axis_index_groups=along_z, tiled=True)  22.3 us
    ppermute x9, starting transfers between devices, move(): return lax.ppermute(value, axes, pairs)  20.5 us
    all_to_all x1, blocking collectives, body(): lax.all_to_all(blocks, 'tp', 0, 0, axis_index_groups=along_yl, tiled=True)  18 us
    all_to_all x1, blocking collectives, body(): incoming = lax.all_to_all(carried, 'ctx', 0, 0, tiled=True).reshape(64, 128)  17.5 us
    all_to_all x1, starting transfers between devices, body(): ends = lax.all_to_all(ends, 'ctx', 0, 0, tiled=True)  15.8 us
    pallas_call x1, Pallas kernels, mix(): pl.pallas_call(mix_kernel, out_shape=(out, out), in_specs=[SMEM] + [pl.Bl...  6.39 us
    ppermute x1, starting transfers between devices, from_behind(): return lax.ppermute(value, axes, pairs)  4.71 us
  transfers between devices with their start and end apart: 12, of which 10 were waited for; matrix products, arithmetic and copies ran while one was open for 3% of the time, Pallas kernels for 4%

profile of v5, /device:TPU:56, one launch (start us, length us, event | category | flops | bytes accessed | tf_op | source)
XLA Modules:
  0.0 173.8 jit_solution(13502638089829478284)
XLA Ops:
  0.0 2.4 %first.1 = f32[32,16,128]{2,1,0:T(8,128)} custom-call(bf16[3,128,512]{2,1,0:T(8,128)(2,1)} %bitcast.7, f32[3,3,512]{2,1,0:T(4,128)} %taps_ref.3, f32[16,512]{1,0:T(8,128)} %rate_ref.5), custom_call_target="tpu_custom_call" | custom-call | flops 1 | bytes 1 | tf_op jit(solution)/shard_map/first/pallas_call | solution.py:215
  2.4 15.8 %all-to-all-start = ((f32[32,16,128]{2,1,0:T(8,128)}), f32[32,16,128]{2,1,0:T(8,128)S(1)}, u32[]{:S(2)}, u32[]{:S(2)}) async-start(f32[32,16,128]{2,1,0:T(8,128)} %first.1), calls=%async_computation | async-start | bytes 524288 | tf_op jit(solution)/shard_map/all_to_all | solution.py:319
  18.3 1.6 collective-permute-start.1
  19.9 0.7 slice.9
  20.6 4.7 %collective-permute-start = (bf16[2,3,512]{2,0,1:T(2,128)(2,1)S(1)}, bf16[2,3,512]{2,0,1:T(2,128)(2,1)S(1)}, u32[]{:S(2)}, u32[]{:S(2)}) collective-permute-start(bf16[2,3,512]{2,0,1:T(2,128)(2,1)S(1)} %slice.9), channel_id=1, source_target_pairs={{0,16},{1,17},{2,18},{3,19},{4,20},{5,21},{6,22},{7,23},{8,24},{9,... | collective-permute-start | bytes 18440 | tf_op jit(solution)/shard_map/ppermute | solution.py:32
  25.3 1.4 sqrt_multiply_fusion.gain_ref
  26.7 1.3 dynamic_slice.3.rate_ref
  28.1 4.1 %collective-permute-done = bf16[2,3,512]{2,0,1:T(2,128)(2,1)S(1)} collective-permute-done((bf16[2,3,512]{2,0,1:T(2,128)(2,1)S(1)}, bf16[2,3,512]{2,0,1:T(2,128)(2,1)S(1)}, u32[]{:S(2)}, u32[]{:S(2)}) %collective-permute-start) | collective-permute-done | bytes 6176 | tf_op jit(solution)/shard_map/ppermute | solution.py:32
  32.2 0.6 copy-done.5
  32.8 2.6 %middle.1 = (f32[128,512]{1,0:T(8,128)}, f32[512,128]{1,0:T(8,128)}, f32[128,128]{1,0:T(8,128)}) custom-call(bf16[3,128,512]{2,1,0:T(8,128)(2,1)} %bitcast.8, bf16[3,2,512]{2,1,0:T(2,128)(2,1)} %bitcast.10, f32[3,3,512]{2,1,0:T(4,128)} %taps_ref.3, f32[16,512]{1,0:T(8,128)} %rate_ref.5), custom_call_target="tpu_custom_call" | custom-call | flops 1 | bytes 1 | tf_op jit(solution)/shard_map/middle/pallas_call | solution.py:238
  35.4 0.0 all-to-all-done.ends_ref
  35.4 0.7 copy-done.3
  36.0 1.6 carry.1
  37.7 0.0 collective-permute-done.1
  37.7 17.5 %all_to_all.20 = f32[32,2,128]{2,1,0:T(2,128)} all-to-all(f32[32,2,128]{2,1,0:T(2,128)} %carry.1), channel_id=1, replica_groups=mesh['ctx'=32,'tp'=16] {'ctx'}, dimensions={0} | all-to-all | bytes 65536 | tf_op jit(solution)/shard_map/all_to_all | solution.py:326
  55.2 1.5 broadcast_in_dim.10
  56.7 3.6 %all-to-all-start.2 = ((bf16[8,512,256]{2,1,0:T(8,128)(2,1)}), bf16[8,512,256]{2,1,0:T(8,128)(2,1)S(1)}, u32[]{:S(2)}, u32[]{:S(2)}) async-start(bf16[8,512,256]{2,1,0:T(8,128)(2,1)} %broadcast_in_dim.10), calls=%async_computation.2 | async-start | bytes 4194304 | tf_op jit(solution)/shard_map/all_to_all | solution.py:328
  60.3 2.5 %back.1 = bf16[128,512]{1,0:T(8,128)(2,1)} custom-call(f32[128,512]{1,0:T(8,128)} %get-tuple-element.24.query_ref, f32[512,128]{1,0:T(8,128)} %get-tuple-element.25.drive_ref, f32[128,128]{1,0:T(8,128)} %get-tuple-element.26.half_ref, f32[64,128]{1,0:T(8,128)} %bitcast.9, f32[16,512]{1,0:T(8,128)} %rate_ref.5, f32[16,512]{1,0:T(8,128)} %sqrt_multiply_fusion.gain_ref, ...), custom_call_target="tpu_custom_call" | custom-call | flops 1 | bytes 1 | tf_op jit(solution)/shard_map/back/pallas_call | solution.py:254
  62.8 1.3 collective-permute-start.2
  64.1 2.2 %collective-permute-done.2 = bf16[128,512]{1,0:T(8,128)(2,1)S(1)} collective-permute-done((bf16[128,512]{1,0:T(8,128)(2,1)}, bf16[128,512]{1,0:T(8,128)(2,1)S(1)}, u32[]{:S(2)}, u32[]{:S(2)}) %collective-permute-start.2) | collective-permute-done | bytes 131104 | tf_op jit(solution)/shard_map/ppermute | solution.py:27
  66.3 0.9 pad_maximum_fusion.1
  67.2 7.3 %collective-permute-start.3 = (bf16[256,512]{1,0:T(8,128)(2,1)S(1)}, bf16[256,512]{1,0:T(8,128)(2,1)S(1)}, u32[]{:S(2)}, u32[]{:S(2)}) collective-permute-start(bf16[256,512]{1,0:T(8,128)(2,1)S(1)} %pad_maximum_fusion.1), channel_id=1, source_target_pairs={{0,256},{1,257},{2,258},{3,259},{8,264},{9,265},{10,266},{11,267},... | collective-permute-start | bytes 786440 | tf_op jit(solution)/shard_map/ppermute | solution.py:27
  74.5 5.0 %collective-permute-done.3 = bf16[256,512]{1,0:T(8,128)(2,1)S(1)} collective-permute-done((bf16[256,512]{1,0:T(8,128)(2,1)S(1)}, bf16[256,512]{1,0:T(8,128)(2,1)S(1)}, u32[]{:S(2)}, u32[]{:S(2)}) %collective-permute-start.3) | collective-permute-done | bytes 262176 | tf_op jit(solution)/shard_map/ppermute | solution.py:27
  79.4 0.9 pad_maximum_fusion.refs_0_
  80.4 0.0 copy-start.1
  80.4 1.3 collective-permute-start.5
  81.7 2.1 %collective-permute-start.4 = (bf16[512,512]{1,0:T(8,128)(2,1)S(1)}, bf16[512,512]{1,0:T(8,128)(2,1)}, u32[]{:S(2)}, u32[]{:S(2)}) collective-permute-start(bf16[512,512]{1,0:T(8,128)(2,1)S(1)} %pad_maximum_fusion.refs_0_), channel_id=1, source_target_pairs={{0,4},{1,5},{2,6},{3,7},{8,12},{9,13},{10,14},{11,15},{20,24},{21,... | collective-permute-start | bytes 1572872 | tf_op jit(solution)/shard_map/ppermute | solution.py:27
  83.8 4.5 %collective-permute-done.5.refs_2_ = bf16[512,512]{1,0:T(8,128)(2,1)S(1)} collective-permute-done((bf16[512,512]{1,0:T(8,128)(2,1)S(1)}, bf16[512,512]{1,0:T(8,128)(2,1)S(1)}, u32[]{:S(2)}, u32[]{:S(2)}) %collective-permute-start.5) | collective-permute-done | bytes 524320 | tf_op jit(solution)/shard_map/ppermute | solution.py:27
  88.4 1.3 collective-permute-done.4.refs_1_
  89.7 22.3 %all-to-all-done.2.refs_5_ = bf16[8,512,256]{2,1,0:T(8,128)(2,1)S(1)} async-done(((bf16[8,512,256]{2,1,0:T(8,128)(2,1)}), bf16[8,512,256]{2,1,0:T(8,128)(2,1)S(1)}, u32[]{:S(2)}, u32[]{:S(2)}) %all-to-all-start.2) | async-done | bytes 2097184 | tf_op jit(solution)/shard_map/all_to_all | solution.py:328
  112.0 1.8 %slice.10 = bf16[256,512]{1,0:T(8,128)(2,1)} slice(bf16[512,512]{1,0:T(8,128)(2,1)} %collective-permute-done.4.refs_1_), slice={[0:256], [0:512]} | slice | bytes 524288 | tf_op jit(solution)/shard_map/slice | solution.py:339
  113.8 0.7 slice.11
  114.6 1.3 collective-permute-start.7
  115.8 1.3 collective-permute-start.6
  117.3 0.6 pad_add_fusion.table_ref
  117.9 5.1 %collective-permute-done.7.refs_4_ = bf16[256,512]{1,0:T(8,128)(2,1)S(1)} collective-permute-done((bf16[256,512]{1,0:T(8,128)(2,1)}, bf16[256,512]{1,0:T(8,128)(2,1)S(1)}, u32[]{:S(2)}, u32[]{:S(2)}) %collective-permute-start.7) | collective-permute-done | bytes 262176 | tf_op jit(solution)/shard_map/ppermute | solution.py:27
  123.0 4.9 %collective-permute-done.6.refs_3_ = bf16[256,512]{1,0:T(8,128)(2,1)} collective-permute-done((bf16[256,512]{1,0:T(8,128)(2,1)}, bf16[256,512]{1,0:T(8,128)(2,1)}, u32[]{:S(2)}, u32[]{:S(2)}) %collective-permute-start.6) | collective-permute-done | bytes 262176 | tf_op jit(solution)/shard_map/ppermute | solution.py:27
  127.9 0.0 copy-done.1
  127.9 0.0 copy-done
  127.9 6.4 %mix.1 = (f32[4,128,512]{2,1,0:T(8,128)}, f32[4,128,512]{2,1,0:T(8,128)}) custom-call(s32[3]{0:T(128)} %pad_add_fusion.table_ref, bf16[512,512]{1,0:T(8,128)(2,1)} %copy-done.1, bf16[512,512]{1,0:T(8,128)(2,1)} %collective-permute-done.4.refs_1_, bf16[512,512]{1,0:T(8,128)(2,1)} %copy-done.2, bf16[256,512]{1,0:T(8,128)(2,1)} %collective-permute-done.6.refs_3_, ...), custom_call_target="tpu_custom_call" | custom-call | flops 1100000000 | bytes 7000000 | tf_op jit(solution)/shard_map/mix/pallas_call | solution.py:267
  134.3 1.9 %collective-permute-start.8 = (f32[4,128,512]{2,1,0:T(8,128)}, f32[4,128,512]{2,1,0:T(8,128)S(1)}, u32[]{:S(2)}, u32[]{:S(2)}) collective-permute-start(f32[4,128,512]{2,1,0:T(8,128)} %get-tuple-element.36), channel_id=1, source_target_pairs={{0,16},{1,17},{2,18},{3,19},{4,20},{5,21},{6,22},{7,23},{8,24},{9,... | collective-permute-start | bytes 3145736 | tf_op jit(solution)/shard_map/ppermute | solution.py:27
  136.3 2.8 %collective-permute-done.8 = f32[4,128,512]{2,1,0:T(8,128)S(1)} collective-permute-done((f32[4,128,512]{2,1,0:T(8,128)}, f32[4,128,512]{2,1,0:T(8,128)S(1)}, u32[]{:S(2)}, u32[]{:S(2)}) %collective-permute-start.8) | collective-permute-done | bytes 1048608 | tf_op jit(solution)/shard_map/ppermute | solution.py:27
  139.1 1.4 add_convert_fusion
  140.5 18.0 %all_to_all.21 = bf16[4,128,512]{2,1,0:T(8,128)(2,1)S(1)} all-to-all(bf16[4,128,512]{2,1,0:T(8,128)(2,1)S(1)} %add_convert_fusion), channel_id=1, replica_groups={{0,1,2,3},{4,5,6,7},{8,9,10,11},{12,13,14,15},{16,17,18,19},{20,21,22,2..., dimensions={0} | all-to-all | bytes 1048576 | tf_op jit(solution)/shard_map/all_to_all | solution.py:350
  158.5 0.1 reduce_sum.12
  158.6 2.4 %collective-permute-start.9 = (bf16[128,512]{1,0:T(8,128)(2,1)S(1)}, bf16[128,512]{1,0:T(8,128)(2,1)S(1)}, u32[]{:S(2)}, u32[]{:S(2)}) collective-permute-start(bf16[128,512]{1,0:T(8,128)(2,1)S(1)} %reduce_sum.12), channel_id=1, source_target_pairs={{0,0},{1,4},{2,256},{3,260},{4,1},{5,5},{6,257},{7,261},{8,2},{9,6... | collective-permute-start | bytes 393224 | tf_op jit(solution)/shard_map/ppermute | solution.py:27
  161.0 12.1 %collective-permute-done.9 = bf16[128,512]{1,0:T(8,128)(2,1)S(1)} collective-permute-done((bf16[128,512]{1,0:T(8,128)(2,1)S(1)}, bf16[128,512]{1,0:T(8,128)(2,1)S(1)}, u32[]{:S(2)}, u32[]{:S(2)}) %collective-permute-start.9) | collective-permute-done | bytes 131104 | tf_op jit(solution)/shard_map/ppermute | solution.py:27
  173.2 0.7 copy.8
  (7 shorter events, 0.0 us)
Async XLA Ops:
  2.4 32.9 %all-to-all-start = ((f32[32,16,128]{2,1,0:T(8,128)}), f32[32,16,128]{2,1,0:T(8,128)S(1)}, u32[]{:S(2)}, u32[]{:S(2)}) async-start(f32[32,16,128]{2,1,0:T(8,128)} %first.1), calls=%async_computation | async-start | bytes 524288 | tf_op jit(solution)/shard_map/all_to_all | solution.py:319
  18.3 19.4 %collective-permute-start.1 = (bf16[512,256]{1,0:T(8,128)(2,1)}, bf16[512,256]{1,0:T(8,128)(2,1)S(1)}, u32[]{:S(2)}, u32[]{:S(2)}) collective-permute-start(bf16[512,256]{1,0:T(8,128)(2,1)} %param.11), channel_id=1, source_target_pairs={{0,0},{1,1},{2,2},{3,3},{4,16},{5,17},{6,18},{7,19},{8,32},{9,33},... | collective-permute-start | bytes 786440 | tf_op jit(solution)/shard_map/ppermute | solution.py:27
  20.6 11.6 %collective-permute-start = (bf16[2,3,512]{2,0,1:T(2,128)(2,1)S(1)}, bf16[2,3,512]{2,0,1:T(2,128)(2,1)S(1)}, u32[]{:S(2)}, u32[]{:S(2)}) collective-permute-start(bf16[2,3,512]{2,0,1:T(2,128)(2,1)S(1)} %slice.9), channel_id=1, source_target_pairs={{0,16},{1,17},{2,18},{3,19},{4,20},{5,21},{6,22},{7,23},{8,24},{9,... | collective-permute-start | bytes 18440 | tf_op jit(solution)/shard_map/ppermute | solution.py:32
  32.2 0.6 copy-start.5
  35.4 0.7 copy-start.3
  56.7 55.3 %all-to-all-start.2 = ((bf16[8,512,256]{2,1,0:T(8,128)(2,1)}), bf16[8,512,256]{2,1,0:T(8,128)(2,1)S(1)}, u32[]{:S(2)}, u32[]{:S(2)}) async-start(bf16[8,512,256]{2,1,0:T(8,128)(2,1)} %broadcast_in_dim.10), calls=%async_computation.2 | async-start | bytes 4194304 | tf_op jit(solution)/shard_map/all_to_all | solution.py:328
  62.8 3.4 %collective-permute-start.2 = (bf16[128,512]{1,0:T(8,128)(2,1)}, bf16[128,512]{1,0:T(8,128)(2,1)S(1)}, u32[]{:S(2)}, u32[]{:S(2)}) collective-permute-start(bf16[128,512]{1,0:T(8,128)(2,1)} %back.1), channel_id=1, source_target_pairs={{4,20},{5,21},{6,22},{7,23},{12,28},{13,29},{14,30},{15,31},{16,0}... | collective-permute-start | bytes 393224 | tf_op jit(solution)/shard_map/ppermute | solution.py:27
  67.2 12.3 %collective-permute-start.3 = (bf16[256,512]{1,0:T(8,128)(2,1)S(1)}, bf16[256,512]{1,0:T(8,128)(2,1)S(1)}, u32[]{:S(2)}, u32[]{:S(2)}) collective-permute-start(bf16[256,512]{1,0:T(8,128)(2,1)S(1)} %pad_maximum_fusion.1), channel_id=1, source_target_pairs={{0,256},{1,257},{2,258},{3,259},{8,264},{9,265},{10,266},{11,267},... | collective-permute-start | bytes 786440 | tf_op jit(solution)/shard_map/ppermute | solution.py:27
  80.4 47.5 %copy-start.1 = (bf16[512,512]{1,0:T(8,128)(2,1)}, bf16[512,512]{1,0:T(8,128)(2,1)S(1)}, u32[]{:S(2)}) copy-start(bf16[512,512]{1,0:T(8,128)(2,1)S(1)} %pad_maximum_fusion.refs_0_) | copy-start | bytes 1572868
  80.4 8.0 %collective-permute-start.5 = (bf16[512,512]{1,0:T(8,128)(2,1)S(1)}, bf16[512,512]{1,0:T(8,128)(2,1)S(1)}, u32[]{:S(2)}, u32[]{:S(2)}) collective-permute-start(bf16[512,512]{1,0:T(8,128)(2,1)S(1)} %pad_maximum_fusion.refs_0_), channel_id=1, source_target_pairs={{0,12},{1,13},{2,14},{3,15},{8,4},{9,5},{10,6},{11,7},{20,16},{21,... | collective-permute-start | bytes 1572872 | tf_op jit(solution)/shard_map/ppermute | solution.py:27
  81.7 8.0 %collective-permute-start.4 = (bf16[512,512]{1,0:T(8,128)(2,1)S(1)}, bf16[512,512]{1,0:T(8,128)(2,1)}, u32[]{:S(2)}, u32[]{:S(2)}) collective-permute-start(bf16[512,512]{1,0:T(8,128)(2,1)S(1)} %pad_maximum_fusion.refs_0_), channel_id=1, source_target_pairs={{0,4},{1,5},{2,6},{3,7},{8,12},{9,13},{10,14},{11,15},{20,24},{21,... | collective-permute-start | bytes 1572872 | tf_op jit(solution)/shard_map/ppermute | solution.py:27
  88.4 39.6 %copy-start.2 = (bf16[512,512]{1,0:T(8,128)(2,1)}, bf16[512,512]{1,0:T(8,128)(2,1)S(1)}, u32[]{:S(2)}) copy-start(bf16[512,512]{1,0:T(8,128)(2,1)S(1)} %collective-permute-done.5.refs_2_) | copy-start | bytes 1572868
  112.0 15.9 %copy-start = (bf16[8,512,256]{2,1,0:T(8,128)(2,1)}, bf16[8,512,256]{2,1,0:T(8,128)(2,1)S(1)}, u32[]{:S(2)}) copy-start(bf16[8,512,256]{2,1,0:T(8,128)(2,1)S(1)} %all-to-all-done.2.refs_5_) | copy-start | bytes 6291460
  114.6 8.5 %collective-permute-start.7 = (bf16[256,512]{1,0:T(8,128)(2,1)}, bf16[256,512]{1,0:T(8,128)(2,1)S(1)}, u32[]{:S(2)}, u32[]{:S(2)}) collective-permute-start(bf16[256,512]{1,0:T(8,128)(2,1)} %slice.11), channel_id=1, source_target_pairs={{4,0},{5,1},{6,2},{7,3},{12,8},{13,9},{14,10},{15,11},{16,28},{17,... | collective-permute-start | bytes 786440 | tf_op jit(solution)/shard_map/ppermute | solution.py:27
  115.8 12.1 %collective-permute-start.6 = (bf16[256,512]{1,0:T(8,128)(2,1)}, bf16[256,512]{1,0:T(8,128)(2,1)}, u32[]{:S(2)}, u32[]{:S(2)}) collective-permute-start(bf16[256,512]{1,0:T(8,128)(2,1)} %slice.10), channel_id=1, source_target_pairs={{4,8},{5,9},{6,10},{7,11},{12,0},{13,1},{14,2},{15,3},{16,20},{17,... | collective-permute-start | bytes 786440 | tf_op jit(solution)/shard_map/ppermute | solution.py:27
  123.0 4.9 %copy-start.4 = (bf16[256,512]{1,0:T(8,128)(2,1)}, bf16[256,512]{1,0:T(8,128)(2,1)S(1)}, u32[]{:S(2)}) copy-start(bf16[256,512]{1,0:T(8,128)(2,1)S(1)} %collective-permute-done.7.refs_4_) | copy-start | bytes 786436
  134.3 4.8 %collective-permute-start.8 = (f32[4,128,512]{2,1,0:T(8,128)}, f32[4,128,512]{2,1,0:T(8,128)S(1)}, u32[]{:S(2)}, u32[]{:S(2)}) collective-permute-start(f32[4,128,512]{2,1,0:T(8,128)} %get-tuple-element.36), channel_id=1, source_target_pairs={{0,16},{1,17},{2,18},{3,19},{4,20},{5,21},{6,22},{7,23},{8,24},{9,... | collective-permute-start | bytes 3145736 | tf_op jit(solution)/shard_map/ppermute | solution.py:27
  158.6 14.6 %collective-permute-start.9 = (bf16[128,512]{1,0:T(8,128)(2,1)S(1)}, bf16[128,512]{1,0:T(8,128)(2,1)S(1)}, u32[]{:S(2)}, u32[]{:S(2)}) collective-permute-start(bf16[128,512]{1,0:T(8,128)(2,1)S(1)} %reduce_sum.12), channel_id=1, source_target_pairs={{0,0},{1,4},{2,256},{3,260},{4,1},{5,5},{6,257},{7,261},{8,2},{9,6... | collective-permute-start | bytes 393224 | tf_op jit(solution)/shard_map/ppermute | solution.py:27

commit v6 on v4

--- a/solution.py
+++ b/solution.py
@@ -153,60 +153,53 @@
             out_ref[rows, cols] = (query_ref[rows, cols] * resp[pl.ds(half * 4 + part, 64, stride=8), :]).astype(jnp.bfloat16)
 
 
-def mix_kernel(table_ref, *refs):
-    line, fwd, bwd, hf, hb, weights = refs[:6]
-    keep_ref, send_ref, g, w, g_sem, w_sem = refs[6:]
+def mix_kernel(part, table_ref, line, fwd, bwd, hf, hb, weights, out_ref, g, w, g_sem, w_sem):
     own = table_ref[0] == 1
     yl = table_ref[1]
-    low, high = table_ref[2], table_ref[3]
-
-    def from_own():
-        return [
-            pltpu.make_async_copy(line, g.at[low], g_sem.at[0]),
-            pltpu.make_async_copy(hf, g.at[high, pl.ds(0, 256)], g_sem.at[1]),
-            pltpu.make_async_copy(hb, g.at[high, pl.ds(256, 256)], g_sem.at[2]),
-        ]
-
-    def from_others():
-        return [
-            pltpu.make_async_copy(fwd, g.at[low], g_sem.at[0]),
-            pltpu.make_async_copy(bwd, g.at[high], g_sem.at[1]),
-        ]
+
+    def copies(pieces):
+        made = []
+        for far in range(2):
+            for source, rows, block in pieces[far]:
+                depth = pl.ds(pl.multiple_of(table_ref[block] * 512, 512), 512)
+                target = g.at[pl.ds(far * 128, 128), depth]
+                made.append(pltpu.make_async_copy(source.at[pl.ds(rows + part * 128, 128), :], target, g_sem.at[len(made)]))
+        return made
+
+    from_own = [[(line, 0, 2), (hf, 0, 3)], [(line, 256, 2), (hb, 0, 3)]]
+    from_others = [[(fwd, 0, 2), (bwd, 0, 3)], [(fwd, 256, 2), (bwd, 256, 3)]]
 
     @pl.when(own)
     def _():
-        for copy in from_own():
+        for copy in copies(from_own):
             copy.start()
 
     @pl.when(jnp.logical_not(own))
     def _():
-        for copy in from_others():
+        for copy in copies(from_others):
             copy.start()
 
-    loads = [pltpu.make_async_copy(weights.at[i], w.at[i], w_sem.at[i]) for i in range(8)]
+    loads = [pltpu.make_async_copy(weights.at[i], w.at[i], w_sem.at[i]) for i in range(4)]
     for copy in loads:
         copy.start()
 
     @pl.when(own)
     def _():
-        for copy in from_own():
+        for copy in copies(from_own):
             copy.wait()
 
     @pl.when(jnp.logical_not(own))
     def _():
-        for copy in from_others():
+        for copy in copies(from_others):
             copy.wait()
 
     for i in range(4):
-        loads[2 * i].wait()
-        loads[2 * i + 1].wait()
-        part = jnp.dot(g[0], w[2 * i], preferred_element_type=jnp.float32)
-        part = part + jnp.dot(g[1], w[2 * i + 1], preferred_element_type=jnp.float32)
+        loads[i].wait()
+        total = jnp.dot(g[...], w[i], preferred_element_type=jnp.float32)
         cols = slice(i % 2 * 256, i % 2 * 256 + 256)
         for far in range(2):
             d = lax.rem(far * 2 + i // 2 - yl + 4, 4)
-            keep_ref[d, :, cols] = part[far * 256 : far * 256 + 128]
-            send_ref[d, :, cols] = part[far * 256 + 128 : far * 256 + 256]
+            out_ref[d, :, cols] = total[far * 128 : far * 128 + 128]
 
 
 TINY = pl.CostEstimate(flops=1, bytes_accessed=1, transcendentals=0)
@@ -264,22 +257,21 @@
     )(query, drive, half, incoming, rate, gain, skip)
 
 
-def mix(table, *operands):
-    out = jax.ShapeDtypeStruct((4, 128, 512), jnp.float32)
-    return pl.pallas_call(
-        mix_kernel,
-        out_shape=(out, out),
+def mix(part, table, *operands):
+    return pl.pallas_call(
+        functools.partial(mix_kernel, part),
+        out_shape=jax.ShapeDtypeStruct((4, 128, 512), jnp.float32),
         in_specs=[SMEM] + [pl.BlockSpec(memory_space=pl.ANY)] * len(operands),
-        out_specs=(VMEM, VMEM),
+        out_specs=VMEM,
         scratch_shapes=[
-            pltpu.VMEM((2, 512, 512), jnp.bfloat16),
-            pltpu.VMEM((8, 512, 256), jnp.bfloat16),
-            pltpu.SemaphoreType.DMA((3,)),
-            pltpu.SemaphoreType.DMA((8,)),
+            pltpu.VMEM((256, 1024), jnp.bfloat16),
+            pltpu.VMEM((4, 1024, 256), jnp.bfloat16),
+            pltpu.SemaphoreType.DMA((4,)),
+            pltpu.SemaphoreType.DMA((4,)),
         ],
         compiler_params=pltpu.CompilerParams(vmem_limit_bytes=60 * 1024 * 1024),
-        cost_estimate=pl.CostEstimate(flops=1_100_000_000, bytes_accessed=7_000_000, transcendentals=0),
-        name="mix",
+        cost_estimate=pl.CostEstimate(flops=600_000_000, bytes_accessed=4_000_000, transcendentals=0),
+        name=("keep", "send")[part],
     )(table, *operands)
 
 
@@ -321,9 +313,10 @@
     ends = lax.all_to_all(ends, "ctx", 0, 0, tiled=True)
     ctx = index // 16
     rate = lax.dynamic_slice(decay_rate, (ctx // 4 * 2, ctx % 4 * 128), (2, 128))
-    ends, weight, halo, rate = tie((ends, weight, halo, rate))
+    ends, rate = tie((ends, rate))
+    carried, weight, halo = tie((carry(ends, rate), weight, halo))
     weights = lax.all_gather(weight, "ctx", axis_index_groups=along_z)
-    incoming = lax.all_to_all(carry(ends, rate), "ctx", 0, 0, tiled=True).reshape(64, 128)
+    incoming = lax.all_to_all(carried, "ctx", 0, 0, tiled=True).reshape(64, 128)
 
     query, drive, half = middle(feat, halo.transpose(1, 0, 2), short_filter, decay_rate)
     gain = residue * jnp.sqrt(-jnp.expm1(-2.0 * decay_rate))
@@ -342,9 +335,11 @@
     low = jnp.where(own, x // 2, (x + 3) % 4 // 2)
     high = jnp.where(own, 1 - x // 2, (x + 1) % 4 // 2)
     table = jnp.stack([own.astype(jnp.int32), yl, low, high]).astype(jnp.int32)
-    keep, send = mix(table, line, fwd, bwd, hf, hb, weights)
-
-    blocks = keep + other_core(send)
+    operands = (table, line, fwd, bwd, hf, hb, weights.reshape(4, 1024, 256))
+    sent = other_core(mix(1, *operands))
+    keep = mix(0, *operands)
+
+    blocks = keep + sent
     parts = [move(blocks[d].astype(jnp.bfloat16), axes, along("yl", d)) for d in range(1, 4)]
     total = blocks[0] + sum(part.astype(jnp.float32) for part in parts)
     return move(

time: 160 us -> 159 us (level)
  waiting for transfers between devices: 50.1 us -> 45.1 us
  Pallas kernels: 15.6 us -> 18.6 us
    ppermute x1, waiting for transfers between devices: 5.49 us -> 0.59 us  [from_behind(): return lax.ppermute(value, axes, pairs)]
    pallas_call x1 -> x2, Pallas kernels: 6.4 us -> 9.39 us  [mix(): pl.pallas_call(functools.partial(mix_kernel, part), out_shape=jax.ShapeDt...]
    ppermute x12, waiting for transfers between devices: 41.4 us -> 38.8 us  [move(): return lax.ppermute(value, axes, pairs)]
    all_to_all x1, waiting for transfers between devices: 0.01 us -> 2.52 us  [body(): ends = lax.all_to_all(ends, 'ctx', 0, 0, tiled=True)]
  transfers between devices with their start and end apart: 16 -> 16, of which waited for: 11 -> 11; matrix products, arithmetic and copies ran while one was open for 4% -> 4% of each run, Pallas kernels for 4% -> 7%
where the time goes in v6:
time: 159 us; the launch traced here: 157 us
  starting transfers between devices  68.7 us (43%)
  waiting for transfers between devices  45.1 us (28%)
  Pallas kernels  18.6 us (12%)
  between operations  13.8 us (9%)
  local copies, waits for them, and re-layouts  5.51 us (3%)
  other arithmetic  5.49 us (3%)
    ppermute x12, waiting for transfers between devices, move(): return lax.ppermute(value, axes, pairs)  38.8 us
    ppermute x12, starting transfers between devices, move(): return lax.ppermute(value, axes, pairs)  34 us
    all_to_all x1, starting transfers between devices, body(): ends = lax.all_to_all(ends, 'ctx', 0, 0, tiled=True)  15.8 us
    all_to_all x1, starting transfers between devices, body(): incoming = lax.all_to_all(carried, 'ctx', 0, 0, tiled=True).reshape(64, 128)  14 us
    pallas_call x2, Pallas kernels, mix(): pl.pallas_call(functools.partial(mix_kernel, part), out_shape=jax.ShapeDt...  9.39 us
    ppermute x1, starting transfers between devices, from_behind(): return lax.ppermute(value, axes, pairs)  4.71 us
    unnamed x19, local copies, waits for them, and re-layouts  3.36 us
  transfers between devices with their start and end apart: 16, of which 11 were waited for; matrix products, arithmetic and copies ran while one was open for 4% of the time, Pallas kernels for 7%

profile of v6, /device:TPU:56, one launch (start us, length us, event | category | flops | bytes accessed | tf_op | source)
XLA Modules:
  0.0 157.2 jit_solution(2642572246327944606)
XLA Ops:
  6.5 2.4 %first.1 = f32[32,16,128]{2,1,0:T(8,128)} custom-call(bf16[3,128,512]{2,1,0:T(8,128)(2,1)} %bitcast.23, f32[3,3,512]{2,1,0:T(4,128)} %taps_ref.3, f32[16,512]{1,0:T(8,128)} %rate_ref.5), custom_call_target="tpu_custom_call" | custom-call | flops 1 | bytes 1 | tf_op jit(solution)/shard_map/first/pallas_call | solution.py:210
  9.0 15.8 %all-to-all-start = ((f32[32,16,128]{2,1,0:T(8,128)}), f32[32,16,128]{2,1,0:T(8,128)S(1)}, u32[]{:S(2)}, u32[]{:S(2)}) async-start(f32[32,16,128]{2,1,0:T(8,128)} %first.1), calls=%async_computation | async-start | bytes 524288 | tf_op jit(solution)/shard_map/all_to_all | solution.py:313
  24.8 0.0 all-gather.3.cloned.1.call-start
  24.9 1.6 %collective-permute-start = (bf16[512,256]{1,0:T(8,128)(2,1)}, bf16[512,256]{1,0:T(8,128)(2,1)S(1)}, u32[]{:S(2)}, u32[]{:S(2)}) collective-permute-start(bf16[512,256]{1,0:T(8,128)(2,1)} %param.11), channel_id=1, source_target_pairs={{0,0},{1,1},{2,2},{3,3},{4,16},{5,17},{6,18},{7,19},{8,32},{9,33},... | collective-permute-start | bytes 786440 | tf_op jit(solution)/shard_map/ppermute | solution.py:27
  26.5 0.7 slice.24
  27.2 4.7 %collective-permute-start.1 = (bf16[2,3,512]{2,0,1:T(2,128)(2,1)S(1)}, bf16[2,3,512]{2,0,1:T(2,128)(2,1)S(1)}, u32[]{:S(2)}, u32[]{:S(2)}) collective-permute-start(bf16[2,3,512]{2,0,1:T(2,128)(2,1)S(1)} %slice.24), channel_id=1, source_target_pairs={{0,16},{1,17},{2,18},{3,19},{4,20},{5,21},{6,22},{7,23},{8,24},{9,... | collective-permute-start | bytes 18440 | tf_op jit(solution)/shard_map/ppermute | solution.py:32
  32.0 1.3 dynamic_slice.3.rate_ref
  33.3 2.5 %all-to-all-done.ends_ref = f32[32,16,128]{2,1,0:T(8,128)S(1)} async-done(((f32[32,16,128]{2,1,0:T(8,128)}), f32[32,16,128]{2,1,0:T(8,128)S(1)}, u32[]{:S(2)}, u32[]{:S(2)}) %all-to-all-start) | async-done | bytes 262176 | tf_op jit(solution)/shard_map/all_to_all | solution.py:313
  35.9 0.7 copy-done.3
  36.6 1.6 %carry.1 = f32[32,2,128]{2,1,0:T(2,128)} custom-call(f32[32,16,128]{2,1,0:T(8,128)} %copy-done.3, f32[2,128]{1,0:T(2,128)} %dynamic_slice.3.rate_ref), custom_call_target="tpu_custom_call" | custom-call | flops 1 | bytes 1 | tf_op jit(solution)/shard_map/carry/pallas_call | solution.py:222
  38.2 0.6 collective-permute-done.1
  38.8 0.7 copy-done.6
  39.5 0.0 all-gather.3.cloned.1.call-update
  39.5 14.0 %all-to-all-start.1 = ((f32[32,2,128]{2,1,0:T(2,128)}), f32[32,2,128]{2,1,0:T(2,128)S(1)}, u32[]{:S(2)}, u32[]{:S(2)}) async-start(f32[32,2,128]{2,1,0:T(2,128)} %carry.1), calls=%async_computation.1 | async-start | bytes 65536 | tf_op jit(solution)/shard_map/all_to_all | solution.py:319
  53.6 1.4 sqrt_multiply_fusion.gain_ref
  55.0 2.6 %middle.1 = (f32[128,512]{1,0:T(8,128)}, f32[512,128]{1,0:T(8,128)}, f32[128,128]{1,0:T(8,128)}) custom-call(bf16[3,128,512]{2,1,0:T(8,128)(2,1)} %bitcast.24, bf16[3,2,512]{2,1,0:T(2,128)(2,1)} %bitcast.26, f32[3,3,512]{2,1,0:T(4,128)} %taps_ref.3, f32[16,512]{1,0:T(8,128)} %rate_ref.5), custom_call_target="tpu_custom_call" | custom-call | flops 1 | bytes 1 | tf_op jit(solution)/shard_map/middle/pallas_call | solution.py:233
  57.6 3.1 %all-to-all-done.1 = f32[32,2,128]{2,1,0:T(2,128)S(1)} async-done(((f32[32,2,128]{2,1,0:T(2,128)}), f32[32,2,128]{2,1,0:T(2,128)S(1)}, u32[]{:S(2)}, u32[]{:S(2)}) %all-to-all-start.1) | async-done | bytes 32800 | tf_op jit(solution)/shard_map/all_to_all | solution.py:319
  60.8 0.6 copy-done.7
  61.4 2.5 %back.1 = bf16[128,512]{1,0:T(8,128)(2,1)} custom-call(f32[128,512]{1,0:T(8,128)} %get-tuple-element.16.query_ref, f32[512,128]{1,0:T(8,128)} %get-tuple-element.17.drive_ref, f32[128,128]{1,0:T(8,128)} %get-tuple-element.18.half_ref, f32[64,128]{1,0:T(8,128)} %bitcast.25, f32[16,512]{1,0:T(8,128)} %rate_ref.5, f32[16,512]{1,0:T(8,128)} %sqrt_multiply_fusion.gain_ref, ...), custom_call_target="tpu_custom_call" | custom-call | flops 1 | bytes 1 | tf_op jit(solution)/shard_map/back/pallas_call | solution.py:249
  63.9 1.3 collective-permute-start.2
  65.2 2.2 %collective-permute-done.2 = bf16[128,512]{1,0:T(8,128)(2,1)S(1)} collective-permute-done((bf16[128,512]{1,0:T(8,128)(2,1)}, bf16[128,512]{1,0:T(8,128)(2,1)S(1)}, u32[]{:S(2)}, u32[]{:S(2)}) %collective-permute-start.2) | collective-permute-done | bytes 131104 | tf_op jit(solution)/shard_map/ppermute | solution.py:27
  67.3 0.9 pad_maximum_fusion.1
  68.3 7.3 %collective-permute-start.3 = (bf16[256,512]{1,0:T(8,128)(2,1)S(1)}, bf16[256,512]{1,0:T(8,128)(2,1)S(1)}, u32[]{:S(2)}, u32[]{:S(2)}) collective-permute-start(bf16[256,512]{1,0:T(8,128)(2,1)S(1)} %pad_maximum_fusion.1), channel_id=1, source_target_pairs={{0,256},{1,257},{2,258},{3,259},{8,264},{9,265},{10,266},{11,267},... | collective-permute-start | bytes 786440 | tf_op jit(solution)/shard_map/ppermute | solution.py:27
  75.6 5.0 %collective-permute-done.3 = bf16[256,512]{1,0:T(8,128)(2,1)S(1)} collective-permute-done((bf16[256,512]{1,0:T(8,128)(2,1)S(1)}, bf16[256,512]{1,0:T(8,128)(2,1)S(1)}, u32[]{:S(2)}, u32[]{:S(2)}) %collective-permute-start.3) | collective-permute-done | bytes 262176 | tf_op jit(solution)/shard_map/ppermute | solution.py:27
  80.5 0.9 pad_maximum_fusion.line
  81.5 1.3 collective-permute-start.5
  82.8 1.3 collective-permute-start.4
  84.2 5.3 %collective-permute-done.5.bwd = bf16[512,512]{1,0:T(8,128)(2,1)S(1)} collective-permute-done((bf16[512,512]{1,0:T(8,128)(2,1)S(1)}, bf16[512,512]{1,0:T(8,128)(2,1)S(1)}, u32[]{:S(2)}, u32[]{:S(2)}) %collective-permute-start.5) | collective-permute-done | bytes 524320 | tf_op jit(solution)/shard_map/ppermute | solution.py:27
  89.5 1.3 collective-permute-start.7
  90.8 0.0 collective-permute-done.4.fwd
  90.8 1.3 collective-permute-start.6
  92.3 0.7 pad_add_fusion.table_ref
  93.0 5.2 %collective-permute-done.7.hb = bf16[256,512]{1,0:T(8,128)(2,1)S(1)} collective-permute-done((bf16[256,512]{1,0:T(8,128)(2,1)S(1)}, bf16[256,512]{1,0:T(8,128)(2,1)S(1)}, u32[]{:S(2)}, u32[]{:S(2)}) %collective-permute-start.7) | collective-permute-done | bytes 262176 | tf_op jit(solution)/shard_map/ppermute | solution.py:27
  98.2 2.1 %collective-permute-done.6.hf = bf16[256,512]{1,0:T(8,128)(2,1)S(1)} collective-permute-done((bf16[256,512]{1,0:T(8,128)(2,1)S(1)}, bf16[256,512]{1,0:T(8,128)(2,1)S(1)}, u32[]{:S(2)}, u32[]{:S(2)}) %collective-permute-start.6) | collective-permute-done | bytes 262176 | tf_op jit(solution)/shard_map/ppermute | solution.py:27
  100.4 0.7 copy-done.5
  101.0 4.7 %send.1 = f32[4,128,512]{2,1,0:T(8,128)} custom-call(s32[4]{0:T(128)} %pad_add_fusion.table_ref, bf16[512,512]{1,0:T(8,128)(2,1)} %copy-done, bf16[512,512]{1,0:T(8,128)(2,1)} %copy-done.2, bf16[512,512]{1,0:T(8,128)(2,1)} %copy-done.1, bf16[256,512]{1,0:T(8,128)(2,1)} %copy-done.5, bf16[256,512]{1,0:T(8,128)(2,1)} %copy-done.4, bf16[4,1024,256]{2,1,0:T(8,128)(2,1)} %bitcast.21), custom_call_target="tpu_custom_call" | custom-call | flops 600000000 | bytes 4000000 | tf_op jit(solution)/shard_map/send/pallas_call | solution.py:261
  105.7 1.9 %collective-permute-start.8 = (f32[4,128,512]{2,1,0:T(8,128)}, f32[4,128,512]{2,1,0:T(8,128)S(1)}, u32[]{:S(2)}, u32[]{:S(2)}) collective-permute-start(f32[4,128,512]{2,1,0:T(8,128)} %send.1), channel_id=1, source_target_pairs={{0,16},{1,17},{2,18},{3,19},{4,20},{5,21},{6,22},{7,23},{8,24},{9,... | collective-permute-start | bytes 3145736 | tf_op jit(solution)/shard_map/ppermute | solution.py:27
  107.6 4.7 %keep.1 = f32[4,128,512]{2,1,0:T(8,128)} custom-call(s32[4]{0:T(128)} %pad_add_fusion.table_ref, bf16[512,512]{1,0:T(8,128)(2,1)} %copy-done, bf16[512,512]{1,0:T(8,128)(2,1)} %copy-done.2, bf16[512,512]{1,0:T(8,128)(2,1)} %copy-done.1, bf16[256,512]{1,0:T(8,128)(2,1)} %copy-done.5, bf16[256,512]{1,0:T(8,128)(2,1)} %copy-done.4, bf16[4,1024,256]{2,1,0:T(8,128)(2,1)} %bitcast.22), custom_call_target="tpu_custom_call" | custom-call | flops 600000000 | bytes 4000000 | tf_op jit(solution)/shard_map/keep/pallas_call | solution.py:261
  112.4 1.5 fusion.2
  113.9 4.8 %collective-permute-start.9 = (bf16[128,512]{1,0:T(8,128)(2,1)S(1)}, bf16[128,512]{1,0:T(8,128)(2,1)S(1)}, u32[]{:S(2)}, u32[]{:S(2)}) collective-permute-start(bf16[128,512]{1,0:T(8,128)(2,1)S(1)} %get-tuple-element.23), channel_id=1, source_target_pairs={{0,1},{1,2},{2,3},{3,0},{4,5},{5,6},{6,7},{7,4},{8,9},{9,10},{10,1... | collective-permute-start | bytes 393224 | tf_op jit(solution)/shard_map/ppermute | solution.py:27
  118.7 3.0 %collective-permute-start.11 = (bf16[128,512]{1,0:T(8,128)(2,1)S(1)}, bf16[128,512]{1,0:T(8,128)(2,1)S(1)}, u32[]{:S(2)}, u32[]{:S(2)}) collective-permute-start(bf16[128,512]{1,0:T(8,128)(2,1)S(1)} %get-tuple-element.24), channel_id=1, source_target_pairs={{0,3},{1,0},{2,1},{3,2},{4,7},{5,4},{6,5},{7,6},{8,11},{9,8},{10,9... | collective-permute-start | bytes 393224 | tf_op jit(solution)/shard_map/ppermute | solution.py:27
  121.7 4.8 %collective-permute-start.10 = (bf16[128,512]{1,0:T(8,128)(2,1)S(1)}, bf16[128,512]{1,0:T(8,128)(2,1)S(1)}, u32[]{:S(2)}, u32[]{:S(2)}) collective-permute-start(bf16[128,512]{1,0:T(8,128)(2,1)S(1)} %get-tuple-element.25), channel_id=1, source_target_pairs={{0,2},{1,3},{2,0},{3,1},{4,6},{5,7},{6,4},{7,5},{8,10},{9,11},{10,... | collective-permute-start | bytes 393224 | tf_op jit(solution)/shard_map/ppermute | solution.py:27
  126.5 2.8 %collective-permute-done.11 = bf16[128,512]{1,0:T(8,128)(2,1)S(1)} collective-permute-done((bf16[128,512]{1,0:T(8,128)(2,1)S(1)}, bf16[128,512]{1,0:T(8,128)(2,1)S(1)}, u32[]{:S(2)}, u32[]{:S(2)}) %collective-permute-start.11) | collective-permute-done | bytes 131104 | tf_op jit(solution)/shard_map/ppermute | solution.py:27
  129.3 5.3 %collective-permute-done.10 = bf16[128,512]{1,0:T(8,128)(2,1)S(1)} collective-permute-done((bf16[128,512]{1,0:T(8,128)(2,1)S(1)}, bf16[128,512]{1,0:T(8,128)(2,1)S(1)}, u32[]{:S(2)}, u32[]{:S(2)}) %collective-permute-start.10) | collective-permute-done | bytes 131104 | tf_op jit(solution)/shard_map/ppermute | solution.py:27
  134.6 0.1 fusion.1
  134.7 4.1 %collective-permute-start.12 = (bf16[128,512]{1,0:T(8,128)(2,1)S(1)}, bf16[128,512]{1,0:T(8,128)(2,1)S(1)}, u32[]{:S(2)}, u32[]{:S(2)}) collective-permute-start(bf16[128,512]{1,0:T(8,128)(2,1)S(1)} %fusion.1), channel_id=1, source_target_pairs={{0,0},{1,4},{2,256},{3,260},{4,1},{5,5},{6,257},{7,261},{8,2},{9,6... | collective-permute-start | bytes 393224 | tf_op jit(solution)/shard_map/ppermute | solution.py:27
  138.8 10.9 %collective-permute-done.12 = bf16[128,512]{1,0:T(8,128)(2,1)S(1)} collective-permute-done((bf16[128,512]{1,0:T(8,128)(2,1)S(1)}, bf16[128,512]{1,0:T(8,128)(2,1)S(1)}, u32[]{:S(2)}, u32[]{:S(2)}) %collective-permute-start.12) | collective-permute-done | bytes 131104 | tf_op jit(solution)/shard_map/ppermute | solution.py:27
  149.7 0.7 copy.8
  (21 shorter events, 0.1 us)
Async XLA Ops:
  9.0 26.9 %all-to-all-start = ((f32[32,16,128]{2,1,0:T(8,128)}), f32[32,16,128]{2,1,0:T(8,128)S(1)}, u32[]{:S(2)}, u32[]{:S(2)}) async-start(f32[32,16,128]{2,1,0:T(8,128)} %first.1), calls=%async_computation | async-start | bytes 524288 | tf_op jit(solution)/shard_map/all_to_all | solution.py:313
  24.8 75.5 %all-gather.3.cloned.1.call-start = ((), (), s32[]{:S(2)}) async-start(), calls=%async_computation.2 | async-start | bytes 2359296 | tf_op jit(solution)/shard_map/all_gather | solution.py:318
  24.9 13.9 %collective-permute-start = (bf16[512,256]{1,0:T(8,128)(2,1)}, bf16[512,256]{1,0:T(8,128)(2,1)S(1)}, u32[]{:S(2)}, u32[]{:S(2)}) collective-permute-start(bf16[512,256]{1,0:T(8,128)(2,1)} %param.11), channel_id=1, source_target_pairs={{0,0},{1,1},{2,2},{3,3},{4,16},{5,17},{6,18},{7,19},{8,32},{9,33},... | collective-permute-start | bytes 786440 | tf_op jit(solution)/shard_map/ppermute | solution.py:27
  27.2 11.6 %collective-permute-start.1 = (bf16[2,3,512]{2,0,1:T(2,128)(2,1)S(1)}, bf16[2,3,512]{2,0,1:T(2,128)(2,1)S(1)}, u32[]{:S(2)}, u32[]{:S(2)}) collective-permute-start(bf16[2,3,512]{2,0,1:T(2,128)(2,1)S(1)} %slice.24), channel_id=1, source_target_pairs={{0,16},{1,17},{2,18},{3,19},{4,20},{5,21},{6,22},{7,23},{8,24},{9,... | collective-permute-start | bytes 18440 | tf_op jit(solution)/shard_map/ppermute | solution.py:32
  35.9 0.7 copy-start.3
  38.8 16.2 %copy-start.8 = (bf16[2,3,512]{2,0,1:T(2,128)(2,1)}, bf16[2,3,512]{2,0,1:T(2,128)(2,1)S(1)}, u32[]{:S(2)}) copy-start(bf16[2,3,512]{2,0,1:T(2,128)(2,1)S(1)} %collective-permute-done.1) | copy-start | bytes 18436
  38.8 0.7 copy-start.6
  39.5 21.2 %all-to-all-start.1 = ((f32[32,2,128]{2,1,0:T(2,128)}), f32[32,2,128]{2,1,0:T(2,128)S(1)}, u32[]{:S(2)}, u32[]{:S(2)}) async-start(f32[32,2,128]{2,1,0:T(2,128)} %carry.1), calls=%async_computation.1 | async-start | bytes 65536 | tf_op jit(solution)/shard_map/all_to_all | solution.py:319
  60.8 0.6 copy-start.7
  63.9 3.4 %collective-permute-start.2 = (bf16[128,512]{1,0:T(8,128)(2,1)}, bf16[128,512]{1,0:T(8,128)(2,1)S(1)}, u32[]{:S(2)}, u32[]{:S(2)}) collective-permute-start(bf16[128,512]{1,0:T(8,128)(2,1)} %back.1), channel_id=1, source_target_pairs={{4,20},{5,21},{6,22},{7,23},{12,28},{13,29},{14,30},{15,31},{16,0}... | collective-permute-start | bytes 393224 | tf_op jit(solution)/shard_map/ppermute | solution.py:27
  68.3 12.3 %collective-permute-start.3 = (bf16[256,512]{1,0:T(8,128)(2,1)S(1)}, bf16[256,512]{1,0:T(8,128)(2,1)S(1)}, u32[]{:S(2)}, u32[]{:S(2)}) collective-permute-start(bf16[256,512]{1,0:T(8,128)(2,1)S(1)} %pad_maximum_fusion.1), channel_id=1, source_target_pairs={{0,256},{1,257},{2,258},{3,259},{8,264},{9,265},{10,266},{11,267},... | collective-permute-start | bytes 786440 | tf_op jit(solution)/shard_map/ppermute | solution.py:27
  81.5 18.8 %copy-start = (bf16[512,512]{1,0:T(8,128)(2,1)}, bf16[512,512]{1,0:T(8,128)(2,1)S(1)}, u32[]{:S(2)}) copy-start(bf16[512,512]{1,0:T(8,128)(2,1)S(1)} %pad_maximum_fusion.line) | copy-start | bytes 1572868
  81.5 8.0 %collective-permute-start.5 = (bf16[512,512]{1,0:T(8,128)(2,1)S(1)}, bf16[512,512]{1,0:T(8,128)(2,1)S(1)}, u32[]{:S(2)}, u32[]{:S(2)}) collective-permute-start(bf16[512,512]{1,0:T(8,128)(2,1)S(1)} %pad_maximum_fusion.line), channel_id=1, source_target_pairs={{0,12},{1,13},{2,14},{3,15},{8,4},{9,5},{10,6},{11,7},{20,16},{21,... | collective-permute-start | bytes 1572872 | tf_op jit(solution)/shard_map/ppermute | solution.py:27
  82.8 8.0 %collective-permute-start.4 = (bf16[512,512]{1,0:T(8,128)(2,1)S(1)}, bf16[512,512]{1,0:T(8,128)(2,1)S(1)}, u32[]{:S(2)}, u32[]{:S(2)}) collective-permute-start(bf16[512,512]{1,0:T(8,128)(2,1)S(1)} %pad_maximum_fusion.line), channel_id=1, source_target_pairs={{0,4},{1,5},{2,6},{3,7},{8,12},{9,13},{10,14},{11,15},{20,24},{21,... | collective-permute-start | bytes 1572872 | tf_op jit(solution)/shard_map/ppermute | solution.py:27
  89.5 10.9 %copy-start.1 = (bf16[512,512]{1,0:T(8,128)(2,1)}, bf16[512,512]{1,0:T(8,128)(2,1)S(1)}, u32[]{:S(2)}) copy-start(bf16[512,512]{1,0:T(8,128)(2,1)S(1)} %collective-permute-done.5.bwd) | copy-start | bytes 1572868
  89.5 8.7 %collective-permute-start.7 = (bf16[256,512]{1,0:T(8,128)(2,1)S(1)}, bf16[256,512]{1,0:T(8,128)(2,1)S(1)}, u32[]{:S(2)}, u32[]{:S(2)}) collective-permute-start(bf16[256,512]{1,0:T(8,128)(2,1)S(1)} %slice.32), channel_id=1, source_target_pairs={{4,0},{5,1},{6,2},{7,3},{12,8},{13,9},{14,10},{15,11},{16,28},{17,... | collective-permute-start | bytes 786440 | tf_op jit(solution)/shard_map/ppermute | solution.py:27
  90.8 9.5 %copy-start.2 = (bf16[512,512]{1,0:T(8,128)(2,1)}, bf16[512,512]{1,0:T(8,128)(2,1)S(1)}, u32[]{:S(2)}) copy-start(bf16[512,512]{1,0:T(8,128)(2,1)S(1)} %collective-permute-done.4.fwd) | copy-start | bytes 1572868
  90.8 9.5 %collective-permute-start.6 = (bf16[256,512]{1,0:T(8,128)(2,1)S(1)}, bf16[256,512]{1,0:T(8,128)(2,1)S(1)}, u32[]{:S(2)}, u32[]{:S(2)}) collective-permute-start(bf16[256,512]{1,0:T(8,128)(2,1)S(1)} %slice.31), channel_id=1, source_target_pairs={{4,8},{5,9},{6,10},{7,11},{12,0},{13,1},{14,2},{15,3},{16,20},{17,... | collective-permute-start | bytes 786440 | tf_op jit(solution)/shard_map/ppermute | solution.py:27
  98.2 2.2 %copy-start.4 = (bf16[256,512]{1,0:T(8,128)(2,1)}, bf16[256,512]{1,0:T(8,128)(2,1)S(1)}, u32[]{:S(2)}) copy-start(bf16[256,512]{1,0:T(8,128)(2,1)S(1)} %collective-permute-done.7.hb) | copy-start | bytes 786436
  100.3 0.7 copy-start.5
  105.7 6.7 %collective-permute-start.8 = (f32[4,128,512]{2,1,0:T(8,128)}, f32[4,128,512]{2,1,0:T(8,128)S(1)}, u32[]{:S(2)}, u32[]{:S(2)}) collective-permute-start(f32[4,128,512]{2,1,0:T(8,128)} %send.1), channel_id=1, source_target_pairs={{0,16},{1,17},{2,18},{3,19},{4,20},{5,21},{6,22},{7,23},{8,24},{9,... | collective-permute-start | bytes 3145736 | tf_op jit(solution)/shard_map/ppermute | solution.py:27
  113.9 12.6 %collective-permute-start.9 = (bf16[128,512]{1,0:T(8,128)(2,1)S(1)}, bf16[128,512]{1,0:T(8,128)(2,1)S(1)}, u32[]{:S(2)}, u32[]{:S(2)}) collective-permute-start(bf16[128,512]{1,0:T(8,128)(2,1)S(1)} %get-tuple-element.23), channel_id=1, source_target_pairs={{0,1},{1,2},{2,3},{3,0},{4,5},{5,6},{6,7},{7,4},{8,9},{9,10},{10,1... | collective-permute-start | bytes 393224 | tf_op jit(solution)/shard_map/ppermute | solution.py:27
  118.7 10.6 %collective-permute-start.11 = (bf16[128,512]{1,0:T(8,128)(2,1)S(1)}, bf16[128,512]{1,0:T(8,128)(2,1)S(1)}, u32[]{:S(2)}, u32[]{:S(2)}) collective-permute-start(bf16[128,512]{1,0:T(8,128)(2,1)S(1)} %get-tuple-element.24), channel_id=1, source_target_pairs={{0,3},{1,0},{2,1},{3,2},{4,7},{5,4},{6,5},{7,6},{8,11},{9,8},{10,9... | collective-permute-start | bytes 393224 | tf_op jit(solution)/shard_map/ppermute | solution.py:27
  121.7 12.9 %collective-permute-start.10 = (bf16[128,512]{1,0:T(8,128)(2,1)S(1)}, bf16[128,512]{1,0:T(8,128)(2,1)S(1)}, u32[]{:S(2)}, u32[]{:S(2)}) collective-permute-start(bf16[128,512]{1,0:T(8,128)(2,1)S(1)} %get-tuple-element.25), channel_id=1, source_target_pairs={{0,2},{1,3},{2,0},{3,1},{4,6},{5,7},{6,4},{7,5},{8,10},{9,11},{10,... | collective-permute-start | bytes 393224 | tf_op jit(solution)/shard_map/ppermute | solution.py:27
  134.7 15.1 %collective-permute-start.12 = (bf16[128,512]{1,0:T(8,128)(2,1)S(1)}, bf16[128,512]{1,0:T(8,128)(2,1)S(1)}, u32[]{:S(2)}, u32[]{:S(2)}) collective-permute-start(bf16[128,512]{1,0:T(8,128)(2,1)S(1)} %fusion.1), channel_id=1, source_target_pairs={{0,0},{1,4},{2,256},{3,260},{4,1},{5,5},{6,257},{7,261},{8,2},{9,6... | collective-permute-start | bytes 393224 | tf_op jit(solution)/shard_map/ppermute | solution.py:27
Sparse Core Ops, SparseCore 0:
  39.6 46.5 all-gather.2

commit v7 on v6

--- a/solution.py
+++ b/solution.py
@@ -153,9 +153,9 @@
             out_ref[rows, cols] = (query_ref[rows, cols] * resp[pl.ds(half * 4 + part, 64, stride=8), :]).astype(jnp.bfloat16)
 
 
-def mix_kernel(part, table_ref, line, fwd, bwd, hf, hb, weights, out_ref, g, w, g_sem, w_sem):
+def mix_kernel(part, table_ref, line, fwd, bwd, hf, hb, weights, out_ref, g, g_sem):
     own = table_ref[0] == 1
-    yl = table_ref[1]
+    yl, x = table_ref[1], table_ref[4]
 
     def copies(pieces):
         made = []
@@ -179,10 +179,6 @@
         for copy in copies(from_others):
             copy.start()
 
-    loads = [pltpu.make_async_copy(weights.at[i], w.at[i], w_sem.at[i]) for i in range(4)]
-    for copy in loads:
-        copy.start()
-
     @pl.when(own)
     def _():
         for copy in copies(from_own):
@@ -194,11 +190,10 @@
             copy.wait()
 
     for i in range(4):
-        loads[i].wait()
-        total = jnp.dot(g[...], w[i], preferred_element_type=jnp.float32)
+        total = jnp.dot(g[...], weights[i], preferred_element_type=jnp.float32)
         cols = slice(i % 2 * 256, i % 2 * 256 + 256)
         for far in range(2):
-            d = lax.rem(far * 2 + i // 2 - yl + 4, 4)
+            d = lax.rem(lax.bitwise_xor(far * 2 + i // 2, x) - yl + 4, 4)
             out_ref[d, :, cols] = total[far * 128 : far * 128 + 128]
 
 
@@ -261,15 +256,13 @@
     return pl.pallas_call(
         functools.partial(mix_kernel, part),
         out_shape=jax.ShapeDtypeStruct((4, 128, 512), jnp.float32),
-        in_specs=[SMEM] + [pl.BlockSpec(memory_space=pl.ANY)] * len(operands),
+        in_specs=[SMEM] + [pl.BlockSpec(memory_space=pl.ANY)] * 5 + [VMEM],
         out_specs=VMEM,
         scratch_shapes=[
             pltpu.VMEM((256, 1024), jnp.bfloat16),
-            pltpu.VMEM((4, 1024, 256), jnp.bfloat16),
-            pltpu.SemaphoreType.DMA((4,)),
             pltpu.SemaphoreType.DMA((4,)),
         ],
-        compiler_params=pltpu.CompilerParams(vmem_limit_bytes=60 * 1024 * 1024),
+        compiler_params=pltpu.CompilerParams(vmem_limit_bytes=8 * 1024 * 1024),
         cost_estimate=pl.CostEstimate(flops=600_000_000, bytes_accessed=4_000_000, transcendentals=0),
         name=("keep", "send")[part],
     )(table, *operands)
@@ -334,7 +327,7 @@
     own = x % 2 == core
     low = jnp.where(own, x // 2, (x + 3) % 4 // 2)
     high = jnp.where(own, 1 - x // 2, (x + 1) % 4 // 2)
-    table = jnp.stack([own.astype(jnp.int32), yl, low, high]).astype(jnp.int32)
+    table = jnp.stack([own.astype(jnp.int32), yl, low, high, x]).astype(jnp.int32)
     operands = (table, line, fwd, bwd, hf, hb, weights.reshape(4, 1024, 256))
     sent = other_core(mix(1, *operands))
     keep = mix(0, *operands)
@@ -342,9 +335,12 @@
     blocks = keep + sent
     parts = [move(blocks[d].astype(jnp.bfloat16), axes, along("yl", d)) for d in range(1, 4)]
     total = blocks[0] + sum(part.astype(jnp.float32) for part in parts)
-    return move(
-        total.astype(jnp.bfloat16), axes, lambda yh, z, core, x, yl: (yh ^ (yl // 2), z, core, yh * 2 + yl % 2, x)
-    )
+
+    def home(yh, z, core, x, yl):
+        block = yl ^ x
+        return yh ^ (block // 2), z, core, yh * 2 + block % 2, x
+
+    return move(total.astype(jnp.bfloat16), axes, home)
 
 
 def shards(*arguments):

time: 159 us -> 150 us (0.943)
  the two profiles are of different devices: /device:TPU:56 before, /device:TPU:19 now
where the time goes in v7:
time: 150 us
  waiting for transfers between devices  58.5 us (39%)
  starting transfers between devices  55.4 us (37%)
  between operations  13.8 us (9%)
  Pallas kernels  11.9 us (8%)
  local copies, waits for them, and re-layouts  6.45 us (4%)
  other arithmetic  3.59 us (2%)
    ppermute x12, waiting for transfers between devices, move(): return lax.ppermute(value, axes, pairs)  42.9 us
    ppermute x12, starting transfers between devices, move(): return lax.ppermute(value, axes, pairs)  29.3 us
    all_to_all x1, starting transfers between devices, body(): ends = lax.all_to_all(ends, 'ctx', 0, 0, tiled=True)  14.6 us
    all_to_all x1, starting transfers between devices, body(): incoming = lax.all_to_all(carried, 'ctx', 0, 0, tiled=True).reshape(64, 128)  9.53 us
    all_to_all x1, waiting for transfers between devices, body(): incoming = lax.all_to_all(carried, 'ctx', 0, 0, tiled=True).reshape(64, 128)  7.8 us
    all_to_all x1, waiting for transfers between devices, body(): ends = lax.all_to_all(ends, 'ctx', 0, 0, tiled=True)  7.78 us
    unnamed x11, local copies, waits for them, and re-layouts  4.24 us
  transfers between devices with their start and end apart: 16, of which 11 were waited for; matrix products, arithmetic and copies ran while one was open for 4% of the time, Pallas kernels for 5%

profile of v7, /device:TPU:19, one launch (start us, length us, event | category | flops | bytes accessed | tf_op | source)
XLA Modules:
  0.0 149.6 jit_solution(7318239893830078079)
XLA Ops:
  6.5 2.4 %first.1 = f32[32,16,128]{2,1,0:T(8,128)} custom-call(bf16[3,128,512]{2,1,0:T(8,128)(2,1)} %bitcast.24, f32[3,3,512]{2,1,0:T(4,128)} %taps_ref.3, f32[16,512]{1,0:T(8,128)} %rate_ref.5), custom_call_target="tpu_custom_call" | custom-call | flops 1 | bytes 1 | tf_op jit(solution)/shard_map/first/pallas_call | solution.py:205
  9.0 14.6 %all-to-all-start = ((f32[32,16,128]{2,1,0:T(8,128)}), f32[32,16,128]{2,1,0:T(8,128)S(1)}, u32[]{:S(2)}, u32[]{:S(2)}) async-start(f32[32,16,128]{2,1,0:T(8,128)} %first.1), calls=%async_computation | async-start | bytes 524288 | tf_op jit(solution)/shard_map/all_to_all | solution.py:306
  23.6 0.0 all-gather.3.cloned.1.call-start
  23.6 4.2 %collective-permute-start = (bf16[512,256]{1,0:T(8,128)(2,1)}, bf16[512,256]{1,0:T(8,128)(2,1)S(1)}, u32[]{:S(2)}, u32[]{:S(2)}) collective-permute-start(bf16[512,256]{1,0:T(8,128)(2,1)} %param.11), channel_id=1, source_target_pairs={{0,0},{1,1},{2,2},{3,3},{4,16},{5,17},{6,18},{7,19},{8,32},{9,33},... | collective-permute-start | bytes 786440 | tf_op jit(solution)/shard_map/ppermute | solution.py:27
  27.8 0.8 slice.24
  28.5 1.9 %collective-permute-start.1 = (bf16[2,3,512]{2,0,1:T(2,128)(2,1)S(1)}, bf16[2,3,512]{2,0,1:T(2,128)(2,1)S(1)}, u32[]{:S(2)}, u32[]{:S(2)}) collective-permute-start(bf16[2,3,512]{2,0,1:T(2,128)(2,1)S(1)} %slice.24), channel_id=1, source_target_pairs={{0,16},{1,17},{2,18},{3,19},{4,20},{5,21},{6,22},{7,23},{8,24},{9,... | collective-permute-start | bytes 18440 | tf_op jit(solution)/shard_map/ppermute | solution.py:32
  30.5 1.3 dynamic_slice.3.rate_ref
  31.8 7.8 %all-to-all-done.ends_ref = f32[32,16,128]{2,1,0:T(8,128)S(1)} async-done(((f32[32,16,128]{2,1,0:T(8,128)}), f32[32,16,128]{2,1,0:T(8,128)S(1)}, u32[]{:S(2)}, u32[]{:S(2)}) %all-to-all-start) | async-done | bytes 262176 | tf_op jit(solution)/shard_map/all_to_all | solution.py:306
  39.6 0.7 copy-done.1
  40.3 1.6 %carry.1 = f32[32,2,128]{2,1,0:T(2,128)} custom-call(f32[32,16,128]{2,1,0:T(8,128)} %copy-done.1, f32[2,128]{1,0:T(2,128)} %dynamic_slice.3.rate_ref), custom_call_target="tpu_custom_call" | custom-call | flops 1 | bytes 1 | tf_op jit(solution)/shard_map/carry/pallas_call | solution.py:217
  42.0 0.7 copy-done.2
  42.7 0.0 all-gather.3.cloned.1.call-update
  42.7 9.5 %all-to-all-start.1 = ((f32[32,2,128]{2,1,0:T(2,128)}), f32[32,2,128]{2,1,0:T(2,128)S(1)}, u32[]{:S(2)}, u32[]{:S(2)}) async-start(f32[32,2,128]{2,1,0:T(2,128)} %carry.1), calls=%async_computation.1 | async-start | bytes 65536 | tf_op jit(solution)/shard_map/all_to_all | solution.py:312
  52.2 1.4 sqrt_multiply_fusion.gain_ref
  53.6 2.6 %middle.1 = (f32[128,512]{1,0:T(8,128)}, f32[512,128]{1,0:T(8,128)}, f32[128,128]{1,0:T(8,128)}) custom-call(bf16[3,128,512]{2,1,0:T(8,128)(2,1)} %bitcast.25, bf16[3,2,512]{2,1,0:T(2,128)(2,1)} %bitcast.27, f32[3,3,512]{2,1,0:T(4,128)} %taps_ref.3, f32[16,512]{1,0:T(8,128)} %rate_ref.5), custom_call_target="tpu_custom_call" | custom-call | flops 1 | bytes 1 | tf_op jit(solution)/shard_map/middle/pallas_call | solution.py:228
  56.2 7.8 %all-to-all-done.1 = f32[32,2,128]{2,1,0:T(2,128)S(1)} async-done(((f32[32,2,128]{2,1,0:T(2,128)}), f32[32,2,128]{2,1,0:T(2,128)S(1)}, u32[]{:S(2)}, u32[]{:S(2)}) %all-to-all-start.1) | async-done | bytes 32800 | tf_op jit(solution)/shard_map/all_to_all | solution.py:312
  64.0 0.6 copy-done.3
  64.6 2.5 %back.1 = bf16[128,512]{1,0:T(8,128)(2,1)} custom-call(f32[128,512]{1,0:T(8,128)} %get-tuple-element.16.query_ref, f32[512,128]{1,0:T(8,128)} %get-tuple-element.17.drive_ref, f32[128,128]{1,0:T(8,128)} %get-tuple-element.18.half_ref, f32[64,128]{1,0:T(8,128)} %bitcast.26, f32[16,512]{1,0:T(8,128)} %rate_ref.5, f32[16,512]{1,0:T(8,128)} %sqrt_multiply_fusion.gain_ref, ...), custom_call_target="tpu_custom_call" | custom-call | flops 1 | bytes 1 | tf_op jit(solution)/shard_map/back/pallas_call | solution.py:244
  67.1 1.3 collective-permute-start.2
  68.4 2.2 %collective-permute-done.2 = bf16[128,512]{1,0:T(8,128)(2,1)S(1)} collective-permute-done((bf16[128,512]{1,0:T(8,128)(2,1)}, bf16[128,512]{1,0:T(8,128)(2,1)S(1)}, u32[]{:S(2)}, u32[]{:S(2)}) %collective-permute-start.2) | collective-permute-done | bytes 131104 | tf_op jit(solution)/shard_map/ppermute | solution.py:27
  70.6 0.9 pad_maximum_fusion.1
  71.5 2.5 %collective-permute-start.3 = (bf16[256,512]{1,0:T(8,128)(2,1)S(1)}, bf16[256,512]{1,0:T(8,128)(2,1)S(1)}, u32[]{:S(2)}, u32[]{:S(2)}) collective-permute-start(bf16[256,512]{1,0:T(8,128)(2,1)S(1)} %pad_maximum_fusion.1), channel_id=1, source_target_pairs={{0,256},{1,257},{2,258},{3,259},{8,264},{9,265},{10,266},{11,267},... | collective-permute-start | bytes 786440 | tf_op jit(solution)/shard_map/ppermute | solution.py:27
  74.1 11.3 %collective-permute-done.3 = bf16[256,512]{1,0:T(8,128)(2,1)S(1)} collective-permute-done((bf16[256,512]{1,0:T(8,128)(2,1)S(1)}, bf16[256,512]{1,0:T(8,128)(2,1)S(1)}, u32[]{:S(2)}, u32[]{:S(2)}) %collective-permute-start.3) | collective-permute-done | bytes 262176 | tf_op jit(solution)/shard_map/ppermute | solution.py:27
  85.3 0.9 pad_maximum_fusion.line
  86.3 1.3 collective-permute-start.5
  87.6 1.3 collective-permute-start.4
  88.9 4.7 %collective-permute-done.5.bwd = bf16[512,512]{1,0:T(8,128)(2,1)S(1)} collective-permute-done((bf16[512,512]{1,0:T(8,128)(2,1)S(1)}, bf16[512,512]{1,0:T(8,128)(2,1)S(1)}, u32[]{:S(2)}, u32[]{:S(2)}) %collective-permute-start.5) | collective-permute-done | bytes 524320 | tf_op jit(solution)/shard_map/ppermute | solution.py:27
  93.7 1.3 collective-permute-start.7
  95.0 0.0 collective-permute-done.4.fwd
  95.0 1.3 collective-permute-start.6
  96.5 0.1 stack.27.table_ref
  96.6 4.2 %collective-permute-done.7.hb = bf16[256,512]{1,0:T(8,128)(2,1)S(1)} collective-permute-done((bf16[256,512]{1,0:T(8,128)(2,1)S(1)}, bf16[256,512]{1,0:T(8,128)(2,1)S(1)}, u32[]{:S(2)}, u32[]{:S(2)}) %collective-permute-start.7) | collective-permute-done | bytes 262176 | tf_op jit(solution)/shard_map/ppermute | solution.py:27
  100.8 1.9 %collective-permute-done.6.hf = bf16[256,512]{1,0:T(8,128)(2,1)S(1)} collective-permute-done((bf16[256,512]{1,0:T(8,128)(2,1)S(1)}, bf16[256,512]{1,0:T(8,128)(2,1)S(1)}, u32[]{:S(2)}, u32[]{:S(2)}) %collective-permute-start.6) | collective-permute-done | bytes 262176 | tf_op jit(solution)/shard_map/ppermute | solution.py:27
  102.7 1.6 %copy-done = bf16[4096,256]{1,0:T(8,128)(2,1)S(1)} copy-done((bf16[4096,256]{1,0:T(8,128)(2,1)S(1)}, bf16[4096,256]{1,0:T(8,128)(2,1)}, u32[]{:S(2)}) %copy-start) | copy-done | bytes 2097176
  104.3 1.4 send.1
  105.7 3.7 %collective-permute-start.8 = (f32[4,128,512]{2,1,0:T(8,128)S(1)}, f32[4,128,512]{2,1,0:T(8,128)S(1)}, u32[]{:S(2)}, u32[]{:S(2)}) collective-permute-start(f32[4,128,512]{2,1,0:T(8,128)S(1)} %send.1), channel_id=1, source_target_pairs={{0,16},{1,17},{2,18},{3,19},{4,20},{5,21},{6,22},{7,23},{8,24},{9,... | collective-permute-start | bytes 3145736 | tf_op jit(solution)/shard_map/ppermute | solution.py:27
  109.4 1.4 keep.1
  110.7 0.9 collective-permute-done.8
  111.6 0.3 fusion.2
  111.9 1.9 %collective-permute-start.9 = (bf16[128,512]{1,0:T(8,128)(2,1)S(1)}, bf16[128,512]{1,0:T(8,128)(2,1)S(1)}, u32[]{:S(2)}, u32[]{:S(2)}) collective-permute-start(bf16[128,512]{1,0:T(8,128)(2,1)S(1)} %get-tuple-element.23), channel_id=1, source_target_pairs={{0,1},{1,2},{2,3},{3,0},{4,5},{5,6},{6,7},{7,4},{8,9},{9,10},{10,1... | collective-permute-start | bytes 393224 | tf_op jit(solution)/shard_map/ppermute | solution.py:27
  113.8 3.4 %collective-permute-start.11 = (bf16[128,512]{1,0:T(8,128)(2,1)S(1)}, bf16[128,512]{1,0:T(8,128)(2,1)S(1)}, u32[]{:S(2)}, u32[]{:S(2)}) collective-permute-start(bf16[128,512]{1,0:T(8,128)(2,1)S(1)} %get-tuple-element.24), channel_id=1, source_target_pairs={{0,3},{1,0},{2,1},{3,2},{4,7},{5,4},{6,5},{7,6},{8,11},{9,8},{10,9... | collective-permute-start | bytes 393224 | tf_op jit(solution)/shard_map/ppermute | solution.py:27
  117.2 3.1 %collective-permute-start.10 = (bf16[128,512]{1,0:T(8,128)(2,1)S(1)}, bf16[128,512]{1,0:T(8,128)(2,1)S(1)}, u32[]{:S(2)}, u32[]{:S(2)}) collective-permute-start(bf16[128,512]{1,0:T(8,128)(2,1)S(1)} %get-tuple-element.25), channel_id=1, source_target_pairs={{0,2},{1,3},{2,0},{3,1},{4,6},{5,7},{6,4},{7,5},{8,10},{9,11},{10,... | collective-permute-start | bytes 393224 | tf_op jit(solution)/shard_map/ppermute | solution.py:27
  120.3 0.2 collective-permute-done.11
  120.5 4.9 %collective-permute-done.10 = bf16[128,512]{1,0:T(8,128)(2,1)S(1)} collective-permute-done((bf16[128,512]{1,0:T(8,128)(2,1)S(1)}, bf16[128,512]{1,0:T(8,128)(2,1)S(1)}, u32[]{:S(2)}, u32[]{:S(2)}) %collective-permute-start.10) | collective-permute-done | bytes 131104 | tf_op jit(solution)/shard_map/ppermute | solution.py:27
  125.4 0.1 fusion.1
  125.5 4.1 %collective-permute-start.12 = (bf16[128,512]{1,0:T(8,128)(2,1)S(1)}, bf16[128,512]{1,0:T(8,128)(2,1)S(1)}, u32[]{:S(2)}, u32[]{:S(2)}) collective-permute-start(bf16[128,512]{1,0:T(8,128)(2,1)S(1)} %fusion.1), channel_id=1, source_target_pairs={{0,0},{1,4},{2,256},{3,260},{4,5},{5,1},{6,261},{7,257},{8,258},{9... | collective-permute-start | bytes 393224 | tf_op jit(solution)/shard_map/ppermute | solution.py:27
  129.6 12.6 %collective-permute-done.12 = bf16[128,512]{1,0:T(8,128)(2,1)S(1)} collective-permute-done((bf16[128,512]{1,0:T(8,128)(2,1)S(1)}, bf16[128,512]{1,0:T(8,128)(2,1)S(1)}, u32[]{:S(2)}, u32[]{:S(2)}) %collective-permute-start.12) | collective-permute-done | bytes 131104 | tf_op jit(solution)/shard_map/ppermute | solution.py:27
  142.1 0.7 copy.8
  (13 shorter events, 0.1 us)
Async XLA Ops:
  9.0 30.7 %all-to-all-start = ((f32[32,16,128]{2,1,0:T(8,128)}), f32[32,16,128]{2,1,0:T(8,128)S(1)}, u32[]{:S(2)}, u32[]{:S(2)}) async-start(f32[32,16,128]{2,1,0:T(8,128)} %first.1), calls=%async_computation | async-start | bytes 524288 | tf_op jit(solution)/shard_map/all_to_all | solution.py:306
  23.6 79.1 %all-gather.3.cloned.1.call-start = ((), (), s32[]{:S(2)}) async-start(), calls=%async_computation.2 | async-start | bytes 2359296 | tf_op jit(solution)/shard_map/all_gather | solution.py:311
  23.6 18.3 %collective-permute-start = (bf16[512,256]{1,0:T(8,128)(2,1)}, bf16[512,256]{1,0:T(8,128)(2,1)S(1)}, u32[]{:S(2)}, u32[]{:S(2)}) collective-permute-start(bf16[512,256]{1,0:T(8,128)(2,1)} %param.11), channel_id=1, source_target_pairs={{0,0},{1,1},{2,2},{3,3},{4,16},{5,17},{6,18},{7,19},{8,32},{9,33},... | collective-permute-start | bytes 786440 | tf_op jit(solution)/shard_map/ppermute | solution.py:27
  28.5 13.4 %collective-permute-start.1 = (bf16[2,3,512]{2,0,1:T(2,128)(2,1)S(1)}, bf16[2,3,512]{2,0,1:T(2,128)(2,1)S(1)}, u32[]{:S(2)}, u32[]{:S(2)}) collective-permute-start(bf16[2,3,512]{2,0,1:T(2,128)(2,1)S(1)} %slice.24), channel_id=1, source_target_pairs={{0,16},{1,17},{2,18},{3,19},{4,20},{5,21},{6,22},{7,23},{8,24},{9,... | collective-permute-start | bytes 18440 | tf_op jit(solution)/shard_map/ppermute | solution.py:32
  39.6 0.7 copy-start.1
  42.0 11.7 %copy-start.4 = (bf16[2,3,512]{2,0,1:T(2,128)(2,1)}, bf16[2,3,512]{2,0,1:T(2,128)(2,1)S(1)}, u32[]{:S(2)}) copy-start(bf16[2,3,512]{2,0,1:T(2,128)(2,1)S(1)} %collective-permute-done.1) | copy-start | bytes 18436
  42.0 0.7 copy-start.2
  42.7 21.3 %all-to-all-start.1 = ((f32[32,2,128]{2,1,0:T(2,128)}), f32[32,2,128]{2,1,0:T(2,128)S(1)}, u32[]{:S(2)}, u32[]{:S(2)}) async-start(f32[32,2,128]{2,1,0:T(2,128)} %carry.1), calls=%async_computation.1 | async-start | bytes 65536 | tf_op jit(solution)/shard_map/all_to_all | solution.py:312
  64.0 0.6 copy-start.3
  67.1 3.4 %collective-permute-start.2 = (bf16[128,512]{1,0:T(8,128)(2,1)}, bf16[128,512]{1,0:T(8,128)(2,1)S(1)}, u32[]{:S(2)}, u32[]{:S(2)}) collective-permute-start(bf16[128,512]{1,0:T(8,128)(2,1)} %back.1), channel_id=1, source_target_pairs={{4,20},{5,21},{6,22},{7,23},{12,28},{13,29},{14,30},{15,31},{16,0}... | collective-permute-start | bytes 393224 | tf_op jit(solution)/shard_map/ppermute | solution.py:27
  71.5 13.8 %collective-permute-start.3 = (bf16[256,512]{1,0:T(8,128)(2,1)S(1)}, bf16[256,512]{1,0:T(8,128)(2,1)S(1)}, u32[]{:S(2)}, u32[]{:S(2)}) collective-permute-start(bf16[256,512]{1,0:T(8,128)(2,1)S(1)} %pad_maximum_fusion.1), channel_id=1, source_target_pairs={{0,256},{1,257},{2,258},{3,259},{8,264},{9,265},{10,266},{11,267},... | collective-permute-start | bytes 786440 | tf_op jit(solution)/shard_map/ppermute | solution.py:27
  86.3 7.4 %collective-permute-start.5 = (bf16[512,512]{1,0:T(8,128)(2,1)S(1)}, bf16[512,512]{1,0:T(8,128)(2,1)S(1)}, u32[]{:S(2)}, u32[]{:S(2)}) collective-permute-start(bf16[512,512]{1,0:T(8,128)(2,1)S(1)} %pad_maximum_fusion.line), channel_id=1, source_target_pairs={{0,12},{1,13},{2,14},{3,15},{8,4},{9,5},{10,6},{11,7},{20,16},{21,... | collective-permute-start | bytes 1572872 | tf_op jit(solution)/shard_map/ppermute | solution.py:27
  87.6 7.4 %collective-permute-start.4 = (bf16[512,512]{1,0:T(8,128)(2,1)S(1)}, bf16[512,512]{1,0:T(8,128)(2,1)S(1)}, u32[]{:S(2)}, u32[]{:S(2)}) collective-permute-start(bf16[512,512]{1,0:T(8,128)(2,1)S(1)} %pad_maximum_fusion.line), channel_id=1, source_target_pairs={{0,4},{1,5},{2,6},{3,7},{8,12},{9,13},{10,14},{11,15},{20,24},{21,... | collective-permute-start | bytes 1572872 | tf_op jit(solution)/shard_map/ppermute | solution.py:27
  93.7 7.1 %collective-permute-start.7 = (bf16[256,512]{1,0:T(8,128)(2,1)S(1)}, bf16[256,512]{1,0:T(8,128)(2,1)S(1)}, u32[]{:S(2)}, u32[]{:S(2)}) collective-permute-start(bf16[256,512]{1,0:T(8,128)(2,1)S(1)} %slice.32), channel_id=1, source_target_pairs={{4,0},{5,1},{6,2},{7,3},{12,8},{13,9},{14,10},{15,11},{16,28},{17,... | collective-permute-start | bytes 786440 | tf_op jit(solution)/shard_map/ppermute | solution.py:27
  95.0 7.7 %collective-permute-start.6 = (bf16[256,512]{1,0:T(8,128)(2,1)S(1)}, bf16[256,512]{1,0:T(8,128)(2,1)S(1)}, u32[]{:S(2)}, u32[]{:S(2)}) collective-permute-start(bf16[256,512]{1,0:T(8,128)(2,1)S(1)} %slice.31), channel_id=1, source_target_pairs={{4,8},{5,9},{6,10},{7,11},{12,0},{13,1},{14,2},{15,3},{16,20},{17,... | collective-permute-start | bytes 786440 | tf_op jit(solution)/shard_map/ppermute | solution.py:27
  102.7 1.6 %copy-start = (bf16[4096,256]{1,0:T(8,128)(2,1)S(1)}, bf16[4096,256]{1,0:T(8,128)(2,1)}, u32[]{:S(2)}) copy-start(bf16[4096,256]{1,0:T(8,128)(2,1)} %all-gather.3.cloned.1.call-done) | copy-start | bytes 6291460
  105.7 5.9 %collective-permute-start.8 = (f32[4,128,512]{2,1,0:T(8,128)S(1)}, f32[4,128,512]{2,1,0:T(8,128)S(1)}, u32[]{:S(2)}, u32[]{:S(2)}) collective-permute-start(f32[4,128,512]{2,1,0:T(8,128)S(1)} %send.1), channel_id=1, source_target_pairs={{0,16},{1,17},{2,18},{3,19},{4,20},{5,21},{6,22},{7,23},{8,24},{9,... | collective-permute-start | bytes 3145736 | tf_op jit(solution)/shard_map/ppermute | solution.py:27
  111.9 8.4 %collective-permute-start.9 = (bf16[128,512]{1,0:T(8,128)(2,1)S(1)}, bf16[128,512]{1,0:T(8,128)(2,1)S(1)}, u32[]{:S(2)}, u32[]{:S(2)}) collective-permute-start(bf16[128,512]{1,0:T(8,128)(2,1)S(1)} %get-tuple-element.23), channel_id=1, source_target_pairs={{0,1},{1,2},{2,3},{3,0},{4,5},{5,6},{6,7},{7,4},{8,9},{9,10},{10,1... | collective-permute-start | bytes 393224 | tf_op jit(solution)/shard_map/ppermute | solution.py:27
  113.8 6.6 %collective-permute-start.11 = (bf16[128,512]{1,0:T(8,128)(2,1)S(1)}, bf16[128,512]{1,0:T(8,128)(2,1)S(1)}, u32[]{:S(2)}, u32[]{:S(2)}) collective-permute-start(bf16[128,512]{1,0:T(8,128)(2,1)S(1)} %get-tuple-element.24), channel_id=1, source_target_pairs={{0,3},{1,0},{2,1},{3,2},{4,7},{5,4},{6,5},{7,6},{8,11},{9,8},{10,9... | collective-permute-start | bytes 393224 | tf_op jit(solution)/shard_map/ppermute | solution.py:27
  117.2 8.2 %collective-permute-start.10 = (bf16[128,512]{1,0:T(8,128)(2,1)S(1)}, bf16[128,512]{1,0:T(8,128)(2,1)S(1)}, u32[]{:S(2)}, u32[]{:S(2)}) collective-permute-start(bf16[128,512]{1,0:T(8,128)(2,1)S(1)} %get-tuple-element.25), channel_id=1, source_target_pairs={{0,2},{1,3},{2,0},{3,1},{4,6},{5,7},{6,4},{7,5},{8,10},{9,11},{10,... | collective-permute-start | bytes 393224 | tf_op jit(solution)/shard_map/ppermute | solution.py:27
  125.5 16.7 %collective-permute-start.12 = (bf16[128,512]{1,0:T(8,128)(2,1)S(1)}, bf16[128,512]{1,0:T(8,128)(2,1)S(1)}, u32[]{:S(2)}, u32[]{:S(2)}) collective-permute-start(bf16[128,512]{1,0:T(8,128)(2,1)S(1)} %fusion.1), channel_id=1, source_target_pairs={{0,0},{1,4},{2,256},{3,260},{4,5},{5,1},{6,261},{7,257},{8,258},{9... | collective-permute-start | bytes 393224 | tf_op jit(solution)/shard_map/ppermute | solution.py:27
Sparse Core Ops, SparseCore 0:
  42.8 39.9 all-gather.2

commit v8 on v7

v8 whole, which is shorter than its diff:
```python
import functools

import jax
import jax.numpy as jnp
from jax import lax
from jax.experimental import pallas as pl
from jax.experimental.pallas import tpu as pltpu
from jax.sharding import PartitionSpec as P

AXES = ("ctx", "tp")
EVERY = [
    (yh, z, core, x, yl)
    for yh in range(2)
    for z in range(8)
    for core in range(2)
    for x in range(4)
    for yl in range(4)
]


def flat(yh, z, core, x, yl):
    return ((yh * 8 + z) * 2 + core) * 16 + x * 4 + yl


def move(value, axes, target, sends=lambda *place: True):
    pairs = [(flat(*p), flat(*target(*p))) for p in EVERY if sends(*p)]
    return lax.ppermute(value, axes, pairs)


VMEM = pl.BlockSpec(memory_space=pltpu.VMEM)
SMEM = pl.BlockSpec(memory_space=pltpu.SMEM)


def spread(ref, value):
    rows = value.shape[0]
    for half in range(2):
        for part in range(4):
            ref[pl.ds(half * 4 + part, rows, stride=8), :] = value[:, part * 128 : part * 128 + 128]


def first_kernel(feat_ref, taps_ref, rate_ref, out_ref, query_ref, drive_ref, half_ref, own_ref, ext, lam):
    totals = []
    sides = []
    for f in range(3):
        taps = [taps_ref[j, f : f + 1, :] for j in range(3)]
        ext[8:136, :] = feat_ref[f].astype(jnp.float32)
        ext[0:8, :] = jnp.zeros((8, 512), jnp.float32)
        total = taps[0] * ext[8:136, :] + taps[1] * ext[7:135, :] + taps[2] * ext[6:134, :]
        totals.append(total)
        last = ext[135:136, :]
        sides.append((total[0:1], total[1:2], taps[1] * last + taps[2] * ext[134:135, :], taps[2] * last))
    query_ref[...] = totals[0]
    own = [sides[1][0], sides[2][0], sides[1][1], sides[2][1]]
    side = jnp.concatenate(own + [sides[1][2], sides[2][2], sides[1][3], sides[2][3]], axis=0)
    for r in range(4):
        for part in range(4):
            own_ref[r * 4 + part : r * 4 + part + 1, :] = own[r][:, part * 128 : part * 128 + 128]
    pack_positions(drive_ref, totals[1] * totals[2])
    spread(lam, jnp.exp(-rate_ref[...]))
    lams = [lam[m * 8 : m * 8 + 8, :] for m in range(16)]

    def step(t, states):
        now = drive_ref[pl.ds(pl.multiple_of(t * 8, 8), 8), :]
        return tuple(a * s + now for a, s in zip(lams, states))

    states = lax.fori_loop(0, 64, step, tuple(jnp.zeros((8, 128), jnp.float32) for _ in range(16)), unroll=4)
    spread(lam, jnp.exp(-64.0 * rate_ref[...]))
    for part in range(4):
        cols = slice(part * 128, part * 128 + 128)
        for pair in range(8):
            out_ref[pair * 4 + part, 8:16, :] = side[:, cols]
            out_ref[pair * 4 + part, 2:3, :] = sides[0][2][:, cols]
            out_ref[pair * 4 + part, 3:4, :] = sides[0][3][:, cols]
    for m in range(16):
        half_ref[m * 8 : m * 8 + 8, :] = states[m]
        end = states[m] + pltpu.roll(lam[m * 8 : m * 8 + 8, :] * states[m], 4, 0)
        for part in range(4):
            out_ref[m // 2 * 4 + part, m % 2 : m % 2 + 1, :] = end[4 + part : 5 + part]


def carry_kernel(ends_ref, rate_ref, out_ref):
    rate = rate_ref[...]
    whole, late, later = jnp.exp(-128.0 * rate), jnp.exp(-127.0 * rate), jnp.exp(-126.0 * rate)
    state = jnp.zeros((2, 128), jnp.float32)
    for k in range(32):
        out_ref[k, 0:2, :] = state
        end = ends_ref[k, 0:2, :]
        if k == 0:
            out_ref[k, 2:8, :] = jnp.zeros((6, 128), jnp.float32)
        else:
            here, before = ends_ref[k, 8:12, :], ends_ref[k - 1, 12:16, :]
            out_ref[k, 2:6, :] = before
            out_ref[k, 6:8, :] = ends_ref[k - 1, 2:4, :]
            full = here + before
            end = end + late * (full[0:1] * full[1:2] - here[0:1] * here[1:2])
            end = end + later * (full[2:3] * full[3:4] - here[2:3] * here[3:4])
        state = whole * state + end


def pack_positions(ref, drive):
    for half in range(2):
        for part in range(4):
            ref[pl.ds(half * 4 + part, 64, stride=8), :] = drive[
                half * 64 : half * 64 + 64, part * 128 : part * 128 + 128
            ]


def back_kernel(
    query_ref, drive_ref, half_ref, own_ref, in_ref, rate_ref, gain_ref, skip_ref, out_ref, lam, late, later, gain, skip, resp
):
    spread(gain, gain_ref[...])
    spread(lam, jnp.exp(-64.0 * rate_ref[...]))
    spread(late, jnp.exp(-63.0 * rate_ref[...]))
    spread(later, jnp.exp(-62.0 * rate_ref[...]))
    own = [own_ref[r * 4 : r * 4 + 4, :] for r in range(4)]
    full = [own[r] + in_ref[pl.ds(2 + r, 4, stride=8), :] for r in range(4)]
    more = [full[0] * full[1] - own[0] * own[1], full[2] * full[3] - own[2] * own[3]]
    states = []
    for m in range(16):
        rows = slice(m * 8, m * 8 + 4)
        came = in_ref[pl.ds(m // 2 * 32 + m % 2, 4, stride=8), :]
        half = half_ref[rows, :] + late[rows, :] * more[0] + later[rows, :] * more[1]
        states.append(jnp.concatenate([came, lam[rows, :] * came + half], axis=0))
    spread(lam, jnp.exp(-rate_ref[...]))
    spread(skip, skip_ref[...])
    lams = [lam[m * 8 : m * 8 + 8, :] for m in range(16)]
    gains = [gain[m * 8 : m * 8 + 8, :] for m in range(16)]
    direct = skip[...]

    def advance(now, states):
        states = tuple(a * s + now for a, s in zip(lams, states))
        sums = [direct * now, None, None, None]
        for m in range(16):
            term = gains[m] * states[m]
            sums[m % 4] = term if sums[m % 4] is None else sums[m % 4] + term
        return (sums[0] + sums[1]) + (sums[2] + sums[3]), states

    states = tuple(states)
    for t in range(2):
        now = drive_ref[t * 8 : t * 8 + 8, :]
        now = now + jnp.concatenate([more[t], jnp.zeros((4, 128), jnp.float32)], axis=0)
        resp[t * 8 : t * 8 + 8, :], states = advance(now, states)

    def step(t, states):
        rows = pl.ds(pl.multiple_of(t * 8, 8), 8)
        resp[rows, :], states = advance(drive_ref[rows, :], states)
        return states

    lax.fori_loop(2, 64, step, states, unroll=2)
    row = lax.broadcasted_iota(jnp.int32, (64, 128), 0)
    for half in range(2):
        for part in range(4):
            rows, cols = slice(half * 64, half * 64 + 64), slice(part * 128, part * 128 + 128)
            query = query_ref[rows, cols]
            if half == 0:
                query = query + jnp.where(row == 0, in_ref[part * 8 + 6 : part * 8 + 7, :], 0.0)
                query = query + jnp.where(row == 1, in_ref[part * 8 + 7 : part * 8 + 8, :], 0.0)
            out_ref[rows, cols] = (query * resp[pl.ds(half * 4 + part, 64, stride=8), :]).astype(jnp.bfloat16)


def mix_kernel(part, table_ref, line, fwd, bwd, hf, hb, weights, out_ref, g, g_sem):
    own = table_ref[0] == 1
    yl, x = table_ref[1], table_ref[4]

    def copies(pieces):
        made = []
        for far in range(2):
            for source, rows, block in pieces[far]:
                depth = pl.ds(pl.multiple_of(table_ref[block] * 512, 512), 512)
                target = g.at[pl.ds(far * 128, 128), depth]
                made.append(pltpu.make_async_copy(source.at[pl.ds(rows + part * 128, 128), :], target, g_sem.at[len(made)]))
        return made

    from_own = [[(line, 0, 2), (hf, 0, 3)], [(line, 256, 2), (hb, 0, 3)]]
    from_others = [[(fwd, 0, 2), (bwd, 0, 3)], [(fwd, 256, 2), (bwd, 256, 3)]]

    @pl.when(own)
    def _():
        for copy in copies(from_own):
            copy.start()

    @pl.when(jnp.logical_not(own))
    def _():
        for copy in copies(from_others):
            copy.start()

    @pl.when(own)
    def _():
        for copy in copies(from_own):
            copy.wait()

    @pl.when(jnp.logical_not(own))
    def _():
        for copy in copies(from_others):
            copy.wait()

    for i in range(4):
        total = jnp.dot(g[...], weights[i], preferred_element_type=jnp.float32)
        cols = slice(i % 2 * 256, i % 2 * 256 + 256)
        for far in range(2):
            d = lax.rem(lax.bitwise_xor(far * 2 + i // 2, x) - yl + 4, 4)
            out_ref[d, :, cols] = total[far * 128 : far * 128 + 128]


TINY = pl.CostEstimate(flops=1, bytes_accessed=1, transcendentals=0)
F32 = jnp.float32


def first(feat, taps, rate):
    return pl.pallas_call(
        first_kernel,
        out_shape=(
            jax.ShapeDtypeStruct((32, 16, 128), F32),
            jax.ShapeDtypeStruct((128, 512), F32),
            jax.ShapeDtypeStruct((512, 128), F32),
            jax.ShapeDtypeStruct((128, 128), F32),
            jax.ShapeDtypeStruct((16, 128), F32),
        ),
        in_specs=[VMEM] * 3,
        out_specs=(VMEM,) * 5,
        scratch_shapes=[pltpu.VMEM((136, 512), F32), pltpu.VMEM((128, 128), F32)],
        cost_estimate=TINY,
        name="first",
    )(feat, taps, rate)


def carry(ends, rate):
    return pl.pallas_call(
        carry_kernel,
        out_shape=jax.ShapeDtypeStruct((32, 8, 128), F32),
        in_specs=[VMEM] * 2,
        out_specs=VMEM,
        cost_estimate=TINY,
        name="carry",
    )(ends, rate)


def back(query, drive, half, own, incoming, rate, gain, skip):
    return pl.pallas_call(
        back_kernel,
        out_shape=jax.ShapeDtypeStruct((128, 512), jnp.bfloat16),
        in_specs=[VMEM] * 8,
        out_specs=VMEM,
        scratch_shapes=[pltpu.VMEM((128, 128), F32)] * 4 + [pltpu.VMEM((8, 128), F32), pltpu.VMEM((512, 128), F32)],
        cost_estimate=TINY,
        name="back",
    )(query, drive, half, own, incoming, rate, gain, skip)


def mix(part, table, *operands):
    return pl.pallas_call(
        functools.partial(mix_kernel, part),
        out_shape=jax.ShapeDtypeStruct((4, 128, 512), jnp.float32),
        in_specs=[SMEM] + [pl.BlockSpec(memory_space=pl.ANY)] * 5 + [VMEM],
        out_specs=VMEM,
        scratch_shapes=[
            pltpu.VMEM((256, 1024), jnp.bfloat16),
            pltpu.SemaphoreType.DMA((4,)),
        ],
        compiler_params=pltpu.CompilerParams(vmem_limit_bytes=8 * 1024 * 1024),
        cost_estimate=pl.CostEstimate(flops=600_000_000, bytes_accessed=4_000_000, transcendentals=0),
        name=("keep", "send")[part],
    )(table, *operands)


def body(features, short_filter, decay_rate, residue, skip, out_weight, axes, first, carry, back, mix):
    index = lax.axis_index(axes)
    yl, x, core = index % 4, index // 4 % 4, index // 16 % 2

    tie = lax.optimization_barrier
    def place(yh, z, core, x, yl):
        return yh, z // 4 * 4 + core * 2 + x // 2, x % 2, z % 4, yl

    def along(axis, by):
        def target(yh, z, core, x, yl):
            if axis == "z":
                return yh, (z + by) % 8, core, x, yl
            if axis == "x":
                return yh, z, core, (x + by) % 4, yl
            return yh, z, core, x, (yl + by) % 4

        return target

    def mine(yh, z, core, x, yl):
        return x % 2 == core

    def others(yh, z, core, x, yl):
        return x % 2 != core

    def other_core(value, sends=lambda *place: True):
        return move(value, axes, lambda yh, z, core, x, yl: (yh, z, 1 - core, x, yl), sends)

    weight = move(out_weight, axes, place)
    along_z = [[(yh * 8 + z) * 2 + core for z in range(8)] for yh in range(2) for core in range(2)]

    feat = features.transpose(1, 0, 2)
    ends, query, drive, half, own = first(feat, short_filter, decay_rate)
    ends = lax.all_to_all(ends, "ctx", 0, 0, tiled=True)
    ctx = index // 16
    rate = lax.dynamic_slice(decay_rate, (ctx // 4 * 2, ctx % 4 * 128), (2, 128))
    gain = residue * jnp.sqrt(-jnp.expm1(-2.0 * decay_rate))
    ends, rate, gain = tie((ends, rate, gain))
    carried, weight = tie((carry(ends, rate), weight))
    weights = lax.all_gather(weight, "ctx", axis_index_groups=along_z)
    incoming = lax.all_to_all(carried, "ctx", 0, 0, tiled=True).reshape(256, 128)

    gated = back(query, drive, half, own, incoming, decay_rate, gain, skip[None])

    both = jnp.concatenate([gated, other_core(gated, others)], axis=0)
    beyond = move(both, axes, lambda yh, z, core, x, yl: (1 - yh, z, core, x, yl), mine)
    line = jnp.concatenate([both, beyond], axis=0)
    fwd = move(line, axes, along("x", 1), mine)
    bwd = move(line, axes, along("x", -1), mine)
    half_rows = line.shape[0] // 2
    hf = move(fwd[:half_rows], axes, along("x", 1), others)
    hb = move(bwd[half_rows:], axes, along("x", -1), others)

    matched = x % 2 == core
    low = jnp.where(matched, x // 2, (x + 3) % 4 // 2)
    high = jnp.where(matched, 1 - x // 2, (x + 1) % 4 // 2)
    table = jnp.stack([matched.astype(jnp.int32), yl, low, high, x]).astype(jnp.int32)
    operands = (table, line, fwd, bwd, hf, hb, weights.reshape(4, 1024, 256))
    sent = other_core(mix(1, *operands))
    keep = mix(0, *operands)

    blocks = keep + sent
    parts = [move(blocks[d].astype(jnp.bfloat16), axes, along("yl", d)) for d in range(1, 4)]
    total = blocks[0] + sum(part.astype(jnp.float32) for part in parts)

    def home(yh, z, core, x, yl):
        block = yl ^ x
        return yh ^ (block // 2), z, core, yh * 2 + block % 2, x

    return move(total.astype(jnp.bfloat16), axes, home)


def shards(*arguments):
    return body(*arguments, AXES, first, carry, back, mix)


def solution(mesh):
    in_specs = (
        P("ctx", None, "tp"),
        P(None, None, "tp"),
        P(None, "tp"),
        P(None, "tp"),
        P("tp"),
        P("tp", "ctx"),
    )
    return jax.shard_map(shards, mesh=mesh, in_specs=in_specs, out_specs=P("ctx", "tp"), check_vma=False)
```

time: 150 us -> 153 us (1.020)
  the two profiles are of different devices: /device:TPU:19 before, /device:TPU:56 now
where the time goes in v8:
time: 153 us; the launch traced here: 151 us
  starting transfers between devices  48.5 us (32%)
  waiting for transfers between devices  46.7 us (31%)
  blocking collectives  23.3 us (15%)
  between operations  13.7 us (9%)
  Pallas kernels  9.78 us (6%)
  local copies, waits for them, and re-layouts  5.14 us (3%)
  other arithmetic  3.59 us (2%)
    ppermute x12, waiting for transfers between devices, move(): return lax.ppermute(value, axes, pairs)  40 us
    ppermute x12, starting transfers between devices, move(): return lax.ppermute(value, axes, pairs)  32.6 us
    all_to_all x1, blocking collectives, body(): lax.all_to_all(carried, 'ctx', 0, 0, tiled=True).reshape(256, 128)  23.3 us
    all_to_all x1, starting transfers between devices, body(): ends = lax.all_to_all(ends, 'ctx', 0, 0, tiled=True)  15.8 us
    all_to_all x1, waiting for transfers between devices, body(): ends = lax.all_to_all(ends, 'ctx', 0, 0, tiled=True)  6.63 us
    unnamed x7, local copies, waits for them, and re-layouts  3.65 us
  transfers between devices with their start and end apart: 14, of which 10 were waited for; matrix products, arithmetic and copies ran while one was open for 3% of the time, Pallas kernels for 4%

profile of v8, /device:TPU:56, one launch (start us, length us, event | category | flops | bytes accessed | tf_op | source)
XLA Modules:
  0.0 150.7 jit_solution(15712895985617269417)
XLA Ops:
  6.5 2.7 %first.1 = (f32[32,16,128]{2,1,0:T(8,128)}, f32[128,512]{1,0:T(8,128)}, f32[512,128]{1,0:T(8,128)}, f32[128,128]{1,0:T(8,128)}, f32[16,128]{1,0:T(8,128)}) custom-call(bf16[3,128,512]{2,1,0:T(8,128)(2,1)} %bitcast.24, f32[3,3,512]{2,1,0:T(4,128)} %taps_ref.1, f32[16,512]{1,0:T(8,128)} %rate_ref.3), custom_call_target="tpu_custom_call" | custom-call | flops 1 | bytes 1 | tf_op jit(solution)/shard_map/first/pallas_call | solution.py:210
  9.3 15.8 %all-to-all-start = ((f32[32,16,128]{2,1,0:T(8,128)}), f32[32,16,128]{2,1,0:T(8,128)S(1)}, u32[]{:S(2)}, u32[]{:S(2)}) async-start(f32[32,16,128]{2,1,0:T(8,128)} %get-tuple-element.19), calls=%async_computation | async-start | bytes 524288 | tf_op jit(solution)/shard_map/all_to_all | solution.py:298
  25.1 0.0 all-gather.3.cloned.1.call-start
  25.2 1.6 %collective-permute-start = (bf16[512,256]{1,0:T(8,128)(2,1)}, bf16[512,256]{1,0:T(8,128)(2,1)S(1)}, u32[]{:S(2)}, u32[]{:S(2)}) collective-permute-start(bf16[512,256]{1,0:T(8,128)(2,1)} %param.11), channel_id=1, source_target_pairs={{0,0},{1,1},{2,2},{3,3},{4,16},{5,17},{6,18},{7,19},{8,32},{9,33},... | collective-permute-start | bytes 786440 | tf_op jit(solution)/shard_map/ppermute | solution.py:27
  26.8 1.3 dynamic_slice.3.rate_ref
  28.1 1.4 sqrt_multiply_fusion.gain_ref
  29.5 6.6 %all-to-all-done.ends_ref = f32[32,16,128]{2,1,0:T(8,128)S(1)} async-done(((f32[32,16,128]{2,1,0:T(8,128)}), f32[32,16,128]{2,1,0:T(8,128)S(1)}, u32[]{:S(2)}, u32[]{:S(2)}) %all-to-all-start) | async-done | bytes 262176 | tf_op jit(solution)/shard_map/all_to_all | solution.py:298
  36.2 0.0 copy-start.1
  36.2 0.7 copy-done.1
  36.9 1.7 %carry.1 = f32[32,8,128]{2,1,0:T(8,128)} custom-call(f32[32,16,128]{2,1,0:T(8,128)} %copy-done.1, f32[2,128]{1,0:T(2,128)} %dynamic_slice.3.rate_ref), custom_call_target="tpu_custom_call" | custom-call | flops 1 | bytes 1 | tf_op jit(solution)/shard_map/carry/pallas_call | solution.py:228
  38.6 0.0 collective-permute-done
  38.6 0.0 copy-start.2
  38.6 0.7 copy-done.2
  39.3 0.0 all-gather.3.cloned.1.call-update
  39.3 23.3 %all_to_all.10 = f32[32,8,128]{2,1,0:T(8,128)} all-to-all(f32[32,8,128]{2,1,0:T(8,128)} %carry.1), channel_id=1, replica_groups=mesh['ctx'=32,'tp'=16] {'ctx'}, dimensions={0} | all-to-all | bytes 262144 | tf_op jit(solution)/shard_map/all_to_all | solution.py:305
  62.6 2.6 %back.1 = bf16[128,512]{1,0:T(8,128)(2,1)} custom-call(f32[128,512]{1,0:T(8,128)} %get-tuple-element.15.query_ref, f32[512,128]{1,0:T(8,128)} %get-tuple-element.16.drive_ref, f32[128,128]{1,0:T(8,128)} %get-tuple-element.17.half_ref, f32[16,128]{1,0:T(8,128)} %get-tuple-element.18.own_ref, f32[256,128]{1,0:T(8,128)} %bitcast.23, f32[16,512]{1,0:T(8,128)} %rate_ref.3, ...), custom_call_target="tpu_custom_call" | custom-call | flops 1 | bytes 1 | tf_op jit(solution)/shard_map/back/pallas_call | solution.py:239
  65.2 1.3 collective-permute-start.1
  66.5 2.2 %collective-permute-done.1 = bf16[128,512]{1,0:T(8,128)(2,1)S(1)} collective-permute-done((bf16[128,512]{1,0:T(8,128)(2,1)}, bf16[128,512]{1,0:T(8,128)(2,1)S(1)}, u32[]{:S(2)}, u32[]{:S(2)}) %collective-permute-start.1) | collective-permute-done | bytes 131104 | tf_op jit(solution)/shard_map/ppermute | solution.py:27
  68.7 0.9 pad_maximum_fusion.1
  69.6 6.8 %collective-permute-start.2 = (bf16[256,512]{1,0:T(8,128)(2,1)S(1)}, bf16[256,512]{1,0:T(8,128)(2,1)S(1)}, u32[]{:S(2)}, u32[]{:S(2)}) collective-permute-start(bf16[256,512]{1,0:T(8,128)(2,1)S(1)} %pad_maximum_fusion.1), channel_id=1, source_target_pairs={{0,256},{1,257},{2,258},{3,259},{8,264},{9,265},{10,266},{11,267},... | collective-permute-start | bytes 786440 | tf_op jit(solution)/shard_map/ppermute | solution.py:27
  76.4 5.5 %collective-permute-done.2 = bf16[256,512]{1,0:T(8,128)(2,1)S(1)} collective-permute-done((bf16[256,512]{1,0:T(8,128)(2,1)S(1)}, bf16[256,512]{1,0:T(8,128)(2,1)S(1)}, u32[]{:S(2)}, u32[]{:S(2)}) %collective-permute-start.2) | collective-permute-done | bytes 262176 | tf_op jit(solution)/shard_map/ppermute | solution.py:27
  81.9 0.9 pad_maximum_fusion.line
  82.8 1.3 collective-permute-start.4
  84.1 1.3 collective-permute-start.3
  85.5 5.3 %collective-permute-done.4.bwd = bf16[512,512]{1,0:T(8,128)(2,1)S(1)} collective-permute-done((bf16[512,512]{1,0:T(8,128)(2,1)S(1)}, bf16[512,512]{1,0:T(8,128)(2,1)S(1)}, u32[]{:S(2)}, u32[]{:S(2)}) %collective-permute-start.4) | collective-permute-done | bytes 524320 | tf_op jit(solution)/shard_map/ppermute | solution.py:27
  90.8 1.3 collective-permute-start.6
  92.1 0.0 collective-permute-done.3.fwd
  92.2 1.3 collective-permute-start.5
  93.6 0.1 stack.27.table_ref
  93.7 5.8 %collective-permute-done.6.hb = bf16[256,512]{1,0:T(8,128)(2,1)S(1)} collective-permute-done((bf16[256,512]{1,0:T(8,128)(2,1)S(1)}, bf16[256,512]{1,0:T(8,128)(2,1)S(1)}, u32[]{:S(2)}, u32[]{:S(2)}) %collective-permute-start.6) | collective-permute-done | bytes 262176 | tf_op jit(solution)/shard_map/ppermute | solution.py:27
  99.5 2.1 %collective-permute-done.5.hf = bf16[256,512]{1,0:T(8,128)(2,1)S(1)} collective-permute-done((bf16[256,512]{1,0:T(8,128)(2,1)S(1)}, bf16[256,512]{1,0:T(8,128)(2,1)S(1)}, u32[]{:S(2)}, u32[]{:S(2)}) %collective-permute-start.5) | collective-permute-done | bytes 262176 | tf_op jit(solution)/shard_map/ppermute | solution.py:27
  101.6 0.0 all-gather.3.cloned.1.call-done
  101.6 1.6 %copy-done = bf16[4096,256]{1,0:T(8,128)(2,1)S(1)} copy-done((bf16[4096,256]{1,0:T(8,128)(2,1)S(1)}, bf16[4096,256]{1,0:T(8,128)(2,1)}, u32[]{:S(2)}) %copy-start) | copy-done | bytes 2097176
  103.2 1.4 send.1
  104.6 1.9 %collective-permute-start.7 = (f32[4,128,512]{2,1,0:T(8,128)S(1)}, f32[4,128,512]{2,1,0:T(8,128)S(1)}, u32[]{:S(2)}, u32[]{:S(2)}) collective-permute-start(f32[4,128,512]{2,1,0:T(8,128)S(1)} %send.1), channel_id=1, source_target_pairs={{0,16},{1,17},{2,18},{3,19},{4,20},{5,21},{6,22},{7,23},{8,24},{9,... | collective-permute-start | bytes 3145736 | tf_op jit(solution)/shard_map/ppermute | solution.py:27
  106.5 1.4 keep.1
  107.9 1.3 collective-permute-done.7
  109.1 0.3 fusion.2
  109.4 7.5 %collective-permute-start.8 = (bf16[128,512]{1,0:T(8,128)(2,1)S(1)}, bf16[128,512]{1,0:T(8,128)(2,1)S(1)}, u32[]{:S(2)}, u32[]{:S(2)}) collective-permute-start(bf16[128,512]{1,0:T(8,128)(2,1)S(1)} %get-tuple-element.27), channel_id=1, source_target_pairs={{0,1},{1,2},{2,3},{3,0},{4,5},{5,6},{6,7},{7,4},{8,9},{9,10},{10,1... | collective-permute-start | bytes 393224 | tf_op jit(solution)/shard_map/ppermute | solution.py:27
  116.9 1.9 %collective-permute-start.10 = (bf16[128,512]{1,0:T(8,128)(2,1)S(1)}, bf16[128,512]{1,0:T(8,128)(2,1)S(1)}, u32[]{:S(2)}, u32[]{:S(2)}) collective-permute-start(bf16[128,512]{1,0:T(8,128)(2,1)S(1)} %get-tuple-element.28), channel_id=1, source_target_pairs={{0,3},{1,0},{2,1},{3,2},{4,7},{5,4},{6,5},{7,6},{8,11},{9,8},{10,9... | collective-permute-start | bytes 393224 | tf_op jit(solution)/shard_map/ppermute | solution.py:27
  118.8 3.4 %collective-permute-start.9 = (bf16[128,512]{1,0:T(8,128)(2,1)S(1)}, bf16[128,512]{1,0:T(8,128)(2,1)S(1)}, u32[]{:S(2)}, u32[]{:S(2)}) collective-permute-start(bf16[128,512]{1,0:T(8,128)(2,1)S(1)} %get-tuple-element.29), channel_id=1, source_target_pairs={{0,2},{1,3},{2,0},{3,1},{4,6},{5,7},{6,4},{7,5},{8,10},{9,11},{10,... | collective-permute-start | bytes 393224 | tf_op jit(solution)/shard_map/ppermute | solution.py:27
  122.3 0.0 collective-permute-done.8
  122.3 4.6 %collective-permute-done.10 = bf16[128,512]{1,0:T(8,128)(2,1)S(1)} collective-permute-done((bf16[128,512]{1,0:T(8,128)(2,1)S(1)}, bf16[128,512]{1,0:T(8,128)(2,1)S(1)}, u32[]{:S(2)}, u32[]{:S(2)}) %collective-permute-start.10) | collective-permute-done | bytes 131104 | tf_op jit(solution)/shard_map/ppermute | solution.py:27
  126.9 4.6 %collective-permute-done.9 = bf16[128,512]{1,0:T(8,128)(2,1)S(1)} collective-permute-done((bf16[128,512]{1,0:T(8,128)(2,1)S(1)}, bf16[128,512]{1,0:T(8,128)(2,1)S(1)}, u32[]{:S(2)}, u32[]{:S(2)}) %collective-permute-start.9) | collective-permute-done | bytes 131104 | tf_op jit(solution)/shard_map/ppermute | solution.py:27
  131.5 0.1 fusion.1
  131.5 2.9 %collective-permute-start.11 = (bf16[128,512]{1,0:T(8,128)(2,1)S(1)}, bf16[128,512]{1,0:T(8,128)(2,1)S(1)}, u32[]{:S(2)}, u32[]{:S(2)}) collective-permute-start(bf16[128,512]{1,0:T(8,128)(2,1)S(1)} %fusion.1), channel_id=1, source_target_pairs={{0,0},{1,4},{2,256},{3,260},{4,5},{5,1},{6,261},{7,257},{8,258},{9... | collective-permute-start | bytes 393224 | tf_op jit(solution)/shard_map/ppermute | solution.py:27
  134.5 8.7 %collective-permute-done.11 = bf16[128,512]{1,0:T(8,128)(2,1)S(1)} collective-permute-done((bf16[128,512]{1,0:T(8,128)(2,1)S(1)}, bf16[128,512]{1,0:T(8,128)(2,1)S(1)}, u32[]{:S(2)}, u32[]{:S(2)}) %collective-permute-start.11) | collective-permute-done | bytes 131104 | tf_op jit(solution)/shard_map/ppermute | solution.py:27
  143.2 0.7 copy.8
  (4 shorter events, 0.1 us)
Async XLA Ops:
  9.3 26.9 %all-to-all-start = ((f32[32,16,128]{2,1,0:T(8,128)}), f32[32,16,128]{2,1,0:T(8,128)S(1)}, u32[]{:S(2)}, u32[]{:S(2)}) async-start(f32[32,16,128]{2,1,0:T(8,128)} %get-tuple-element.19), calls=%async_computation | async-start | bytes 524288 | tf_op jit(solution)/shard_map/all_to_all | solution.py:298
  25.1 76.5 %all-gather.3.cloned.1.call-start = ((), (), s32[]{:S(2)}) async-start(), calls=%async_computation.2 | async-start | bytes 2359296 | tf_op jit(solution)/shard_map/all_gather | solution.py:304
  25.2 13.4 %collective-permute-start = (bf16[512,256]{1,0:T(8,128)(2,1)}, bf16[512,256]{1,0:T(8,128)(2,1)S(1)}, u32[]{:S(2)}, u32[]{:S(2)}) collective-permute-start(bf16[512,256]{1,0:T(8,128)(2,1)} %param.11), channel_id=1, source_target_pairs={{0,0},{1,1},{2,2},{3,3},{4,16},{5,17},{6,18},{7,19},{8,32},{9,33},... | collective-permute-start | bytes 786440 | tf_op jit(solution)/shard_map/ppermute | solution.py:27
  36.2 0.7 copy-start.1
  38.6 0.7 copy-start.2
  65.2 3.4 %collective-permute-start.1 = (bf16[128,512]{1,0:T(8,128)(2,1)}, bf16[128,512]{1,0:T(8,128)(2,1)S(1)}, u32[]{:S(2)}, u32[]{:S(2)}) collective-permute-start(bf16[128,512]{1,0:T(8,128)(2,1)} %back.1), channel_id=1, source_target_pairs={{4,20},{5,21},{6,22},{7,23},{12,28},{13,29},{14,30},{15,31},{16,0}... | collective-permute-start | bytes 393224 | tf_op jit(solution)/shard_map/ppermute | solution.py:27
  69.6 12.3 %collective-permute-start.2 = (bf16[256,512]{1,0:T(8,128)(2,1)S(1)}, bf16[256,512]{1,0:T(8,128)(2,1)S(1)}, u32[]{:S(2)}, u32[]{:S(2)}) collective-permute-start(bf16[256,512]{1,0:T(8,128)(2,1)S(1)} %pad_maximum_fusion.1), channel_id=1, source_target_pairs={{0,256},{1,257},{2,258},{3,259},{8,264},{9,265},{10,266},{11,267},... | collective-permute-start | bytes 786440 | tf_op jit(solution)/shard_map/ppermute | solution.py:27
  82.8 8.0 %collective-permute-start.4 = (bf16[512,512]{1,0:T(8,128)(2,1)S(1)}, bf16[512,512]{1,0:T(8,128)(2,1)S(1)}, u32[]{:S(2)}, u32[]{:S(2)}) collective-permute-start(bf16[512,512]{1,0:T(8,128)(2,1)S(1)} %pad_maximum_fusion.line), channel_id=1, source_target_pairs={{0,12},{1,13},{2,14},{3,15},{8,4},{9,5},{10,6},{11,7},{20,16},{21,... | collective-permute-start | bytes 1572872 | tf_op jit(solution)/shard_map/ppermute | solution.py:27
  84.1 8.0 %collective-permute-start.3 = (bf16[512,512]{1,0:T(8,128)(2,1)S(1)}, bf16[512,512]{1,0:T(8,128)(2,1)S(1)}, u32[]{:S(2)}, u32[]{:S(2)}) collective-permute-start(bf16[512,512]{1,0:T(8,128)(2,1)S(1)} %pad_maximum_fusion.line), channel_id=1, source_target_pairs={{0,4},{1,5},{2,6},{3,7},{8,12},{9,13},{10,14},{11,15},{20,24},{21,... | collective-permute-start | bytes 1572872 | tf_op jit(solution)/shard_map/ppermute | solution.py:27
  90.8 8.7 %collective-permute-start.6 = (bf16[256,512]{1,0:T(8,128)(2,1)S(1)}, bf16[256,512]{1,0:T(8,128)(2,1)S(1)}, u32[]{:S(2)}, u32[]{:S(2)}) collective-permute-start(bf16[256,512]{1,0:T(8,128)(2,1)S(1)} %slice.28), channel_id=1, source_target_pairs={{4,0},{5,1},{6,2},{7,3},{12,8},{13,9},{14,10},{15,11},{16,28},{17,... | collective-permute-start | bytes 786440 | tf_op jit(solution)/shard_map/ppermute | solution.py:27
  92.2 9.5 %collective-permute-start.5 = (bf16[256,512]{1,0:T(8,128)(2,1)S(1)}, bf16[256,512]{1,0:T(8,128)(2,1)S(1)}, u32[]{:S(2)}, u32[]{:S(2)}) collective-permute-start(bf16[256,512]{1,0:T(8,128)(2,1)S(1)} %slice.27), channel_id=1, source_target_pairs={{4,8},{5,9},{6,10},{7,11},{12,0},{13,1},{14,2},{15,3},{16,20},{17,... | collective-permute-start | bytes 786440 | tf_op jit(solution)/shard_map/ppermute | solution.py:27
  101.6 1.6 %copy-start = (bf16[4096,256]{1,0:T(8,128)(2,1)S(1)}, bf16[4096,256]{1,0:T(8,128)(2,1)}, u32[]{:S(2)}) copy-start(bf16[4096,256]{1,0:T(8,128)(2,1)} %all-gather.3.cloned.1.call-done) | copy-start | bytes 6291460
  104.6 4.6 %collective-permute-start.7 = (f32[4,128,512]{2,1,0:T(8,128)S(1)}, f32[4,128,512]{2,1,0:T(8,128)S(1)}, u32[]{:S(2)}, u32[]{:S(2)}) collective-permute-start(f32[4,128,512]{2,1,0:T(8,128)S(1)} %send.1), channel_id=1, source_target_pairs={{0,16},{1,17},{2,18},{3,19},{4,20},{5,21},{6,22},{7,23},{8,24},{9,... | collective-permute-start | bytes 3145736 | tf_op jit(solution)/shard_map/ppermute | solution.py:27
  109.4 12.8 %collective-permute-start.8 = (bf16[128,512]{1,0:T(8,128)(2,1)S(1)}, bf16[128,512]{1,0:T(8,128)(2,1)S(1)}, u32[]{:S(2)}, u32[]{:S(2)}) collective-permute-start(bf16[128,512]{1,0:T(8,128)(2,1)S(1)} %get-tuple-element.27), channel_id=1, source_target_pairs={{0,1},{1,2},{2,3},{3,0},{4,5},{5,6},{6,7},{7,4},{8,9},{9,10},{10,1... | collective-permute-start | bytes 393224 | tf_op jit(solution)/shard_map/ppermute | solution.py:27
  116.9 10.0 %collective-permute-start.10 = (bf16[128,512]{1,0:T(8,128)(2,1)S(1)}, bf16[128,512]{1,0:T(8,128)(2,1)S(1)}, u32[]{:S(2)}, u32[]{:S(2)}) collective-permute-start(bf16[128,512]{1,0:T(8,128)(2,1)S(1)} %get-tuple-element.28), channel_id=1, source_target_pairs={{0,3},{1,0},{2,1},{3,2},{4,7},{5,4},{6,5},{7,6},{8,11},{9,8},{10,9... | collective-permute-start | bytes 393224 | tf_op jit(solution)/shard_map/ppermute | solution.py:27
  118.8 12.6 %collective-permute-start.9 = (bf16[128,512]{1,0:T(8,128)(2,1)S(1)}, bf16[128,512]{1,0:T(8,128)(2,1)S(1)}, u32[]{:S(2)}, u32[]{:S(2)}) collective-permute-start(bf16[128,512]{1,0:T(8,128)(2,1)S(1)} %get-tuple-element.29), channel_id=1, source_target_pairs={{0,2},{1,3},{2,0},{3,1},{4,6},{5,7},{6,4},{7,5},{8,10},{9,11},{10,... | collective-permute-start | bytes 393224 | tf_op jit(solution)/shard_map/ppermute | solution.py:27
  131.5 11.6 %collective-permute-start.11 = (bf16[128,512]{1,0:T(8,128)(2,1)S(1)}, bf16[128,512]{1,0:T(8,128)(2,1)S(1)}, u32[]{:S(2)}, u32[]{:S(2)}) collective-permute-start(bf16[128,512]{1,0:T(8,128)(2,1)S(1)} %fusion.1), channel_id=1, source_target_pairs={{0,0},{1,4},{2,256},{3,260},{4,5},{5,1},{6,261},{7,257},{8,258},{9... | collective-permute-start | bytes 393224 | tf_op jit(solution)/shard_map/ppermute | solution.py:27
Sparse Core Ops, SparseCore 0:
  39.4 47.9 all-gather.2

commit v9 on v8

--- a/solution.py
+++ b/solution.py
@@ -290,7 +290,6 @@
     def other_core(value, sends=lambda *place: True):
         return move(value, axes, lambda yh, z, core, x, yl: (yh, z, 1 - core, x, yl), sends)
 
-    weight = move(out_weight, axes, place)
     along_z = [[(yh * 8 + z) * 2 + core for z in range(8)] for yh in range(2) for core in range(2)]
 
     feat = features.transpose(1, 0, 2)
@@ -299,10 +298,12 @@
     ctx = index // 16
     rate = lax.dynamic_slice(decay_rate, (ctx // 4 * 2, ctx % 4 * 128), (2, 128))
     gain = residue * jnp.sqrt(-jnp.expm1(-2.0 * decay_rate))
-    ends, rate, gain = tie((ends, rate, gain))
-    carried, weight = tie((carry(ends, rate), weight))
+    ends, rate, gain, out_weight = tie((ends, rate, gain, out_weight))
+    weight = move(out_weight, axes, place)
+    carried = carry(ends, rate)
+    incoming = lax.all_to_all(carried, "ctx", 0, 0, tiled=True).reshape(256, 128)
+    incoming, weight = tie((incoming, weight))
     weights = lax.all_gather(weight, "ctx", axis_index_groups=along_z)
-    incoming = lax.all_to_all(carried, "ctx", 0, 0, tiled=True).reshape(256, 128)
 
     gated = back(query, drive, half, own, incoming, decay_rate, gain, skip[None])
 

time: 153 us -> 154 us (level)
  the two profiles are of different devices: /device:TPU:56 before, /device:TPU:6 now
where the time goes in v9:
time: 154 us
  waiting for transfers between devices  56.4 us (37%)
  starting transfers between devices  45.5 us (30%)
  blocking collectives  19.9 us (13%)
  between operations  13.8 us (9%)
  Pallas kernels  9.78 us (6%)
  local copies, waits for them, and re-layouts  4.46 us (3%)
  other arithmetic  3.59 us (2%)
    ppermute x12, waiting for transfers between devices, move(): return lax.ppermute(value, axes, pairs)  44.7 us
    ppermute x12, starting transfers between devices, move(): return lax.ppermute(value, axes, pairs)  29.5 us
    all_to_all x1, blocking collectives, body(): lax.all_to_all(carried, 'ctx', 0, 0, tiled=True).reshape(256, 128)  19.9 us
    all_to_all x1, starting transfers between devices, body(): ends = lax.all_to_all(ends, 'ctx', 0, 0, tiled=True)  16 us
    all_to_all x1, waiting for transfers between devices, body(): ends = lax.all_to_all(ends, 'ctx', 0, 0, tiled=True)  11.7 us
  transfers between devices with their start and end apart: 14, of which 9 were waited for; matrix products, arithmetic and copies ran while one was open for 3% of the time, Pallas kernels for 4%

profile of v9, /device:TPU:6, one launch (start us, length us, event | category | flops | bytes accessed | tf_op | source)
XLA Modules:
  0.0 153.5 jit_solution(8946783052783478578)
XLA Ops:
  6.5 2.7 %first.1 = (f32[32,16,128]{2,1,0:T(8,128)}, f32[128,512]{1,0:T(8,128)}, f32[512,128]{1,0:T(8,128)}, f32[128,128]{1,0:T(8,128)}, f32[16,128]{1,0:T(8,128)}) custom-call(bf16[3,128,512]{2,1,0:T(8,128)(2,1)} %bitcast.24, f32[3,3,512]{2,1,0:T(4,128)} %taps_ref.1, f32[16,512]{1,0:T(8,128)} %rate_ref.3), custom_call_target="tpu_custom_call" | custom-call | flops 1 | bytes 1 | tf_op jit(solution)/shard_map/first/pallas_call | solution.py:210
  9.3 16.0 %all-to-all-start = ((f32[32,16,128]{2,1,0:T(8,128)}), f32[32,16,128]{2,1,0:T(8,128)S(1)}, u32[]{:S(2)}, u32[]{:S(2)}) async-start(f32[32,16,128]{2,1,0:T(8,128)} %get-tuple-element.20), calls=%async_computation | async-start | bytes 524288 | tf_op jit(solution)/shard_map/all_to_all | solution.py:297
  25.3 0.0 all-gather.3.cloned.1.call-start
  25.4 1.3 dynamic_slice.3.rate_ref
  26.7 1.4 sqrt_multiply_fusion.gain_ref
  28.1 11.7 %all-to-all-done.ends_ref = f32[32,16,128]{2,1,0:T(8,128)S(1)} async-done(((f32[32,16,128]{2,1,0:T(8,128)}), f32[32,16,128]{2,1,0:T(8,128)S(1)}, u32[]{:S(2)}, u32[]{:S(2)}) %all-to-all-start) | async-done | bytes 262176 | tf_op jit(solution)/shard_map/all_to_all | solution.py:297
  39.8 0.0 copy-start.1
  39.8 1.9 %collective-permute-start = (bf16[512,256]{1,0:T(8,128)(2,1)}, bf16[512,256]{1,0:T(8,128)(2,1)S(1)}, u32[]{:S(2)}, u32[]{:S(2)}) collective-permute-start(bf16[512,256]{1,0:T(8,128)(2,1)} %param.11), channel_id=1, source_target_pairs={{0,0},{1,1},{2,2},{3,3},{4,16},{5,17},{6,18},{7,19},{8,32},{9,33},... | collective-permute-start | bytes 786440 | tf_op jit(solution)/shard_map/ppermute | solution.py:27
  41.8 0.0 copy-done.1
  41.8 1.7 %carry.1 = f32[32,8,128]{2,1,0:T(8,128)} custom-call(f32[32,16,128]{2,1,0:T(8,128)} %copy-done.1, f32[2,128]{1,0:T(2,128)} %dynamic_slice.3.rate_ref), custom_call_target="tpu_custom_call" | custom-call | flops 1 | bytes 1 | tf_op jit(solution)/shard_map/carry/pallas_call | solution.py:228
  43.5 19.9 %all_to_all.10 = f32[32,8,128]{2,1,0:T(8,128)} all-to-all(f32[32,8,128]{2,1,0:T(8,128)} %carry.1), channel_id=1, replica_groups=mesh['ctx'=32,'tp'=16] {'ctx'}, dimensions={0} | all-to-all | bytes 262144 | tf_op jit(solution)/shard_map/all_to_all | solution.py:304
  63.4 0.0 collective-permute-done
  63.4 0.0 copy-start.2
  63.4 0.7 copy-done.2
  64.1 0.0 all-gather.3.cloned.1.call-update
  64.1 2.6 %back.1 = bf16[128,512]{1,0:T(8,128)(2,1)} custom-call(f32[128,512]{1,0:T(8,128)} %get-tuple-element.16.query_ref, f32[512,128]{1,0:T(8,128)} %get-tuple-element.17.drive_ref, f32[128,128]{1,0:T(8,128)} %get-tuple-element.18.half_ref, f32[16,128]{1,0:T(8,128)} %get-tuple-element.19.own_ref, f32[256,128]{1,0:T(8,128)} %bitcast.23, f32[16,512]{1,0:T(8,128)} %rate_ref.3, ...), custom_call_target="tpu_custom_call" | custom-call | flops 1 | bytes 1 | tf_op jit(solution)/shard_map/back/pallas_call | solution.py:239
  66.8 1.3 collective-permute-start.1
  68.1 1.2 collective-permute-done.1
  69.2 0.9 pad_maximum_fusion.1
  70.1 0.7 collective-permute-start.2
  70.8 0.0 collective-permute-done.2
  70.8 0.9 pad_maximum_fusion.line
  71.8 1.3 collective-permute-start.4
  73.1 1.3 collective-permute-start.3
  74.4 21.5 %collective-permute-done.4.bwd = bf16[512,512]{1,0:T(8,128)(2,1)S(1)} collective-permute-done((bf16[512,512]{1,0:T(8,128)(2,1)S(1)}, bf16[512,512]{1,0:T(8,128)(2,1)S(1)}, u32[]{:S(2)}, u32[]{:S(2)}) %collective-permute-start.4) | collective-permute-done | bytes 524320 | tf_op jit(solution)/shard_map/ppermute | solution.py:27
  95.9 2.2 %collective-permute-start.6 = (bf16[256,512]{1,0:T(8,128)(2,1)S(1)}, bf16[256,512]{1,0:T(8,128)(2,1)S(1)}, u32[]{:S(2)}, u32[]{:S(2)}) collective-permute-start(bf16[256,512]{1,0:T(8,128)(2,1)S(1)} %slice.28), channel_id=1, source_target_pairs={{4,0},{5,1},{6,2},{7,3},{12,8},{13,9},{14,10},{15,11},{16,28},{17,... | collective-permute-start | bytes 786440 | tf_op jit(solution)/shard_map/ppermute | solution.py:27
  98.1 0.0 collective-permute-done.3.fwd
  98.2 1.3 collective-permute-start.5
  99.6 0.1 stack.27.table_ref
  99.7 2.3 %collective-permute-done.6.hb = bf16[256,512]{1,0:T(8,128)(2,1)S(1)} collective-permute-done((bf16[256,512]{1,0:T(8,128)(2,1)S(1)}, bf16[256,512]{1,0:T(8,128)(2,1)S(1)}, u32[]{:S(2)}, u32[]{:S(2)}) %collective-permute-start.6) | collective-permute-done | bytes 262176 | tf_op jit(solution)/shard_map/ppermute | solution.py:27
  102.0 1.4 collective-permute-done.5.hf
  103.3 0.0 all-gather.3.cloned.1.call-done
  103.3 1.6 %copy-done = bf16[4096,256]{1,0:T(8,128)(2,1)S(1)} copy-done((bf16[4096,256]{1,0:T(8,128)(2,1)S(1)}, bf16[4096,256]{1,0:T(8,128)(2,1)}, u32[]{:S(2)}) %copy-start) | copy-done | bytes 2097176
  104.9 1.4 send.1
  106.3 1.9 %collective-permute-start.7 = (f32[4,128,512]{2,1,0:T(8,128)S(1)}, f32[4,128,512]{2,1,0:T(8,128)S(1)}, u32[]{:S(2)}, u32[]{:S(2)}) collective-permute-start(f32[4,128,512]{2,1,0:T(8,128)S(1)} %send.1), channel_id=1, source_target_pairs={{0,16},{1,17},{2,18},{3,19},{4,20},{5,21},{6,22},{7,23},{8,24},{9,... | collective-permute-start | bytes 3145736 | tf_op jit(solution)/shard_map/ppermute | solution.py:27
  108.2 1.4 keep.1
  109.6 1.2 collective-permute-done.7
  110.9 0.3 fusion.2
  111.2 4.6 %collective-permute-start.8 = (bf16[128,512]{1,0:T(8,128)(2,1)S(1)}, bf16[128,512]{1,0:T(8,128)(2,1)S(1)}, u32[]{:S(2)}, u32[]{:S(2)}) collective-permute-start(bf16[128,512]{1,0:T(8,128)(2,1)S(1)} %get-tuple-element.29), channel_id=1, source_target_pairs={{0,1},{1,2},{2,3},{3,0},{4,5},{5,6},{6,7},{7,4},{8,9},{9,10},{10,1... | collective-permute-start | bytes 393224 | tf_op jit(solution)/shard_map/ppermute | solution.py:27
  115.8 3.0 %collective-permute-start.10 = (bf16[128,512]{1,0:T(8,128)(2,1)S(1)}, bf16[128,512]{1,0:T(8,128)(2,1)S(1)}, u32[]{:S(2)}, u32[]{:S(2)}) collective-permute-start(bf16[128,512]{1,0:T(8,128)(2,1)S(1)} %get-tuple-element.30), channel_id=1, source_target_pairs={{0,3},{1,0},{2,1},{3,2},{4,7},{5,4},{6,5},{7,6},{8,11},{9,8},{10,9... | collective-permute-start | bytes 393224 | tf_op jit(solution)/shard_map/ppermute | solution.py:27
  118.8 7.2 %collective-permute-start.9 = (bf16[128,512]{1,0:T(8,128)(2,1)S(1)}, bf16[128,512]{1,0:T(8,128)(2,1)S(1)}, u32[]{:S(2)}, u32[]{:S(2)}) collective-permute-start(bf16[128,512]{1,0:T(8,128)(2,1)S(1)} %get-tuple-element.31), channel_id=1, source_target_pairs={{0,2},{1,3},{2,0},{3,1},{4,6},{5,7},{6,4},{7,5},{8,10},{9,11},{10,... | collective-permute-start | bytes 393224 | tf_op jit(solution)/shard_map/ppermute | solution.py:27
  126.0 0.0 collective-permute-done.8
  126.0 0.1 collective-permute-done.10
  126.2 6.8 %collective-permute-done.9 = bf16[128,512]{1,0:T(8,128)(2,1)S(1)} collective-permute-done((bf16[128,512]{1,0:T(8,128)(2,1)S(1)}, bf16[128,512]{1,0:T(8,128)(2,1)S(1)}, u32[]{:S(2)}, u32[]{:S(2)}) %collective-permute-start.9) | collective-permute-done | bytes 131104 | tf_op jit(solution)/shard_map/ppermute | solution.py:27
  132.9 0.1 fusion.1
  133.0 2.7 %collective-permute-start.11 = (bf16[128,512]{1,0:T(8,128)(2,1)S(1)}, bf16[128,512]{1,0:T(8,128)(2,1)S(1)}, u32[]{:S(2)}, u32[]{:S(2)}) collective-permute-start(bf16[128,512]{1,0:T(8,128)(2,1)S(1)} %fusion.1), channel_id=1, source_target_pairs={{0,0},{1,4},{2,256},{3,260},{4,5},{5,1},{6,261},{7,257},{8,258},{9... | collective-permute-start | bytes 393224 | tf_op jit(solution)/shard_map/ppermute | solution.py:27
  135.8 10.2 %collective-permute-done.11 = bf16[128,512]{1,0:T(8,128)(2,1)S(1)} collective-permute-done((bf16[128,512]{1,0:T(8,128)(2,1)S(1)}, bf16[128,512]{1,0:T(8,128)(2,1)S(1)}, u32[]{:S(2)}, u32[]{:S(2)}) %collective-permute-start.11) | collective-permute-done | bytes 131104 | tf_op jit(solution)/shard_map/ppermute | solution.py:27
  146.0 0.7 copy.8
  (4 shorter events, 0.1 us)
Async XLA Ops:
  9.3 30.6 %all-to-all-start = ((f32[32,16,128]{2,1,0:T(8,128)}), f32[32,16,128]{2,1,0:T(8,128)S(1)}, u32[]{:S(2)}, u32[]{:S(2)}) async-start(f32[32,16,128]{2,1,0:T(8,128)} %get-tuple-element.20), calls=%async_computation | async-start | bytes 524288 | tf_op jit(solution)/shard_map/all_to_all | solution.py:297
  25.3 78.1 %all-gather.3.cloned.1.call-start = ((), (), s32[]{:S(2)}) async-start(), calls=%async_computation.2 | async-start | bytes 2359296 | tf_op jit(solution)/shard_map/all_gather | solution.py:306
  39.8 1.9 %copy-start.1 = (f32[32,16,128]{2,1,0:T(8,128)}, f32[32,16,128]{2,1,0:T(8,128)S(1)}, u32[]{:S(2)}) copy-start(f32[32,16,128]{2,1,0:T(8,128)S(1)} %all-to-all-done.ends_ref) | copy-start | bytes 786436
  39.8 23.6 %collective-permute-start = (bf16[512,256]{1,0:T(8,128)(2,1)}, bf16[512,256]{1,0:T(8,128)(2,1)S(1)}, u32[]{:S(2)}, u32[]{:S(2)}) collective-permute-start(bf16[512,256]{1,0:T(8,128)(2,1)} %param.11), channel_id=1, source_target_pairs={{0,0},{1,1},{2,2},{3,3},{4,16},{5,17},{6,18},{7,19},{8,32},{9,33},... | collective-permute-start | bytes 786440 | tf_op jit(solution)/shard_map/ppermute | solution.py:27
  63.4 0.7 copy-start.2
  66.8 2.5 %collective-permute-start.1 = (bf16[128,512]{1,0:T(8,128)(2,1)}, bf16[128,512]{1,0:T(8,128)(2,1)S(1)}, u32[]{:S(2)}, u32[]{:S(2)}) collective-permute-start(bf16[128,512]{1,0:T(8,128)(2,1)} %back.1), channel_id=1, source_target_pairs={{4,20},{5,21},{6,22},{7,23},{12,28},{13,29},{14,30},{15,31},{16,0}... | collective-permute-start | bytes 393224 | tf_op jit(solution)/shard_map/ppermute | solution.py:27
  70.1 0.7 collective-permute-start.2
  71.8 24.1 %collective-permute-start.4 = (bf16[512,512]{1,0:T(8,128)(2,1)S(1)}, bf16[512,512]{1,0:T(8,128)(2,1)S(1)}, u32[]{:S(2)}, u32[]{:S(2)}) collective-permute-start(bf16[512,512]{1,0:T(8,128)(2,1)S(1)} %pad_maximum_fusion.line), channel_id=1, source_target_pairs={{0,12},{1,13},{2,14},{3,15},{8,4},{9,5},{10,6},{11,7},{20,16},{21,... | collective-permute-start | bytes 1572872 | tf_op jit(solution)/shard_map/ppermute | solution.py:27
  73.1 25.0 %collective-permute-start.3 = (bf16[512,512]{1,0:T(8,128)(2,1)S(1)}, bf16[512,512]{1,0:T(8,128)(2,1)S(1)}, u32[]{:S(2)}, u32[]{:S(2)}) collective-permute-start(bf16[512,512]{1,0:T(8,128)(2,1)S(1)} %pad_maximum_fusion.line), channel_id=1, source_target_pairs={{0,4},{1,5},{2,6},{3,7},{8,12},{9,13},{10,14},{11,15},{20,24},{21,... | collective-permute-start | bytes 1572872 | tf_op jit(solution)/shard_map/ppermute | solution.py:27
  95.9 6.1 %collective-permute-start.6 = (bf16[256,512]{1,0:T(8,128)(2,1)S(1)}, bf16[256,512]{1,0:T(8,128)(2,1)S(1)}, u32[]{:S(2)}, u32[]{:S(2)}) collective-permute-start(bf16[256,512]{1,0:T(8,128)(2,1)S(1)} %slice.28), channel_id=1, source_target_pairs={{4,0},{5,1},{6,2},{7,3},{12,8},{13,9},{14,10},{15,11},{16,28},{17,... | collective-permute-start | bytes 786440 | tf_op jit(solution)/shard_map/ppermute | solution.py:27
  98.2 5.2 %collective-permute-start.5 = (bf16[256,512]{1,0:T(8,128)(2,1)S(1)}, bf16[256,512]{1,0:T(8,128)(2,1)S(1)}, u32[]{:S(2)}, u32[]{:S(2)}) collective-permute-start(bf16[256,512]{1,0:T(8,128)(2,1)S(1)} %slice.27), channel_id=1, source_target_pairs={{4,8},{5,9},{6,10},{7,11},{12,0},{13,1},{14,2},{15,3},{16,20},{17,... | collective-permute-start | bytes 786440 | tf_op jit(solution)/shard_map/ppermute | solution.py:27
  103.3 1.6 %copy-start = (bf16[4096,256]{1,0:T(8,128)(2,1)S(1)}, bf16[4096,256]{1,0:T(8,128)(2,1)}, u32[]{:S(2)}) copy-start(bf16[4096,256]{1,0:T(8,128)(2,1)} %all-gather.3.cloned.1.call-done) | copy-start | bytes 6291460
  106.3 4.6 %collective-permute-start.7 = (f32[4,128,512]{2,1,0:T(8,128)S(1)}, f32[4,128,512]{2,1,0:T(8,128)S(1)}, u32[]{:S(2)}, u32[]{:S(2)}) collective-permute-start(f32[4,128,512]{2,1,0:T(8,128)S(1)} %send.1), channel_id=1, source_target_pairs={{0,16},{1,17},{2,18},{3,19},{4,20},{5,21},{6,22},{7,23},{8,24},{9,... | collective-permute-start | bytes 3145736 | tf_op jit(solution)/shard_map/ppermute | solution.py:27
  111.2 14.9 %collective-permute-start.8 = (bf16[128,512]{1,0:T(8,128)(2,1)S(1)}, bf16[128,512]{1,0:T(8,128)(2,1)S(1)}, u32[]{:S(2)}, u32[]{:S(2)}) collective-permute-start(bf16[128,512]{1,0:T(8,128)(2,1)S(1)} %get-tuple-element.29), channel_id=1, source_target_pairs={{0,1},{1,2},{2,3},{3,0},{4,5},{5,6},{6,7},{7,4},{8,9},{9,10},{10,1... | collective-permute-start | bytes 393224 | tf_op jit(solution)/shard_map/ppermute | solution.py:27
  115.8 10.4 %collective-permute-start.10 = (bf16[128,512]{1,0:T(8,128)(2,1)S(1)}, bf16[128,512]{1,0:T(8,128)(2,1)S(1)}, u32[]{:S(2)}, u32[]{:S(2)}) collective-permute-start(bf16[128,512]{1,0:T(8,128)(2,1)S(1)} %get-tuple-element.30), channel_id=1, source_target_pairs={{0,3},{1,0},{2,1},{3,2},{4,7},{5,4},{6,5},{7,6},{8,11},{9,8},{10,9... | collective-permute-start | bytes 393224 | tf_op jit(solution)/shard_map/ppermute | solution.py:27
  118.8 14.1 %collective-permute-start.9 = (bf16[128,512]{1,0:T(8,128)(2,1)S(1)}, bf16[128,512]{1,0:T(8,128)(2,1)S(1)}, u32[]{:S(2)}, u32[]{:S(2)}) collective-permute-start(bf16[128,512]{1,0:T(8,128)(2,1)S(1)} %get-tuple-element.31), channel_id=1, source_target_pairs={{0,2},{1,3},{2,0},{3,1},{4,6},{5,7},{6,4},{7,5},{8,10},{9,11},{10,... | collective-permute-start | bytes 393224 | tf_op jit(solution)/shard_map/ppermute | solution.py:27
  133.0 13.0 %collective-permute-start.11 = (bf16[128,512]{1,0:T(8,128)(2,1)S(1)}, bf16[128,512]{1,0:T(8,128)(2,1)S(1)}, u32[]{:S(2)}, u32[]{:S(2)}) collective-permute-start(bf16[128,512]{1,0:T(8,128)(2,1)S(1)} %fusion.1), channel_id=1, source_target_pairs={{0,0},{1,4},{2,256},{3,260},{4,5},{5,1},{6,261},{7,257},{8,258},{9... | collective-permute-start | bytes 393224 | tf_op jit(solution)/shard_map/ppermute | solution.py:27
Sparse Core Ops, SparseCore 0:
  64.3 38.2 all-gather.2
